TPU v7x, 32 devices: a whole 2x2x4 slice. The times are simulated.
32 devices in a mesh: gx: 4 (over z), gy: 4 (over y, x), gz: 2 (over core).
Axes of the slice: x: 2, y: 2, z: 4, core: 2. Of those that a mesh axis runs over, the one named last changes fastest.
Arguments:
- rhs: float32 [2, 4, 32, 64, 256], P(None, None, 'gx', 'gy', 'gz'), may hold values from -6 to 6
- density: float32 [32, 64, 256], P('gx', 'gy', 'gz'), may hold values from 0.5 to 2
- shift_real: float32 [32, 64, 256], P('gx', 'gy', 'gz'), may hold values from 0 to 0.04
- shift_imag: float32 [32, 64, 256], P('gx', 'gy', 'gz'), may hold values from 0.02 to 0.08
Outputs:
- solution: float32 [2, 4, 32, 64, 256], P(None, None, 'gx', 'gy', 'gz')
All inputs are finite; a program needn't handle non-finite values.
Results may differ from a plain program's by a relative error of at most 0.00002.
Values sent between devices are 32-bit elements; how exact they have to be, the bound alone decides.
No kernel may reach another device: no remote copies, remote signals or barrier semaphores. Data moves between devices by JAX's collectives and lax.ppermute only.
A program may use at most 192 MiB of HBM per device.

v0:
```python
import jax
import jax.numpy as jnp
from jax import lax
from jax.sharding import PartitionSpec as P

NU = 2
CSWEEPS = 4


omega_damp = 0.8


def padded(cells, sides, width):
    for axis, dim in sides:
        count = lax.axis_size(axis)
        ends = count - 1
        head = lax.slice_in_dim(cells, 0, width, axis=dim)
        tail = lax.slice_in_dim(cells, cells.shape[dim] - width, cells.shape[dim], axis=dim)
        cells = jnp.concatenate(
            [
                lax.ppermute(tail, axis, [(i, (i + 1) % count) for i in range(ends)]),
                cells,
                lax.ppermute(head, axis, [((i + 1) % count, i) for i in range(ends)]),
            ],
            axis=dim,
        )
    return cells


def face_coefs(rho_pad):
    center = rho_pad[1:-1, 1:-1, 1:-1]
    others = [
        rho_pad[2:, 1:-1, 1:-1],
        rho_pad[:-2, 1:-1, 1:-1],
        rho_pad[1:-1, 2:, 1:-1],
        rho_pad[1:-1, :-2, 1:-1],
        rho_pad[1:-1, 1:-1, 2:],
        rho_pad[1:-1, 1:-1, :-2],
    ]
    result = []
    for other in others:
        total = center + other
        result.append(2.0 / jnp.where(total > 0.0, total, 1.0))
    return result


def make_level(rho_pad, shift_re, shift_im, scale):
    coefs = face_coefs(rho_pad)
    bsum = coefs[0] + coefs[1] + coefs[2] + coefs[3] + coefs[4] + coefs[5]
    diag_re = scale * bsum - shift_re
    diag_im = -shift_im
    magnitude = diag_re * diag_re + diag_im * diag_im
    return (coefs, bsum, shift_re, shift_im, scale, diag_re / magnitude, -diag_im / magnitude)


def apply_op(upad, level):
    coefs, bsum, shift_re, shift_im, scale, inv_re, inv_im = level
    center = upad[:, :, 1:-1, 1:-1, 1:-1]
    nbsum = coefs[0] * upad[:, :, 2:, 1:-1, 1:-1] + coefs[1] * upad[:, :, :-2, 1:-1, 1:-1]
    nbsum = nbsum + coefs[2] * upad[:, :, 1:-1, 2:, 1:-1] + coefs[3] * upad[:, :, 1:-1, :-2, 1:-1]
    nbsum = nbsum + coefs[4] * upad[:, :, 1:-1, 1:-1, 2:] + coefs[5] * upad[:, :, 1:-1, 1:-1, :-2]
    lap = scale * (bsum * center - nbsum)
    out_re = lap[0] - shift_re * center[0] + shift_im * center[1]
    out_im = lap[1] - shift_re * center[1] - shift_im * center[0]
    return jnp.stack([out_re, out_im])


def precondition(resid, level):
    inv_re, inv_im = (level[5], level[6])
    upd_re = inv_re * resid[0] - inv_im * resid[1]
    upd_im = inv_re * resid[1] + inv_im * resid[0]
    return omega_damp * jnp.stack([upd_re, upd_im])


def smooth(field, target, level, padder, count):
    for sweep in range(count):
        field = field + precondition(target - apply_op(padder(field), level), level)
    return field


def restrict(field):
    lead = field.shape[:-3]
    sx, sy, sz = field.shape[-3:]
    blocks = field.reshape(lead + (sx // 2, 2, sy // 2, 2, sz // 2, 2))
    return jnp.mean(blocks, axis=(-5, -3, -1))


def prolong(field):
    return jnp.repeat(jnp.repeat(jnp.repeat(field, 2, -3), 2, -2), 2, -1)


def fine_pad(field):
    return padded(field, (("gx", 2), ("gy", 3), ("gz", 4)), 1)


def coarse_pad(field):
    return padded(field, (("gx", 2), ("gy", 3), ("gz", 4)), 1)


def brick_density(rho):
    return padded(rho, (("gx", 0), ("gy", 1), ("gz", 2)), 1)


def local(rhs, density, shift_real, shift_imag):
    rho1, sr1, si1 = (restrict(density), restrict(shift_real), restrict(shift_imag))
    level1 = make_level(brick_density(rho1), sr1, si1, 0.25)
    rho2, sr2, si2 = (restrict(rho1), restrict(sr1), restrict(si1))
    level0 = make_level(brick_density(density), shift_real, shift_imag, 1.0)
    fine = precondition(rhs, level0)
    fine = smooth(fine, rhs, level0, fine_pad, NU - 1)
    coarse_rhs = restrict(rhs - apply_op(fine_pad(fine), level0))
    middle = precondition(coarse_rhs, level1)
    middle = smooth(middle, coarse_rhs, level1, coarse_pad, NU - 1)
    lowest_rhs = restrict(coarse_rhs - apply_op(coarse_pad(middle), level1))
    level2 = make_level(brick_density(rho2), sr2, si2, 0.0625)
    lowest = precondition(lowest_rhs, level2)
    lowest = smooth(lowest, lowest_rhs, level2, coarse_pad, CSWEEPS - 1)
    middle = smooth(middle + prolong(lowest), coarse_rhs, level1, coarse_pad, NU)
    corrected = fine + prolong(middle)
    fine = smooth(corrected, rhs, level0, fine_pad, NU)
    return fine


def solution(mesh):
    placed = (
        P(None, None, "gx", "gy", "gz"),
        P("gx", "gy", "gz"),
        P("gx", "gy", "gz"),
        P("gx", "gy", "gz"),
    )
    return jax.shard_map(
        local,
        mesh=mesh,
        in_specs=placed,
        out_specs=P(None, None, "gx", "gy", "gz"),
        check_vma=False,
    )
```

profile of v0, /device:TPU:29, one launch (start us, length us, event | category | flops | bytes accessed | tf_op | source)
XLA Modules:
  0.0 406.6 jit_solution(15574814157310585983)
XLA Ops:
  6.0 6.3 %reshape.89 = f32[4,2,8,2,64,2]{5,4,3,2,1,0:T(8,128)} reshape(f32[8,16,128]{2,1,0:T(8,128)} %param.5) | data formatting | bytes 131072 | tf_op jit(solution)/shard_map/reshape | solution.py:84
  23.6 4.6 %collective-permute-start.4 = (f32[10,18,1]{2,1,0:T(8,128)S(1)}, f32[10,18,1]{2,1,0:T(8,128)S(1)}, u32[]{:S(2)}, u32[]{:S(2)}) collective-permute-start(f32[10,18,1]{2,1,0:T(8,128)S(1)} %get-tuple-element.128), channel_id=1, source_target_pairs={{1,0},{3,2},{5,4},{7,6},{9,8},{11,10},{13,12},{15,14},{17,16},{19,... | collective-permute-start | bytes 2168 | tf_op jit(solution)/shard_map/ppermute | solution.py:23
  41.0 5.5 %reshape.90 = f32[4,2,8,2,64,2]{5,4,3,2,1,0:T(8,128)} reshape(f32[8,16,128]{2,1,0:T(8,128)S(1)} %copy-done.14) | data formatting | bytes 131072 | tf_op jit(solution)/shard_map/reshape | solution.py:84
  46.5 5.5 %reshape.91 = f32[4,2,8,2,64,2]{5,4,3,2,1,0:T(8,128)} reshape(f32[8,16,128]{2,1,0:T(8,128)S(1)} %copy-done.9) | data formatting | bytes 131072 | tf_op jit(solution)/shard_map/reshape | solution.py:84
  75.0 5.6 %collective-permute-start.10 = (f32[2,4,10,18,1]{3,1,4,2,0:T(4,128)S(1)}, f32[2,4,10,18,1]{3,1,4,2,0:T(4,128)}, u32[]{:S(2)}, u32[]{:S(2)}) collective-permute-start(f32[2,4,10,18,1]{3,1,4,2,0:T(4,128)S(1)} %copy.880), channel_id=1, source_target_pairs={{1,0},{3,2},{5,4},{7,6},{9,8},{11,10},{13,12},{15,14},{17,16},{19,... | collective-permute-start | bytes 17288 | tf_op jit(solution)/shard_map/ppermute | solution.py:23
  109.3 4.5 %collective-permute-start.22 = (f32[2,4,10,18,1]{3,1,4,2,0:T(4,128)S(1)}, f32[2,4,10,18,1]{3,1,4,2,0:T(4,128)}, u32[]{:S(2)}, u32[]{:S(2)}) collective-permute-start(f32[2,4,10,18,1]{3,1,4,2,0:T(4,128)S(1)} %copy.890), channel_id=1, source_target_pairs={{1,0},{3,2},{5,4},{7,6},{9,8},{11,10},{13,12},{15,14},{17,16},{19,... | collective-permute-start | bytes 17288 | tf_op jit(solution)/shard_map/ppermute | solution.py:23
  119.3 8.8 %copy.894 = f32[2,4,8,16,128]{1,4,3,2,0:T(8,128)} copy(f32[2,4,8,16,128]{4,3,2,1,0:T(8,128)S(1)} %maximum_subtract_fusion.2) | data formatting | bytes 1048576 | tf_op jit(solution)/shard_map/sub | solution.py:111
  128.1 13.2 %reduce_sum.75 = f32[2,4,4,8,64]{1,4,3,2,0:T(8,128)} reduce(f32[2,4,4,2,8,2,64,2]{1,7,6,5,4,3,2,0:T(2,128)} %bitcast.16, f32[]{:T(128)} %constant.9.clone.1), dimensions={3,5,7}, to_apply=%region_3.4 | reduce | flops 114688 | bytes 589828 | tf_op jit(solution)/shard_map/reduce_sum | solution.py:85
  150.0 4.6 %collective-permute-start.30 = (f32[1,4,32]{2,1,0:T(4,128)S(1)}, f32[1,4,32]{2,1,0:T(4,128)S(1)}, u32[]{:S(2)}, u32[]{:S(2)}) collective-permute-start(f32[1,4,32]{2,1,0:T(4,128)S(1)} %get-tuple-element.181), channel_id=1, source_target_pairs={{8,0},{16,8},{24,16},{9,1},{17,9},{25,17},{10,2},{18,10},{26,18},{... | collective-permute-start | bytes 1544 | tf_op jit(solution)/shard_map/ppermute | solution.py:23
  188.4 4.8 %collective-permute-start.38 = (f32[2,4,6,1,64]{4,1,3,2,0:T(4,128)S(1)}, f32[2,4,6,1,64]{4,1,3,2,0:T(4,128)S(1)}, u32[]{:S(2)}, u32[]{:S(2)}) collective-permute-start(f32[2,4,6,1,64]{4,1,3,2,0:T(4,128)S(1)} %copy.904), channel_id=1, source_target_pairs={{2,0},{4,2},{6,4},{3,1},{5,3},{7,5},{10,8},{12,10},{14,12},{11,9},... | collective-permute-start | bytes 36872 | tf_op jit(solution)/shard_map/ppermute | solution.py:23
  219.9 4.8 %collective-permute-start.44 = (f32[2,4,4,1,32]{4,3,2,1,0:T(1,128)S(1)}, f32[2,4,4,1,32]{4,3,2,1,0:T(1,128)S(1)}, u32[]{:S(2)}, u32[]{:S(2)}) collective-permute-start(f32[2,4,4,1,32]{4,3,2,1,0:T(1,128)S(1)} %get-tuple-element.153), channel_id=1, source_target_pairs={{2,0},{4,2},{6,4},{3,1},{5,3},{7,5},{10,8},{12,10},{14,12},{11,9},... | collective-permute-start | bytes 12296 | tf_op jit(solution)/shard_map/ppermute | solution.py:23
  225.8 5.3 %collective-permute-start.46 = (f32[2,4,4,6,1]{4,2,3,1,0:T(4,128)S(1)}, f32[2,4,4,6,1]{4,2,3,1,0:T(4,128)S(1)}, u32[]{:S(2)}, u32[]{:S(2)}) collective-permute-start(f32[2,4,4,6,1]{4,2,3,1,0:T(4,128)S(1)} %get-tuple-element.139), channel_id=1, source_target_pairs={{1,0},{3,2},{5,4},{7,6},{9,8},{11,10},{13,12},{15,14},{17,16},{19,... | collective-permute-start | bytes 2312 | tf_op jit(solution)/shard_map/ppermute | solution.py:23
  243.9 4.8 %collective-permute-start.50 = (f32[2,4,4,1,32]{4,3,2,1,0:T(1,128)S(1)}, f32[2,4,4,1,32]{4,3,2,1,0:T(1,128)S(1)}, u32[]{:S(2)}, u32[]{:S(2)}) collective-permute-start(f32[2,4,4,1,32]{4,3,2,1,0:T(1,128)S(1)} %get-tuple-element.151), channel_id=1, source_target_pairs={{2,0},{4,2},{6,4},{3,1},{5,3},{7,5},{10,8},{12,10},{14,12},{11,9},... | collective-permute-start | bytes 12296 | tf_op jit(solution)/shard_map/ppermute | solution.py:23
  249.7 4.4 %collective-permute-start.52 = (f32[2,4,4,6,1]{4,2,3,1,0:T(4,128)S(1)}, f32[2,4,4,6,1]{4,2,3,1,0:T(4,128)S(1)}, u32[]{:S(2)}, u32[]{:S(2)}) collective-permute-start(f32[2,4,4,6,1]{4,2,3,1,0:T(4,128)S(1)} %get-tuple-element.135), channel_id=1, source_target_pairs={{1,0},{3,2},{5,4},{7,6},{9,8},{11,10},{13,12},{15,14},{17,16},{19,... | collective-permute-start | bytes 2312 | tf_op jit(solution)/shard_map/ppermute | solution.py:23
  254.1 11.3 %collective-permute-start.53 = (f32[2,4,4,6,1]{4,2,3,1,0:T(4,128)S(1)}, f32[2,4,4,6,1]{4,2,3,1,0:T(4,128)S(1)}, u32[]{:S(2)}, u32[]{:S(2)}) collective-permute-start(f32[2,4,4,6,1]{4,2,3,1,0:T(4,128)S(1)} %get-tuple-element.136), channel_id=1, source_target_pairs={{0,1},{2,3},{4,5},{6,7},{8,9},{10,11},{12,13},{14,15},{16,17},{18,... | collective-permute-start | bytes 2312 | tf_op jit(solution)/shard_map/ppermute | solution.py:21
  274.5 4.8 %collective-permute-start.56 = (f32[2,4,4,1,32]{4,3,2,1,0:T(1,128)S(1)}, f32[2,4,4,1,32]{4,3,2,1,0:T(1,128)S(1)}, u32[]{:S(2)}, u32[]{:S(2)}) collective-permute-start(f32[2,4,4,1,32]{4,3,2,1,0:T(1,128)S(1)} %get-tuple-element.149), channel_id=1, source_target_pairs={{2,0},{4,2},{6,4},{3,1},{5,3},{7,5},{10,8},{12,10},{14,12},{11,9},... | collective-permute-start | bytes 12296 | tf_op jit(solution)/shard_map/ppermute | solution.py:23
  280.3 5.3 %collective-permute-start.58 = (f32[2,4,4,6,1]{4,2,3,1,0:T(4,128)S(1)}, f32[2,4,4,6,1]{4,2,3,1,0:T(4,128)S(1)}, u32[]{:S(2)}, u32[]{:S(2)}) collective-permute-start(f32[2,4,4,6,1]{4,2,3,1,0:T(4,128)S(1)} %get-tuple-element.131), channel_id=1, source_target_pairs={{1,0},{3,2},{5,4},{7,6},{9,8},{11,10},{13,12},{15,14},{17,16},{19,... | collective-permute-start | bytes 2312 | tf_op jit(solution)/shard_map/ppermute | solution.py:23
  299.2 4.8 %collective-permute-start.62 = (f32[2,4,6,1,64]{4,1,3,2,0:T(4,128)S(1)}, f32[2,4,6,1,64]{4,1,3,2,0:T(4,128)S(1)}, u32[]{:S(2)}, u32[]{:S(2)}) collective-permute-start(f32[2,4,6,1,64]{4,1,3,2,0:T(4,128)S(1)} %copy.941), channel_id=1, source_target_pairs={{2,0},{4,2},{6,4},{3,1},{5,3},{7,5},{10,8},{12,10},{14,12},{11,9},... | collective-permute-start | bytes 36872 | tf_op jit(solution)/shard_map/ppermute | solution.py:23
  305.2 4.4 %collective-permute-start.64 = (f32[2,4,6,10,1]{4,1,3,2,0:T(4,128)S(1)}, f32[2,4,6,10,1]{4,1,3,2,0:T(4,128)S(1)}, u32[]{:S(2)}, u32[]{:S(2)}) collective-permute-start(f32[2,4,6,10,1]{4,1,3,2,0:T(4,128)S(1)} %get-tuple-element.91), channel_id=1, source_target_pairs={{1,0},{3,2},{5,4},{7,6},{9,8},{11,10},{13,12},{15,14},{17,16},{19,... | collective-permute-start | bytes 5768 | tf_op jit(solution)/shard_map/ppermute | solution.py:23
  321.9 4.8 %collective-permute-start.68 = (f32[2,4,6,1,64]{4,1,3,2,0:T(4,128)S(1)}, f32[2,4,6,1,64]{4,1,3,2,0:T(4,128)S(1)}, u32[]{:S(2)}, u32[]{:S(2)}) collective-permute-start(f32[2,4,6,1,64]{4,1,3,2,0:T(4,128)S(1)} %copy.948), channel_id=1, source_target_pairs={{2,0},{4,2},{6,4},{3,1},{5,3},{7,5},{10,8},{12,10},{14,12},{11,9},... | collective-permute-start | bytes 36872 | tf_op jit(solution)/shard_map/ppermute | solution.py:23
  327.8 4.4 %collective-permute-start.70 = (f32[2,4,6,10,1]{4,1,3,2,0:T(4,128)S(1)}, f32[2,4,6,10,1]{4,1,3,2,0:T(4,128)S(1)}, u32[]{:S(2)}, u32[]{:S(2)}) collective-permute-start(f32[2,4,6,10,1]{4,1,3,2,0:T(4,128)S(1)} %get-tuple-element.87), channel_id=1, source_target_pairs={{1,0},{3,2},{5,4},{7,6},{9,8},{11,10},{13,12},{15,14},{17,16},{19,... | collective-permute-start | bytes 5768 | tf_op jit(solution)/shard_map/ppermute | solution.py:23
  352.0 4.8 %collective-permute-start.74 = (f32[2,4,10,1,128]{4,1,3,2,0:T(4,128)S(1)}, f32[2,4,10,1,128]{4,1,3,2,0:T(4,128)S(1)}, u32[]{:S(2)}, u32[]{:S(2)}) collective-permute-start(f32[2,4,10,1,128]{4,1,3,2,0:T(4,128)S(1)} %copy.958), channel_id=1, source_target_pairs={{2,0},{4,2},{6,4},{3,1},{5,3},{7,5},{10,8},{12,10},{14,12},{11,9},... | collective-permute-start | bytes 122888 | tf_op jit(solution)/shard_map/ppermute | solution.py:23
  366.0 5.5 %collective-permute-start.76 = (f32[2,4,10,18,1]{3,1,4,2,0:T(4,128)S(1)}, f32[2,4,10,18,1]{3,1,4,2,0:T(4,128)}, u32[]{:S(2)}, u32[]{:S(2)}) collective-permute-start(f32[2,4,10,18,1]{3,1,4,2,0:T(4,128)S(1)} %copy.964), channel_id=1, source_target_pairs={{1,0},{3,2},{5,4},{7,6},{9,8},{11,10},{13,12},{15,14},{17,16},{19,... | collective-permute-start | bytes 17288 | tf_op jit(solution)/shard_map/ppermute | solution.py:23
  395.1 5.4 %collective-permute-start.82 = (f32[2,4,10,18,1]{3,1,4,2,0:T(4,128)S(1)}, f32[2,4,10,18,1]{3,1,4,2,0:T(4,128)}, u32[]{:S(2)}, u32[]{:S(2)}) collective-permute-start(f32[2,4,10,18,1]{3,1,4,2,0:T(4,128)S(1)} %copy.974), channel_id=1, source_target_pairs={{1,0},{3,2},{5,4},{7,6},{9,8},{11,10},{13,12},{15,14},{17,16},{19,... | collective-permute-start | bytes 17288 | tf_op jit(solution)/shard_map/ppermute | solution.py:23
  (550 shorter events, 265.1 us)
Async XLA Ops:
  0.7 14.2 %collective-permute-start.1 = (f32[1,16,128]{2,1,0:T(8,128)S(1)}, f32[1,16,128]{2,1,0:T(8,128)S(1)}, u32[]{:S(2)}, u32[]{:S(2)}) collective-permute-start(f32[1,16,128]{2,1,0:T(8,128)S(1)} %get-tuple-element.156), channel_id=1, source_target_pairs={{0,8},{8,16},{16,24},{1,9},{9,17},{17,25},{2,10},{10,18},{18,26},{... | collective-permute-start | bytes 24584 | tf_op jit(solution)/shard_map/ppermute | solution.py:21
  2.0 12.9 %collective-permute-start = (f32[1,16,128]{2,1,0:T(8,128)S(1)}, f32[1,16,128]{2,1,0:T(8,128)S(1)}, u32[]{:S(2)}, u32[]{:S(2)}) collective-permute-start(f32[1,16,128]{2,1,0:T(8,128)S(1)} %get-tuple-element.155), channel_id=1, source_target_pairs={{8,0},{16,8},{24,16},{9,1},{17,9},{25,17},{10,2},{18,10},{26,18},{... | collective-permute-start | bytes 24584 | tf_op jit(solution)/shard_map/ppermute | solution.py:23
  23.6 11.9 %collective-permute-start.4 = (f32[10,18,1]{2,1,0:T(8,128)S(1)}, f32[10,18,1]{2,1,0:T(8,128)S(1)}, u32[]{:S(2)}, u32[]{:S(2)}) collective-permute-start(f32[10,18,1]{2,1,0:T(8,128)S(1)} %get-tuple-element.128), channel_id=1, source_target_pairs={{1,0},{3,2},{5,4},{7,6},{9,8},{11,10},{13,12},{15,14},{17,16},{19,... | collective-permute-start | bytes 2168 | tf_op jit(solution)/shard_map/ppermute | solution.py:23
  29.5 34.3 %collective-permute-start.13 = (f32[1,8,64]{2,1,0:T(8,128)S(1)}, f32[1,8,64]{2,1,0:T(8,128)S(1)}, u32[]{:S(2)}, u32[]{:S(2)}) collective-permute-start(f32[1,8,64]{2,1,0:T(8,128)S(1)} %get-tuple-element.174), channel_id=1, source_target_pairs={{0,8},{8,16},{16,24},{1,9},{9,17},{17,25},{2,10},{10,18},{18,26},{... | collective-permute-start | bytes 6152 | tf_op jit(solution)/shard_map/ppermute | solution.py:21
  30.8 33.0 %collective-permute-start.12 = (f32[1,8,64]{2,1,0:T(8,128)S(1)}, f32[1,8,64]{2,1,0:T(8,128)S(1)}, u32[]{:S(2)}, u32[]{:S(2)}) collective-permute-start(f32[1,8,64]{2,1,0:T(8,128)S(1)} %get-tuple-element.173), channel_id=1, source_target_pairs={{8,0},{16,8},{24,16},{9,1},{17,9},{25,17},{10,2},{18,10},{26,18},{... | collective-permute-start | bytes 6152 | tf_op jit(solution)/shard_map/ppermute | solution.py:23
  37.0 21.3 %collective-permute-start.6 = (f32[2,4,1,16,128]{4,3,2,1,0:T(8,128)S(1)}, f32[2,4,1,16,128]{4,3,2,1,0:T(8,128)S(1)}, u32[]{:S(2)}, u32[]{:S(2)}) collective-permute-start(f32[2,4,1,16,128]{4,3,2,1,0:T(8,128)S(1)} %get-tuple-element.68), channel_id=1, source_target_pairs={{8,0},{16,8},{24,16},{9,1},{17,9},{25,17},{10,2},{18,10},{26,18},{... | collective-permute-start | bytes 196616 | tf_op jit(solution)/shard_map/ppermute | solution.py:23
  39.1 19.2 %collective-permute-start.7 = (f32[2,4,1,16,128]{4,3,2,1,0:T(8,128)S(1)}, f32[2,4,1,16,128]{4,3,2,1,0:T(8,128)S(1)}, u32[]{:S(2)}, u32[]{:S(2)}) collective-permute-start(f32[2,4,1,16,128]{4,3,2,1,0:T(8,128)S(1)} %get-tuple-element.67), channel_id=1, source_target_pairs={{0,8},{8,16},{16,24},{1,9},{9,17},{17,25},{2,10},{10,18},{18,26},{... | collective-permute-start | bytes 196616 | tf_op jit(solution)/shard_map/ppermute | solution.py:21
  58.4 11.8 %collective-permute-start.8 = (f32[2,4,10,1,128]{4,1,3,2,0:T(4,128)S(1)}, f32[2,4,10,1,128]{4,1,3,2,0:T(4,128)S(1)}, u32[]{:S(2)}, u32[]{:S(2)}) collective-permute-start(f32[2,4,10,1,128]{4,1,3,2,0:T(4,128)S(1)} %copy.874), channel_id=1, source_target_pairs={{2,0},{4,2},{6,4},{3,1},{5,3},{7,5},{10,8},{12,10},{14,12},{11,9},... | collective-permute-start | bytes 122888 | tf_op jit(solution)/shard_map/ppermute | solution.py:23
  60.4 9.9 %collective-permute-start.9 = (f32[2,4,10,1,128]{4,1,3,2,0:T(4,128)S(1)}, f32[2,4,10,1,128]{4,1,3,2,0:T(4,128)S(1)}, u32[]{:S(2)}, u32[]{:S(2)}) collective-permute-start(f32[2,4,10,1,128]{4,1,3,2,0:T(4,128)S(1)} %copy.876), channel_id=1, source_target_pairs={{0,2},{2,4},{4,6},{1,3},{3,5},{5,7},{8,10},{10,12},{12,14},{9,11},... | collective-permute-start | bytes 122888 | tf_op jit(solution)/shard_map/ppermute | solution.py:21
  64.4 16.3 %collective-permute-start.14 = (f32[6,1,64]{2,1,0:T(1,128)}, f32[6,1,64]{2,1,0:T(1,128)}, u32[]{:S(2)}, u32[]{:S(2)}) collective-permute-start(f32[6,1,64]{2,1,0:T(1,128)} %get-tuple-element.168), channel_id=1, source_target_pairs={{2,0},{4,2},{6,4},{3,1},{5,3},{7,5},{10,8},{12,10},{14,12},{11,9},... | collective-permute-start | bytes 4616 | tf_op jit(solution)/shard_map/ppermute | solution.py:23
  67.2 13.5 %collective-permute-start.15 = (f32[6,1,64]{2,1,0:T(1,128)}, f32[6,1,64]{2,1,0:T(1,128)}, u32[]{:S(2)}, u32[]{:S(2)}) collective-permute-start(f32[6,1,64]{2,1,0:T(1,128)} %get-tuple-element.167), channel_id=1, source_target_pairs={{0,2},{2,4},{4,6},{1,3},{3,5},{5,7},{8,10},{10,12},{12,14},{9,11},... | collective-permute-start | bytes 4616 | tf_op jit(solution)/shard_map/ppermute | solution.py:21
  73.2 8.8 %collective-permute-start.11 = (f32[2,4,10,18,1]{3,1,4,2,0:T(4,128)}, f32[2,4,10,18,1]{3,1,4,2,0:T(4,128)S(1)}, u32[]{:S(2)}, u32[]{:S(2)}) collective-permute-start(f32[2,4,10,18,1]{3,1,4,2,0:T(4,128)} %copy.882), channel_id=1, source_target_pairs={{0,1},{2,3},{4,5},{6,7},{8,9},{10,11},{12,13},{14,15},{16,17},{18,... | collective-permute-start | bytes 17288 | tf_op jit(solution)/shard_map/ppermute | solution.py:21
  86.9 8.3 %collective-permute-start.18 = (f32[2,4,1,16,128]{4,3,2,1,0:T(8,128)S(1)}, f32[2,4,1,16,128]{4,3,2,1,0:T(8,128)S(1)}, u32[]{:S(2)}, u32[]{:S(2)}) collective-permute-start(f32[2,4,1,16,128]{4,3,2,1,0:T(8,128)S(1)} %get-tuple-element.66), channel_id=1, source_target_pairs={{8,0},{16,8},{24,16},{9,1},{17,9},{25,17},{10,2},{18,10},{26,18},{... | collective-permute-start | bytes 196616 | tf_op jit(solution)/shard_map/ppermute | solution.py:23
  92.6 9.3 %collective-permute-start.16 = (f32[6,10,1]{2,1,0:T(8,128)S(1)}, f32[6,10,1]{2,1,0:T(8,128)S(1)}, u32[]{:S(2)}, u32[]{:S(2)}) collective-permute-start(f32[6,10,1]{2,1,0:T(8,128)S(1)} %get-tuple-element.160), channel_id=1, source_target_pairs={{1,0},{3,2},{5,4},{7,6},{9,8},{11,10},{13,12},{15,14},{17,16},{19,... | collective-permute-start | bytes 728 | tf_op jit(solution)/shard_map/ppermute | solution.py:23
  93.9 8.0 %collective-permute-start.17 = (f32[6,10,1]{2,1,0:T(8,128)S(1)}, f32[6,10,1]{2,1,0:T(8,128)S(1)}, u32[]{:S(2)}, u32[]{:S(2)}) collective-permute-start(f32[6,10,1]{2,1,0:T(8,128)S(1)} %get-tuple-element.159), channel_id=1, source_target_pairs={{0,1},{2,3},{4,5},{6,7},{8,9},{10,11},{12,13},{14,15},{16,17},{18,... | collective-permute-start | bytes 728 | tf_op jit(solution)/shard_map/ppermute | solution.py:21
  143.8 10.8 %collective-permute-start.24 = (f32[2,4,1,8,64]{4,3,2,1,0:T(8,128)S(1)}, f32[2,4,1,8,64]{4,3,2,1,0:T(8,128)S(1)}, u32[]{:S(2)}, u32[]{:S(2)}) collective-permute-start(f32[2,4,1,8,64]{4,3,2,1,0:T(8,128)S(1)} %get-tuple-element.126), channel_id=1, source_target_pairs={{8,0},{16,8},{24,16},{9,1},{17,9},{25,17},{10,2},{18,10},{26,18},{... | collective-permute-start | bytes 49160 | tf_op jit(solution)/shard_map/ppermute | solution.py:23
  154.7 12.5 %collective-permute-start.27 = (f32[2,4,6,1,64]{4,1,3,2,0:T(4,128)S(1)}, f32[2,4,6,1,64]{4,1,3,2,0:T(4,128)S(1)}, u32[]{:S(2)}, u32[]{:S(2)}) collective-permute-start(f32[2,4,6,1,64]{4,1,3,2,0:T(4,128)S(1)} %copy.898), channel_id=1, source_target_pairs={{0,2},{2,4},{4,6},{1,3},{3,5},{5,7},{8,10},{10,12},{12,14},{9,11},... | collective-permute-start | bytes 36872 | tf_op jit(solution)/shard_map/ppermute | solution.py:21
  156.7 16.2 %collective-permute-start.32 = (f32[4,1,32]{2,1,0:T(1,128)S(1)}, f32[4,1,32]{2,1,0:T(1,128)S(1)}, u32[]{:S(2)}, u32[]{:S(2)}) collective-permute-start(f32[4,1,32]{2,1,0:T(1,128)S(1)} %get-tuple-element.178), channel_id=1, source_target_pairs={{2,0},{4,2},{6,4},{3,1},{5,3},{7,5},{10,8},{12,10},{14,12},{11,9},... | collective-permute-start | bytes 1544 | tf_op jit(solution)/shard_map/ppermute | solution.py:23
  161.0 11.9 %collective-permute-start.33 = (f32[4,1,32]{2,1,0:T(1,128)S(1)}, f32[4,1,32]{2,1,0:T(1,128)S(1)}, u32[]{:S(2)}, u32[]{:S(2)}) collective-permute-start(f32[4,1,32]{2,1,0:T(1,128)S(1)} %get-tuple-element.177), channel_id=1, source_target_pairs={{0,2},{2,4},{4,6},{1,3},{3,5},{5,7},{8,10},{10,12},{12,14},{9,11},... | collective-permute-start | bytes 1544 | tf_op jit(solution)/shard_map/ppermute | solution.py:21
  175.6 8.7 %collective-permute-start.36 = (f32[2,4,1,8,64]{4,3,2,1,0:T(8,128)S(1)}, f32[2,4,1,8,64]{4,3,2,1,0:T(8,128)S(1)}, u32[]{:S(2)}, u32[]{:S(2)}) collective-permute-start(f32[2,4,1,8,64]{4,3,2,1,0:T(8,128)S(1)} %get-tuple-element.124), channel_id=1, source_target_pairs={{8,0},{16,8},{24,16},{9,1},{17,9},{25,17},{10,2},{18,10},{26,18},{... | collective-permute-start | bytes 49160 | tf_op jit(solution)/shard_map/ppermute | solution.py:23
  184.4 8.8 %collective-permute-start.39 = (f32[2,4,6,1,64]{4,1,3,2,0:T(4,128)S(1)}, f32[2,4,6,1,64]{4,1,3,2,0:T(4,128)S(1)}, u32[]{:S(2)}, u32[]{:S(2)}) collective-permute-start(f32[2,4,6,1,64]{4,1,3,2,0:T(4,128)S(1)} %copy.906), channel_id=1, source_target_pairs={{0,2},{2,4},{4,6},{1,3},{3,5},{5,7},{8,10},{10,12},{12,14},{9,11},... | collective-permute-start | bytes 36872 | tf_op jit(solution)/shard_map/ppermute | solution.py:21
  194.3 8.0 %collective-permute-start.40 = (f32[2,4,6,10,1]{4,1,3,2,0:T(4,128)S(1)}, f32[2,4,6,10,1]{4,1,3,2,0:T(4,128)S(1)}, u32[]{:S(2)}, u32[]{:S(2)}) collective-permute-start(f32[2,4,6,10,1]{4,1,3,2,0:T(4,128)S(1)} %get-tuple-element.95), channel_id=1, source_target_pairs={{1,0},{3,2},{5,4},{7,6},{9,8},{11,10},{13,12},{15,14},{17,16},{19,... | collective-permute-start | bytes 5768 | tf_op jit(solution)/shard_map/ppermute | solution.py:23
  249.7 15.7 %collective-permute-start.52 = (f32[2,4,4,6,1]{4,2,3,1,0:T(4,128)S(1)}, f32[2,4,4,6,1]{4,2,3,1,0:T(4,128)S(1)}, u32[]{:S(2)}, u32[]{:S(2)}) collective-permute-start(f32[2,4,4,6,1]{4,2,3,1,0:T(4,128)S(1)} %get-tuple-element.135), channel_id=1, source_target_pairs={{1,0},{3,2},{5,4},{7,6},{9,8},{11,10},{13,12},{15,14},{17,16},{19,... | collective-permute-start | bytes 2312 | tf_op jit(solution)/shard_map/ppermute | solution.py:23
  254.1 11.3 %collective-permute-start.53 = (f32[2,4,4,6,1]{4,2,3,1,0:T(4,128)S(1)}, f32[2,4,4,6,1]{4,2,3,1,0:T(4,128)S(1)}, u32[]{:S(2)}, u32[]{:S(2)}) collective-permute-start(f32[2,4,4,6,1]{4,2,3,1,0:T(4,128)S(1)} %get-tuple-element.136), channel_id=1, source_target_pairs={{0,1},{2,3},{4,5},{6,7},{8,9},{10,11},{12,13},{14,15},{16,17},{18,... | collective-permute-start | bytes 2312 | tf_op jit(solution)/shard_map/ppermute | solution.py:21
  (141 other events, 1286.0 us)
where the time goes:
time: 414 us; the launch traced here: 407 us
  starting transfers between devices  234 us (57%)
  local copies, waits for them, and re-layouts  70.3 us (17%)
  waiting for transfers between devices  50.9 us (12%)
  other arithmetic  48.4 us (12%)
    ppermute x42, starting transfers between devices, padded(): lax.ppermute(head, axis, [((i + 1) % count, i) for i in range(ends)])  156 us
    ppermute x42, starting transfers between devices, padded(): lax.ppermute(tail, axis, [(i, (i + 1) % count) for i in range(ends)])  77.8 us
    ppermute x42, waiting for transfers between devices, padded(): lax.ppermute(tail, axis, [(i, (i + 1) % count) for i in range(ends)])  45.2 us
    reduce_sum x8, other arithmetic, restrict(): return jnp.mean(blocks, axis=(-5, -3, -1))  26.4 us
    reshape x3, local copies, waits for them, and re-layouts, restrict(): blocks = field.reshape(lead + (sx // 2, 2, sy // 2, 2, sz // 2, 2))  17.3 us
    sub x1, local copies, waits for them, and re-layouts, local(): coarse_rhs = restrict(rhs - apply_op(fine_pad(fine), level0))  8.81 us
  transfers between devices with their start and end apart: 84, of which 24 were waited for; matrix products, arithmetic and copies ran while one was open for 11% of the time, Pallas kernels for 0%

commit v1 on v0

--- a/solution.py
+++ b/solution.py
@@ -1,6 +1,8 @@
 import jax
 import jax.numpy as jnp
 from jax import lax
+from jax.experimental import pallas as pl
+from jax.experimental.pallas import tpu as pltpu
 from jax.sharding import PartitionSpec as P
 
 NU = 2
@@ -89,11 +91,7 @@
     return jnp.repeat(jnp.repeat(jnp.repeat(field, 2, -3), 2, -2), 2, -1)
 
 
-def fine_pad(field):
-    return padded(field, (("gx", 2), ("gy", 3), ("gz", 4)), 1)
-
-
-def coarse_pad(field):
+def field_pad(field):
     return padded(field, (("gx", 2), ("gy", 3), ("gz", 4)), 1)
 
 
@@ -101,27 +99,455 @@
     return padded(rho, (("gx", 0), ("gy", 1), ("gz", 2)), 1)
 
 
-def local(rhs, density, shift_real, shift_imag):
+def local_general(rhs, density, shift_real, shift_imag):
     rho1, sr1, si1 = (restrict(density), restrict(shift_real), restrict(shift_imag))
     level1 = make_level(brick_density(rho1), sr1, si1, 0.25)
     rho2, sr2, si2 = (restrict(rho1), restrict(sr1), restrict(si1))
     level0 = make_level(brick_density(density), shift_real, shift_imag, 1.0)
     fine = precondition(rhs, level0)
-    fine = smooth(fine, rhs, level0, fine_pad, NU - 1)
-    coarse_rhs = restrict(rhs - apply_op(fine_pad(fine), level0))
+    fine = smooth(fine, rhs, level0, field_pad, NU - 1)
+    coarse_rhs = restrict(rhs - apply_op(field_pad(fine), level0))
     middle = precondition(coarse_rhs, level1)
-    middle = smooth(middle, coarse_rhs, level1, coarse_pad, NU - 1)
-    lowest_rhs = restrict(coarse_rhs - apply_op(coarse_pad(middle), level1))
+    middle = smooth(middle, coarse_rhs, level1, field_pad, NU - 1)
+    lowest_rhs = restrict(coarse_rhs - apply_op(field_pad(middle), level1))
     level2 = make_level(brick_density(rho2), sr2, si2, 0.0625)
     lowest = precondition(lowest_rhs, level2)
-    lowest = smooth(lowest, lowest_rhs, level2, coarse_pad, CSWEEPS - 1)
-    middle = smooth(middle + prolong(lowest), coarse_rhs, level1, coarse_pad, NU)
+    lowest = smooth(lowest, lowest_rhs, level2, field_pad, CSWEEPS - 1)
+    middle = smooth(middle + prolong(lowest), coarse_rhs, level1, field_pad, NU)
     corrected = fine + prolong(middle)
-    fine = smooth(corrected, rhs, level0, fine_pad, NU)
-    return fine
+    return smooth(corrected, rhs, level0, field_pad, NU)
+
+
+HALO = 2
+MIB = 1 << 20
+F32 = jnp.float32
+
+
+def loop(count, body):
+    lax.fori_loop(0, count, lambda i, c: (body(i), c)[1], 0)
+
+
+def safe(total):
+    return jnp.where(total > 0.0, total, 1.0)
+
+
+def level_coefs(rho, sr, si, scale, bx, by, bz, wr, wi, dr, step):
+    n, ny, nz = sr.shape
+    two = 2.0 * scale
+    bx[pl.ds(0, 1)] = two / safe(rho[pl.ds(0, 1)] + rho[pl.ds(1, 1)])
+
+    def body(i):
+        p = i * step
+        r = rho[pl.ds(p + 1, step)]
+        row = lax.broadcasted_iota(jnp.int32, r.shape, 1)
+        lane = lax.broadcasted_iota(jnp.int32, r.shape, 2)
+        bx[pl.ds(p + 1, step)] = two / safe(r + rho[pl.ds(p + 2, step)])
+        edge = two / safe(r)
+        bsum = bx[pl.ds(p, step)] + bx[pl.ds(p + 1, step)]
+        last = row == ny - 1
+        up = jnp.where(last, 0.0, pltpu.roll(r, ny - 1, 1))
+        face = two / safe(r + up)
+        bsum = bsum + face + jnp.where(row == 0, edge, pltpu.roll(face, 1, 1))
+        by[pl.ds(p, step)] = jnp.where(last, 0.0, face)
+        last = lane == nz - 1
+        up = jnp.where(last, 0.0, pltpu.roll(r, nz - 1, 2))
+        face = two / safe(r + up)
+        bsum = bsum + face + jnp.where(lane == 0, edge, pltpu.roll(face, 1, 2))
+        bz[pl.ds(p, step)] = jnp.where(last, 0.0, face)
+        d = bsum - sr[pl.ds(p, step)]
+        e = si[pl.ds(p, step)]
+        w = jnp.where(r > 0.0, omega_damp, 0.0) / (d * d + e * e)
+        wr[pl.ds(p, step)] = w * d
+        wi[pl.ds(p, step)] = w * e
+        dr[pl.ds(p, step)] = d
+
+    loop(n // step, body)
+
+
+def near(u, at, c, p, step, bx, by, bz):
+    mid = u[c, pl.ds(at, step)]
+    ny, nz = mid.shape[1:]
+    b = by[pl.ds(p, step)]
+    total = bx[pl.ds(p, step)] * u[c, pl.ds(at - 1, step)] + bx[pl.ds(p + 1, step)] * u[c, pl.ds(at + 1, step)]
+    total = total + (b * pltpu.roll(mid, ny - 1, 1) + pltpu.roll(b * mid, 1, 1))
+    b = bz[pl.ds(p, step)]
+    return mid, total + (b * pltpu.roll(mid, nz - 1, 2) + pltpu.roll(b * mid, 1, 2))
+
+
+def weigh(tr, ti, p, step, wr, wi):
+    a, b = wr[pl.ds(p, step)], wi[pl.ds(p, step)]
+    return a * tr - b * ti, a * ti + b * tr
+
+
+def sweep_planes(u, at, g, gat, p, step, coefs):
+    bx, by, bz, wr, wi = coefs
+    mr, nr = near(u, at, 0, p, step, bx, by, bz)
+    mi, ni = near(u, at, 1, p, step, bx, by, bz)
+    vr, vi = weigh(g[0, pl.ds(gat, step)] + nr, g[1, pl.ds(gat, step)] + ni, p, step, wr, wi)
+    rest = 1.0 - omega_damp
+    return rest * mr + vr, rest * mi + vi
+
+
+def resid_planes(u, at, g, gat, p, step, coefs, dr, si):
+    bx, by, bz = coefs[:3]
+    mr, nr = near(u, at, 0, p, step, bx, by, bz)
+    mi, ni = near(u, at, 1, p, step, bx, by, bz)
+    d, e = dr[pl.ds(p, step)], si[pl.ds(p, step)]
+    return g[0, pl.ds(gat, step)] + nr - (d * mr + e * mi), g[1, pl.ds(gat, step)] + ni - (d * mi - e * mr)
+
+
+def pick(nrow, ncol, down, value):
+    row = lax.broadcasted_iota(jnp.int32, (nrow, ncol), 0)
+    col = lax.broadcasted_iota(jnp.int32, (nrow, ncol), 1)
+    hit = (row // 2 == col) if down else (row == col // 2)
+    return jnp.where(hit, value, 0.0).astype(F32)
+
+
+def dot(a, b):
+    return jnp.dot(a, b, precision=lax.Precision.HIGHEST, preferred_element_type=F32)
+
+
+def send_kernel(rhs, rho, sr, si, out):
+    half = out.shape[1]
+    at = (1 - lax.axis_index("gz")) * half
+    m = rhs.shape[1]
+    for c in range(2):
+        for r in range(m):
+            out[2 * r + c] = rhs[c, r, pl.ds(at, half)]
+    for j, ref in enumerate((rho, sr, si)):
+        out[2 * m + j] = ref[pl.ds(at, half)]
+
+
+def spread_kernel(rhs, rho, sr, si, came, out):
+    half = came.shape[1]
+    at = lax.axis_index("gz") * half
+    m = rhs.shape[1]
+    for r in range(m):
+        for c in range(2):
+            out[r, 0, c] = rhs[c, r, pl.ds(at, half)]
+            out[r, 1, c] = came[2 * r + c]
+        for j, ref in enumerate((rho, sr, si)):
+            out[r, 0, 2 + j] = ref[pl.ds(at, half)]
+            out[r, 1, 2 + j] = came[2 * m + j]
+
+
+def edge_kernel(blocks, over_gz, over_gx):
+    k = lax.axis_index("gz")
+    half = blocks.shape[3]
+    for out, high in ((over_gz, 1 - k), (over_gx, k)):
+        two, three = high * (half - HALO), high * (half - HALO - 1)
+        for s in range(blocks.shape[0]):
+            for t in range(2):
+                for j, f in enumerate((0, 1, 3, 4)):
+                    out[s, t, pl.ds(HALO * j, HALO)] = blocks[s, t, f, pl.ds(two, HALO)]
+                out[s, t, pl.ds(4 * HALO, HALO + 1)] = blocks[s, t, 2, pl.ds(three, HALO + 1)]
+
+
+def fine_kernel(blocks, from_gz, from_gx, own, up_gz, up_gx, packed, g, bx, by, bz, wr, wi, rho, sr, si, dr, ua, ub, sums, narrow):
+    k = lax.axis_index("gz")
+    nsrc, _, _, half, rows, lanes = blocks.shape
+    ny, nz = g.shape[2:]
+
+    def place(ref, first, count, s, z, value):
+        ref[pl.ds(first, count), s * rows : (s + 1) * rows, pl.ds(pl.multiple_of(z * lanes, lanes), lanes)] = value
+
+    for s in range(nsrc):
+        for t in range(2):
+            z = k if t == 0 else 1 - k
+            for f, ref in ((0, g.at[0]), (1, g.at[1]), (3, sr), (4, si)):
+                place(ref, HALO, half, s, z, blocks[s, t, f])
+            place(rho, HALO + 1, half, s, z, blocks[s, t, 2])
+
+    def halo(came, low):
+        for s in range(nsrc):
+            for t in range(2):
+                z = 1 - k if t == 0 else k
+                first = 0 if low else half + HALO
+                for j, ref in enumerate((g.at[0], g.at[1], sr, si)):
+                    place(ref, first, HALO, s, z, came[s, t, HALO * j : HALO * (j + 1)])
+                place(rho, 0 if low else half + HALO + 1, HALO + 1, s, z, came[s, t, 4 * HALO : 5 * HALO + 1])
+
+    @pl.when(k == 0)
+    def _():
+        halo(from_gx, True)
+        halo(from_gz, False)
+
+    @pl.when(k == 1)
+    def _():
+        halo(from_gz, True)
+        halo(from_gx, False)
+
+    level_coefs(rho, sr, si, 1.0, bx, by, bz, wr, wi, dr, 1)
+    coefs = (bx, by, bz, wr, wi)
+
+    def first(p):
+        ua[0, pl.ds(p, 1)], ua[1, pl.ds(p, 1)] = weigh(g[0, pl.ds(p, 1)], g[1, pl.ds(p, 1)], p, 1, wr, wi)
+
+    loop(half + 2 * HALO, first)
+
+    def second(i):
+        p = i + 1
+        ub[0, pl.ds(p, 1)], ub[1, pl.ds(p, 1)] = sweep_planes(ua, p, g, p, p, 1, coefs)
+
+    loop(half + 2 * HALO - 2, second)
+    for c in range(2):
+        own[c] = ub[c, pl.ds(HALO, half)]
+        up_gz[c] = ub[c, pl.ds(HALO + (1 - k) * (half - HALO), HALO)]
+        up_gx[c] = ub[c, pl.ds(HALO + k * (half - HALO), HALO)]
+
+    pairs = half // 2
+
+    def down(q):
+        p = HALO + 2 * q
+        ar, ai = resid_planes(ub, p, g, p, p, 1, coefs, dr, si)
+        br, bi = resid_planes(ub, p + 1, g, p + 1, p + 1, 1, coefs, dr, si)
+        totals = (ar + br, ai + bi, rho[pl.ds(p + 1, 1)] + rho[pl.ds(p + 2, 1)], sr[pl.ds(p, 1)] + sr[pl.ds(p + 1, 1)], si[pl.ds(p, 1)] + si[pl.ds(p + 1, 1)])
+        for j, v in enumerate(totals):
+            sums[pl.ds(pl.multiple_of((j * pairs + q) * ny, ny), ny), :] = v[0]
+
+    loop(pairs, down)
+    narrow[...] = dot(sums[...], pick(nz, nz // 2, True, 0.125))
+    n = 5 * pairs * ny // 2
+    done = (narrow[pl.ds(0, n, 2), :] + narrow[pl.ds(1, n, 2), :]).reshape(5, pairs, ny // 2, nz // 2)
+    for d in range(packed.shape[0]):
+        packed[d] = done
+
+
+def coarse_kernel(
+    mine, other, own, from_gz, from_gx, g0, bx0, by0, bz0, wr0, wi0, out,
+    rho1, sr1, si1, g1, bx1, by1, bz1, wr1, wi1, dr1, ua1, ub1,
+    rho2, sr2, si2, g2, bx2, by2, bz2, wr2, wi2, dr2, ua2, ub2,
+    sums, narrow, wide, tall, ua0, ub0,
+):
+    k = lax.axis_index("gz")
+    chip = lax.axis_index("gx")
+    chips, _, pairs, ny, nz = mine.shape
+    n1 = sr1.shape[0]
+    zero = jnp.zeros((1, ny, nz), F32)
+    rho1[pl.ds(0, 1)] = zero
+    rho1[pl.ds(n1 + 1, 1)] = zero
+    for u in (ua1, ub1):
+        for c in range(2):
+            u[c, pl.ds(0, 1)] = zero
+            u[c, pl.ds(n1 + 1, 1)] = zero
+    for s in range(chips):
+        for ref, z in ((mine, k), (other, 1 - k)):
+            at = 2 * pairs * s + pairs * z
+            for c in range(2):
+                g1[c, pl.ds(at, pairs)] = ref[s, c]
+            rho1[pl.ds(at + 1, pairs)] = ref[s, 2]
+            sr1[pl.ds(at, pairs)] = ref[s, 3]
+            si1[pl.ds(at, pairs)] = ref[s, 4]
+    step1 = 4
+    level_coefs(rho1, sr1, si1, 0.25, bx1, by1, bz1, wr1, wi1, dr1, step1)
+    coefs1 = (bx1, by1, bz1, wr1, wi1)
+
+    def first(i):
+        p = i * step1
+        r, m = weigh(g1[0, pl.ds(p, step1)], g1[1, pl.ds(p, step1)], p, step1, wr1, wi1)
+        ua1[0, pl.ds(p + 1, step1)], ua1[1, pl.ds(p + 1, step1)] = r, m
+
+    loop(n1 // step1, first)
+
+    def sweep1(src, dst):
+        def body(i):
+            p = i * step1
+            r, m = sweep_planes(src, p + 1, g1, p, p, step1, coefs1)
+            dst[0, pl.ds(p + 1, step1)], dst[1, pl.ds(p + 1, step1)] = r, m
+
+        loop(n1 // step1, body)
+
+    sweep1(ua1, ub1)
+    n2 = n1 // 2
+    ny2 = ny // 2
+
+    def down(q):
+        p = 2 * q
+        r, m = resid_planes(ub1, p + 1, g1, p, p, 2, coefs1, dr1, si1)
+        totals = (r[0] + r[1], m[0] + m[1], rho1[p + 1] + rho1[p + 2], sr1[p] + sr1[p + 1], si1[p] + si1[p + 1])
+        for j, v in enumerate(totals):
+            sums[pl.ds(pl.multiple_of((j * n2 + q) * ny, ny), ny), :] = v
+
+    loop(n2, down)
+    narrow[...] = dot(sums[...], pick(nz, nz, True, 0.125))
+    n = n2 * ny2
+    zero2 = jnp.zeros((1, ny2, nz), F32)
+    rho2[pl.ds(0, 1)] = zero2
+    rho2[pl.ds(n2 + 1, 1)] = zero2
+    for u in (ua2, ub2):
+        for c in range(2):
+            u[c, pl.ds(0, 1)] = zero2
+            u[c, pl.ds(n2 + 1, 1)] = zero2
+    for j, ref in enumerate((g2.at[0], g2.at[1], rho2.at[pl.ds(1, n2)], sr2, si2)):
+        at = 2 * n * j
+        ref[...] = (narrow[pl.ds(at, n, 2), :] + narrow[pl.ds(at + 1, n, 2), :]).reshape(n2, ny2, nz)
+    level_coefs(rho2, sr2, si2, 0.0625, bx2, by2, bz2, wr2, wi2, dr2, n2)
+    coefs2 = (bx2, by2, bz2, wr2, wi2)
+    ua2[0, pl.ds(1, n2)], ua2[1, pl.ds(1, n2)] = weigh(g2[0], g2[1], 0, n2, wr2, wi2)
+    src, dst = ua2, ub2
+    for _ in range(CSWEEPS - 1):
+        dst[0, pl.ds(1, n2)], dst[1, pl.ds(1, n2)] = sweep_planes(src, 1, g2, 0, 0, n2, coefs2)
+        src, dst = dst, src
+
+    widen = pick(nz, nz, False, 1.0)
+    for c in range(2):
+        wide[pl.ds(c * n, n), :] = dot(src[c, pl.ds(1, n2)].reshape(n, nz), widen)
+    twice = wide[pl.ds(0, 2 * n), :]
+    tall[pl.ds(0, 2 * n, 2), :] = twice
+    tall[pl.ds(1, 2 * n, 2), :] = twice
+
+    def lift(q):
+        for c in range(2):
+            v = tall[pl.ds(pl.multiple_of((c * n2 + q) * ny, ny), ny), :]
+            for j in range(2):
+                ub1[c, 2 * q + j + 1] = ub1[c, 2 * q + j + 1] + v
+
+    loop(n2, lift)
+    sweep1(ub1, ua1)
+    sweep1(ua1, ub1)
+
+    half = own.shape[1]
+    pad = half + 2 * HALO
+    quads = pad // 2
+    base = (2 * chip + k) * pairs
+    fine_z = own.shape[3]
+    fine_y = own.shape[2]
+    rows = quads * ny
+
+    @pl.when(k == 0)
+    def _():
+        ua0[:, pl.ds(0, HALO)] = from_gx[...]
+        ua0[:, pl.ds(HALO + half, HALO)] = from_gz[...]
+
+    @pl.when(k == 1)
+    def _():
+        ua0[:, pl.ds(0, HALO)] = from_gz[...]
+        ua0[:, pl.ds(HALO + half, HALO)] = from_gx[...]
+
+    ua0[:, pl.ds(HALO, half)] = own[...]
+    for h in range(fine_z // nz):
+        col = lax.broadcasted_iota(jnp.int32, (nz, nz), 1) + h * nz
+        row = lax.broadcasted_iota(jnp.int32, (nz, nz), 0)
+        widen = jnp.where(row == col // 2, 1.0, 0.0).astype(F32)
+        for c in range(2):
+            v = dot(ub1[c, pl.ds(base, quads)].reshape(rows, nz), widen)
+            tall[pl.ds(0, rows, 2), :] = v
+            tall[pl.ds(1, rows, 2), :] = v
+            for q in range(quads):
+                w = tall[pl.ds(q * fine_y, fine_y), :]
+                for j in range(2):
+                    p = 2 * q + j
+                    ua0[c, p, :, h * nz : (h + 1) * nz] = ua0[c, p, :, h * nz : (h + 1) * nz] + w
+    coefs0 = (bx0, by0, bz0, wr0, wi0)
+
+    def third(i):
+        p = i + 1
+        ub0[0, pl.ds(p, 1)], ub0[1, pl.ds(p, 1)] = sweep_planes(ua0, p, g0, p, p, 1, coefs0)
+
+    loop(pad - 2, third)
+    dests, _, _, _, drows, lanes = out.shape
+
+    def fourth(i):
+        p = i + HALO
+        r, m = sweep_planes(ub0, p, g0, p, p, 1, coefs0)
+        for c, v in enumerate((r, m)):
+            for d in range(dests):
+                for z in range(2):
+                    slot = jnp.where(k == z, 0, 1)
+                    out[d, slot, c, i] = v[0, d * drows : (d + 1) * drows, z * lanes : (z + 1) * lanes]
+
+    loop(half, fourth)
+
+
+def gather_kernel(kept, came, out):
+    half = kept.shape[3]
+    k = lax.axis_index("gz")
+    for r in range(kept.shape[0]):
+        for c in range(2):
+            out[c, r, pl.ds(k * half, half)] = kept[r, 0, c]
+            out[c, r, pl.ds((1 - k) * half, half)] = came[r, c]
+
+
+def call(kernel, outs, args, scratch=(), limit=24):
+    vm = pl.BlockSpec(memory_space=pltpu.VMEM)
+    single = not isinstance(outs, list)
+    shapes = [outs] if single else outs
+    result = pl.pallas_call(
+        kernel,
+        out_shape=[jax.ShapeDtypeStruct(s, F32) for s in shapes],
+        in_specs=[vm] * len(args),
+        out_specs=[vm] * len(shapes),
+        scratch_shapes=[pltpu.VMEM(s, F32) for s in scratch],
+        compiler_params=pltpu.CompilerParams(vmem_limit_bytes=limit * MIB),
+    )(*args)
+    return result[0] if single else result
+
+
+def local_planes(rhs, density, shift_real, shift_imag):
+    _, m, xs, rows, lanes = rhs.shape
+    half = xs // 2
+    chips = lax.axis_size("gx")
+    ny, nz = rows * m, 2 * lanes
+    pad = half + 2 * HALO
+    swap = [(0, 1), (1, 0)]
+    ends = [p for c in range(chips - 1) for p in ((2 * c + 1, 2 * c + 2), (2 * c + 2, 2 * c + 1))]
+    fields = (rhs, density, shift_real, shift_imag)
+
+    away = call(send_kernel, (2 * m + 3, half, rows, lanes), fields)
+    came = lax.ppermute(away, "gz", swap)
+    spread = call(spread_kernel, (m, 2, 5, half, rows, lanes), fields + (came,))
+    blocks = lax.all_to_all(spread, "gy", 0, 0, tiled=True)
+
+    edges = (m, 2, 5 * HALO + 1, rows, lanes)
+    to_gz, to_gx = call(edge_kernel, [edges, edges], (blocks,))
+    from_gx = lax.ppermute(to_gx, ("gx", "gz"), ends)
+    from_gz = lax.ppermute(to_gz, "gz", swap)
+
+    pairs = half // 2
+    plane = (ny, nz)
+    own, up_gz, up_gx, packed, g, bx, by, bz, wr, wi = call(
+        fine_kernel,
+        [(2, half) + plane, (2, HALO) + plane, (2, HALO) + plane, (chips, 5, pairs, ny // 2, nz // 2), (2, pad) + plane, (pad + 1,) + plane]
+        + [(pad,) + plane] * 4,
+        (blocks, from_gz, from_gx),
+        scratch=[(pad + 2,) + plane] + [(pad,) + plane] * 3 + [(2, pad) + plane] * 2 + [(5 * pairs * ny, nz), (5 * pairs * ny, nz // 2)],
+        limit=40,
+    )
+    u_gx = lax.ppermute(up_gx, ("gx", "gz"), ends)
+    u_gz = lax.ppermute(up_gz, "gz", swap)
+    mine = lax.all_to_all(packed, "gx", 0, 0, tiled=True)
+    other = lax.ppermute(mine, "gz", swap)
+
+    n1, n2 = chips * xs // 2, chips * xs // 4
+    p1, p2 = (ny // 2, nz // 2), (ny // 4, nz // 2)
+
+    def level(n, p):
+        return [(n + 2,) + p, (n,) + p, (n,) + p, (2, n) + p, (n + 1,) + p] + [(n,) + p] * 5 + [(2, n + 2) + p] * 2
+
+    tall = max(2 * n2 * p1[0], pad * ny // 2 * 2)
+    result = call(
+        coarse_kernel,
+        (m, 2, 2, half, rows, lanes),
+        (mine, other, own, u_gz, u_gx, g, bx, by, bz, wr, wi),
+        scratch=level(n1, p1)
+        + level(n2, p2)
+        + [(5 * n2 * p1[0], p1[1])] * 2
+        + [(2 * n2 * p2[0], p1[1]), (tall, p1[1]), (2, pad) + plane, (2, pad) + plane],
+        limit=40,
+    )
+    back = lax.all_to_all(result, "gy", 0, 0, tiled=True)
+    last = lax.ppermute(back[:, 1], "gz", swap)
+    return call(gather_kernel, rhs.shape, (back, last))
 
 
 def solution(mesh):
+    sizes = dict(mesh.shape)
+
+    def local(rhs, density, shift_real, shift_imag):
+        _, m, xs, rows, lanes = rhs.shape
+        planes = sizes["gz"] == 2 and sizes["gy"] == m and xs % 8 == 0 and rows % 16 == 0 and lanes == 128
+        return (local_planes if planes else local_general)(rhs, density, shift_real, shift_imag)
+
     placed = (
         P(None, None, "gx", "gy", "gz"),
         P("gx", "gy", "gz"),

time: 414 us -> 94.1 us (0.23)
  the two profiles are of different devices: /device:TPU:29 before, /device:TPU:0 now
where the time goes in v1:
time: 94.1 us; the launch traced here: 92.7 us
  blocking collectives  63.7 us (68%)
  Pallas kernels  13 us (14%)
  starting transfers between devices  7.1 us (8%)
  waiting for transfers between devices  5.22 us (6%)
  local copies, waits for them, and re-layouts  3.58 us (4%)
    all_to_all x1, blocking collectives, local_planes(): mine = lax.all_to_all(packed, 'gx', 0, 0, tiled=True)  32 us
    all_to_all x1, blocking collectives, local_planes(): blocks = lax.all_to_all(spread, 'gy', 0, 0, tiled=True)  22.1 us
    pallas_call x6, Pallas kernels, call(): pl.pallas_call(kernel, out_shape=[jax.ShapeDtypeStruct(s, F32) for s in s...  13 us
    all_to_all x1, blocking collectives, local_planes(): back = lax.all_to_all(result, 'gy', 0, 0, tiled=True)  9.53 us
    ppermute x1, starting transfers between devices, local_planes(): last = lax.ppermute(back[:, 1], 'gz', swap)  4.63 us
    unnamed x8, local copies, waits for them, and re-layouts  3.56 us
  transfers between devices with their start and end apart: 7, of which 4 were waited for; matrix products, arithmetic and copies ran while one was open for 0% of the time, Pallas kernels for 0%

profile of v1, /device:TPU:0, one launch (start us, length us, event | category | flops | bytes accessed | tf_op | source)
XLA Modules:
  0.0 92.7 jit_solution(12571031417615428156)
XLA Ops:
  0.0 1.0 %copy-done = f32[2,4,8,16,128]{4,3,2,1,0:T(8,128)S(1)} copy-done((f32[2,4,8,16,128]{4,3,2,1,0:T(8,128)S(1)}, f32[2,4,8,16,128]{4,3,2,1,0:T(8,128)}, u32[]{:S(2)}) %copy-start) | copy-done | bytes 524312
  1.0 0.8 copy-done.1
  1.9 0.8 copy-done.2
  2.7 0.8 copy-done.3
  3.6 0.5 collective-permute-start
  4.1 1.3 %collective-permute-done.came = f32[11,4,16,128]{3,2,1,0:T(8,128)S(1)} collective-permute-done((f32[11,4,16,128]{3,2,1,0:T(8,128)S(1)}, f32[11,4,16,128]{3,2,1,0:T(8,128)S(1)}, u32[]{:S(2)}, u32[]{:S(2)}) %collective-permute-start) | collective-permute-done | bytes 360480 | tf_op jit(solution)/shard_map/ppermute | solution.py:497
  5.4 0.1 shard_map.47
  5.5 22.1 %all_to_all.15.blocks = f32[4,2,5,4,16,128]{5,4,3,2,1,0:T(8,128)S(1)} all-to-all(f32[4,2,5,4,16,128]{5,4,3,2,1,0:T(8,128)S(1)} %shard_map.47), channel_id=1, replica_groups=mesh['gx'=4,'gy'=4,'gz'=2] {'gy'}, dimensions={0} | all-to-all | bytes 2621440 | tf_op jit(solution)/shard_map/all_to_all | solution.py:499
  27.6 0.1 shard_map.48
  27.7 0.1 collective-permute-start.1
  27.8 0.7 collective-permute-start.2
  28.5 1.5 %collective-permute-done.1.from_gz = f32[4,2,11,16,128]{4,3,2,1,0:T(8,128)S(1)} collective-permute-done((f32[4,2,11,16,128]{4,3,2,1,0:T(8,128)S(1)}, f32[4,2,11,16,128]{4,3,2,1,0:T(8,128)S(1)}, u32[]{:S(2)}, u32[]{:S(2)}) %collective-permute-start.1) | collective-permute-done | bytes 720928 | tf_op jit(solution)/shard_map/ppermute | solution.py:504
  30.0 0.0 collective-permute-done.2.from_gx
  30.0 4.4 %shard_map.49 = (f32[2,4,64,256]{3,2,1,0:T(8,128)S(1)}, f32[2,2,64,256]{3,2,1,0:T(8,128)S(1)}, f32[2,2,64,256]{3,2,1,0:T(8,128)S(1)}, f32[4,5,2,32,128]{4,3,2,1,...) custom-call(f32[4,2,5,4,16,128]{5,4,3,2,1,0:T(8,128)S(1)} %all_to_al, ...), custom_call_target="tpu_custom_call" | custom-call | tf_op jit(solution)/shard_map/pallas_call | solution.py:475
  34.4 32.0 %all_to_all.16.mine = f32[4,5,2,32,128]{4,3,2,1,0:T(8,128)S(1)} all-to-all(f32[4,5,2,32,128]{4,3,2,1,0:T(8,128)S(1)} %get-tuple-element.19), channel_id=1, replica_groups=mesh['gx'=4,'gy'=4,'gz'=2] {'gx'}, dimensions={0} | all-to-all | bytes 1310720 | tf_op jit(solution)/shard_map/all_to_all | solution.py:518
  66.4 0.0 collective-permute-start.3
  66.4 0.5 collective-permute-start.4
  66.9 0.7 collective-permute-start.5
  67.6 1.3 %collective-permute-done.4.from_gz = f32[2,2,64,256]{3,2,1,0:T(8,128)S(1)} collective-permute-done((f32[2,2,64,256]{3,2,1,0:T(8,128)S(1)}, f32[2,2,64,256]{3,2,1,0:T(8,128)S(1)}, u32[]{:S(2)}, u32[]{:S(2)}) %collective-permute-start.4) | collective-permute-done | bytes 262176 | tf_op jit(solution)/shard_map/ppermute | solution.py:517
  68.9 7.6 %shard_map.50 = f32[4,2,2,4,16,128]{5,4,3,2,1,0:T(8,128)S(1)} custom-call(f32[4,5,2,32,128]{4,3,2,1,0:T(8,128)S(1)} %all_to_all.16.mine, f32[4,5,2,32,128]{4,3,2,1,0:T(8,128)S(1)} %collective-permute-done.3.other, f32[2,4,64,256]{3,2,1,0:T(8,128)S(1)} %get-tuple-element.20.own, f32[2,2,64,256]{3,2,1,0:T(8,128)S(1)} %collective-permute-done.4.from_gz, ...), custom_call_target="tpu_custom_call" | custom-call | tf_op jit(solution)/shard_map/pallas_call | solution.py:475
  76.5 9.5 %all_to_all.17.kept = f32[4,2,2,4,16,128]{5,4,3,2,1,0:T(8,128)S(1)} all-to-all(f32[4,2,2,4,16,128]{5,4,3,2,1,0:T(8,128)S(1)} %shard_map.50), channel_id=1, replica_groups=mesh['gx'=4,'gy'=4,'gz'=2] {'gy'}, dimensions={0} | all-to-all | bytes 1048576 | tf_op jit(solution)/shard_map/all_to_all | solution.py:538
  86.1 4.6 %collective-permute-start.6 = (f32[4,2,4,16,128]{4,3,2,1,0:T(8,128)S(1)}, f32[4,2,4,16,128]{4,3,2,1,0:T(8,128)S(1)}, u32[]{:S(2)}, u32[]{:S(2)}) collective-permute-start(f32[4,2,4,16,128]{4,3,2,1,0:T(8,128)S(1)} %slice_bitcast_fusion), channel_id=1, source_target_pairs={{0,1},{1,0},{2,3},{3,2},{4,5},{5,4},{6,7},{7,6},{8,9},{9,8},{10,11... | collective-permute-start | bytes 786440 | tf_op jit(solution)/shard_map/ppermute | solution.py:539
  90.7 1.2 %collective-permute-done.6.came = f32[4,2,4,16,128]{4,3,2,1,0:T(8,128)S(1)} collective-permute-done((f32[4,2,4,16,128]{4,3,2,1,0:T(8,128)S(1)}, f32[4,2,4,16,128]{4,3,2,1,0:T(8,128)S(1)}, u32[]{:S(2)}, u32[]{:S(2)}) %collective-permute-start.6) | collective-permute-done | bytes 262176 | tf_op jit(solution)/shard_map/ppermute | solution.py:539
  91.8 0.8 shard_map.51
  (8 shorter events, 0.1 us)
Async XLA Ops:
  0.0 1.0 %copy-start = (f32[2,4,8,16,128]{4,3,2,1,0:T(8,128)S(1)}, f32[2,4,8,16,128]{4,3,2,1,0:T(8,128)}, u32[]{:S(2)}) copy-start(f32[2,4,8,16,128]{4,3,2,1,0:T(8,128)} %rhs.3) | copy-start | bytes 1572868
  1.0 0.8 copy-start.1
  1.9 0.8 copy-start.2
  2.7 0.8 copy-start.3
  3.6 1.8 %collective-permute-start = (f32[11,4,16,128]{3,2,1,0:T(8,128)S(1)}, f32[11,4,16,128]{3,2,1,0:T(8,128)S(1)}, u32[]{:S(2)}, u32[]{:S(2)}) collective-permute-start(f32[11,4,16,128]{3,2,1,0:T(8,128)S(1)} %shard_map.46), channel_id=1, source_target_pairs={{0,1},{1,0},{2,3},{3,2},{4,5},{5,4},{6,7},{7,6},{8,9},{9,8},{10,11... | collective-permute-start | bytes 1081352 | tf_op jit(solution)/shard_map/ppermute | solution.py:497
  27.7 2.3 %collective-permute-start.1 = (f32[4,2,11,16,128]{4,3,2,1,0:T(8,128)S(1)}, f32[4,2,11,16,128]{4,3,2,1,0:T(8,128)S(1)}, u32[]{:S(2)}, u32[]{:S(2)}) collective-permute-start(f32[4,2,11,16,128]{4,3,2,1,0:T(8,128)S(1)} %get-tuple-element.17), channel_id=1, source_target_pairs={{0,1},{1,0},{2,3},{3,2},{4,5},{5,4},{6,7},{7,6},{8,9},{9,8},{10,11... | collective-permute-start | bytes 2162696 | tf_op jit(solution)/shard_map/ppermute | solution.py:504
  27.8 2.2 %collective-permute-start.2 = (f32[4,2,11,16,128]{4,3,2,1,0:T(8,128)S(1)}, f32[4,2,11,16,128]{4,3,2,1,0:T(8,128)S(1)}, u32[]{:S(2)}, u32[]{:S(2)}) collective-permute-start(f32[4,2,11,16,128]{4,3,2,1,0:T(8,128)S(1)} %get-tuple-element.18), channel_id=1, source_target_pairs={{1,8},{8,1},{9,16},{16,9},{17,24},{24,17},{3,10},{10,3},{11,18},{1... | collective-permute-start | bytes 2162696 | tf_op jit(solution)/shard_map/ppermute | solution.py:503
  66.4 2.5 %collective-permute-start.3 = (f32[4,5,2,32,128]{4,3,2,1,0:T(8,128)S(1)}, f32[4,5,2,32,128]{4,3,2,1,0:T(8,128)S(1)}, u32[]{:S(2)}, u32[]{:S(2)}) collective-permute-start(f32[4,5,2,32,128]{4,3,2,1,0:T(8,128)S(1)} %all_to_all.16.mine), channel_id=1, source_target_pairs={{0,1},{1,0},{2,3},{3,2},{4,5},{5,4},{6,7},{7,6},{8,9},{9,8},{10,11... | collective-permute-start | bytes 1966088 | tf_op jit(solution)/shard_map/ppermute | solution.py:519
  66.4 2.5 %collective-permute-start.4 = (f32[2,2,64,256]{3,2,1,0:T(8,128)S(1)}, f32[2,2,64,256]{3,2,1,0:T(8,128)S(1)}, u32[]{:S(2)}, u32[]{:S(2)}) collective-permute-start(f32[2,2,64,256]{3,2,1,0:T(8,128)S(1)} %get-tuple-element.21), channel_id=1, source_target_pairs={{0,1},{1,0},{2,3},{3,2},{4,5},{5,4},{6,7},{7,6},{8,9},{9,8},{10,11... | collective-permute-start | bytes 786440 | tf_op jit(solution)/shard_map/ppermute | solution.py:517
  66.9 2.0 %collective-permute-start.5 = (f32[2,2,64,256]{3,2,1,0:T(8,128)S(1)}, f32[2,2,64,256]{3,2,1,0:T(8,128)S(1)}, u32[]{:S(2)}, u32[]{:S(2)}) collective-permute-start(f32[2,2,64,256]{3,2,1,0:T(8,128)S(1)} %get-tuple-element.22), channel_id=1, source_target_pairs={{1,8},{8,1},{9,16},{16,9},{17,24},{24,17},{3,10},{10,3},{11,18},{1... | collective-permute-start | bytes 786440 | tf_op jit(solution)/shard_map/ppermute | solution.py:516
  86.1 5.8 %collective-permute-start.6 = (f32[4,2,4,16,128]{4,3,2,1,0:T(8,128)S(1)}, f32[4,2,4,16,128]{4,3,2,1,0:T(8,128)S(1)}, u32[]{:S(2)}, u32[]{:S(2)}) collective-permute-start(f32[4,2,4,16,128]{4,3,2,1,0:T(8,128)S(1)} %slice_bitcast_fusion), channel_id=1, source_target_pairs={{0,1},{1,0},{2,3},{3,2},{4,5},{5,4},{6,7},{7,6},{8,9},{9,8},{10,11... | collective-permute-start | bytes 786440 | tf_op jit(solution)/shard_map/ppermute | solution.py:539

commit v2 on v1

--- a/solution.py
+++ b/solution.py
@@ -120,6 +120,8 @@
 
 HALO = 2
 MIB = 1 << 20
+COARSE_COST = 5 * 10**9
+LAY_COST = 5 * 10**9
 F32 = jnp.float32
 
 
@@ -131,13 +133,13 @@
     return jnp.where(total > 0.0, total, 1.0)
 
 
-def level_coefs(rho, sr, si, scale, bx, by, bz, wr, wi, dr, step):
-    n, ny, nz = sr.shape
+def level_coefs(rho, sr, si, scale, bx, by, bz, wr, wi, dr, step, start, count):
+    ny, nz = sr.shape[1:]
     two = 2.0 * scale
-    bx[pl.ds(0, 1)] = two / safe(rho[pl.ds(0, 1)] + rho[pl.ds(1, 1)])
+    bx[pl.ds(start, 1)] = two / safe(rho[pl.ds(start, 1)] + rho[pl.ds(start + 1, 1)])
 
     def body(i):
-        p = i * step
+        p = start + i * step
         r = rho[pl.ds(p + 1, step)]
         row = lax.broadcasted_iota(jnp.int32, r.shape, 1)
         lane = lax.broadcasted_iota(jnp.int32, r.shape, 2)
@@ -161,7 +163,7 @@
         wi[pl.ds(p, step)] = w * e
         dr[pl.ds(p, step)] = d
 
-    loop(n // step, body)
+    loop(count // step, body)
 
 
 def near(u, at, c, p, step, bx, by, bz):
@@ -207,100 +209,99 @@
     return jnp.dot(a, b, precision=lax.Precision.HIGHEST, preferred_element_type=F32)
 
 
-def send_kernel(rhs, rho, sr, si, out):
-    half = out.shape[1]
-    at = (1 - lax.axis_index("gz")) * half
+def send_kernel(rhs, rho, sr, si, away, kept, sems):
+    half = away.shape[1]
     m = rhs.shape[1]
-    for c in range(2):
+    k = lax.axis_index("gz")
+    copies = []
+    for n, (out, side) in enumerate(((away, 1 - k), (kept, k))):
+        planes = pl.ds(side * half, half)
+        pieces = [(rhs.at[c, :, planes], out.at[pl.ds(c * m, m)]) for c in range(2)]
+        pieces += [(ref.at[planes], out.at[2 * m + j]) for j, ref in enumerate((rho, sr, si))]
+        copies += [pltpu.make_async_copy(src, dst, sems.at[5 * n + j]) for j, (src, dst) in enumerate(pieces)]
+    for copy in copies:
+        copy.start()
+    for copy in copies:
+        copy.wait()
+
+
+def spread_kernel(kept, came, close, far):
+    k = lax.axis_index("gz")
+    m = close.shape[0]
+    half = kept.shape[1]
+    rest = half - HALO
+    for t, ref in enumerate((kept, came)):
         for r in range(m):
-            out[2 * r + c] = rhs[c, r, pl.ds(at, half)]
-    for j, ref in enumerate((rho, sr, si)):
-        out[2 * m + j] = ref[pl.ds(at, half)]
-
-
-def spread_kernel(rhs, rho, sr, si, came, out):
-    half = came.shape[1]
-    at = lax.axis_index("gz") * half
-    m = rhs.shape[1]
-    for r in range(m):
-        for c in range(2):
-            out[r, 0, c] = rhs[c, r, pl.ds(at, half)]
-            out[r, 1, c] = came[2 * r + c]
-        for j, ref in enumerate((rho, sr, si)):
-            out[r, 0, 2 + j] = ref[pl.ds(at, half)]
-            out[r, 1, 2 + j] = came[2 * m + j]
-
-
-def edge_kernel(blocks, over_gz, over_gx):
-    k = lax.axis_index("gz")
-    half = blocks.shape[3]
-    for out, high in ((over_gz, 1 - k), (over_gx, k)):
-        two, three = high * (half - HALO), high * (half - HALO - 1)
-        for s in range(blocks.shape[0]):
-            for t in range(2):
-                for j, f in enumerate((0, 1, 3, 4)):
-                    out[s, t, pl.ds(HALO * j, HALO)] = blocks[s, t, f, pl.ds(two, HALO)]
-                out[s, t, pl.ds(4 * HALO, HALO + 1)] = blocks[s, t, 2, pl.ds(three, HALO + 1)]
-
-
-def fine_kernel(blocks, from_gz, from_gx, own, up_gz, up_gx, packed, g, bx, by, bz, wr, wi, rho, sr, si, dr, ua, ub, sums, narrow):
-    k = lax.axis_index("gz")
-    nsrc, _, _, half, rows, lanes = blocks.shape
-    ny, nz = g.shape[2:]
-
-    def place(ref, first, count, s, z, value):
-        ref[pl.ds(first, count), s * rows : (s + 1) * rows, pl.ds(pl.multiple_of(z * lanes, lanes), lanes)] = value
-
-    for s in range(nsrc):
+            for j, f in enumerate((r, m + r, 2 * m + 1, 2 * m + 2)):
+                close[r, t, HALO * j : HALO * (j + 1)] = ref[f, pl.ds(k * rest, HALO)]
+                far[r, t, rest * j : rest * (j + 1)] = ref[f, pl.ds((1 - k) * HALO, rest)]
+            close[r, t, 4 * HALO : 5 * HALO + 1] = ref[2 * m, pl.ds(k * (rest - 1), HALO + 1)]
+            far[r, t, 4 * rest : 5 * rest - 1] = ref[2 * m, pl.ds((1 - k) * (HALO + 1), rest - 1)]
+
+
+def edge_kernel(close, far, out):
+    k = lax.axis_index("gz")
+    for s in range(close.shape[0]):
         for t in range(2):
-            z = k if t == 0 else 1 - k
-            for f, ref in ((0, g.at[0]), (1, g.at[1]), (3, sr), (4, si)):
-                place(ref, HALO, half, s, z, blocks[s, t, f])
-            place(rho, HALO + 1, half, s, z, blocks[s, t, 2])
-
-    def halo(came, low):
-        for s in range(nsrc):
-            for t in range(2):
-                z = 1 - k if t == 0 else k
-                first = 0 if low else half + HALO
-                for j, ref in enumerate((g.at[0], g.at[1], sr, si)):
-                    place(ref, first, HALO, s, z, came[s, t, HALO * j : HALO * (j + 1)])
-                place(rho, 0 if low else half + HALO + 1, HALO + 1, s, z, came[s, t, 4 * HALO : 5 * HALO + 1])
-
-    @pl.when(k == 0)
-    def _():
-        halo(from_gx, True)
-        halo(from_gz, False)
-
-    @pl.when(k == 1)
-    def _():
-        halo(from_gz, True)
-        halo(from_gx, False)
-
-    level_coefs(rho, sr, si, 1.0, bx, by, bz, wr, wi, dr, 1)
+            out[s, t, 0 : 4 * HALO] = far[s, t, 0 : 4 * HALO]
+            out[s, t, pl.ds(4 * HALO + k, HALO)] = close[s, t, pl.ds(5 * HALO - 1 - k, HALO)]
+            out[s, t, 5 * HALO - k * HALO] = far[s, t, 4 * HALO]
+
+
+def put_planes(came, other, arrays, rho, first, first_rho):
+    k = lax.axis_index("gz")
+    rows, lanes = came.shape[3:]
+    count = came.shape[2] // 4
+    for s in range(came.shape[0]):
+        for t in range(2):
+            z = jnp.where(k == t, 1, 0) if other else jnp.where(k == t, 0, 1)
+            spot = (slice(s * rows, (s + 1) * rows), pl.ds(pl.multiple_of(z * lanes, lanes), lanes))
+            for j, ref in enumerate(arrays):
+                ref[(pl.ds(first, count), *spot)] = came[s, t, count * j : count * (j + 1)]
+            rho[(pl.ds(first_rho, came.shape[2] - 4 * count), *spot)] = came[s, t, 4 * count :]
+
+
+def lay_kernel(close, far, from_gx, g, rho, sr, si, bx, by, bz, wr, wi, dr):
+    k = lax.axis_index("gz")
+    pad = g.shape[1]
+    half = pad - 2 * HALO
+    rest = half - HALO
+    arrays = (g.at[0], g.at[1], sr, si)
+    put_planes(close, False, arrays, rho, HALO + k * rest, HALO + 1 + k * (rest - 1))
+    put_planes(far, False, arrays, rho, HALO + (1 - k) * HALO, HALO + 1 + (1 - k) * (HALO + 1))
+    put_planes(from_gx, True, arrays, rho, k * (half + HALO), k * (half + HALO + 1))
+    level_coefs(rho, sr, si, 1.0, bx, by, bz, wr, wi, dr, 1, k * (HALO + 1), pad - HALO - 1)
+
+
+def fine_kernel(from_gz, *refs):
+    g, rho, sr, si, bx, by, bz, wr, wi, dr, own, up_gz, up_gx, packed, ua, sums, narrow = refs[10:]
+    k = lax.axis_index("gz")
+    pad, ny, nz = g.shape[1:]
+    half = pad - 2 * HALO
+    put_planes(from_gz, True, (g.at[0], g.at[1], sr, si), rho, (1 - k) * (half + HALO), (1 - k) * (half + HALO + 1))
+    level_coefs(rho, sr, si, 1.0, bx, by, bz, wr, wi, dr, 1, (1 - k) * (pad - HALO - 1), HALO + 1)
     coefs = (bx, by, bz, wr, wi)
 
     def first(p):
         ua[0, pl.ds(p, 1)], ua[1, pl.ds(p, 1)] = weigh(g[0, pl.ds(p, 1)], g[1, pl.ds(p, 1)], p, 1, wr, wi)
 
-    loop(half + 2 * HALO, first)
+    loop(pad, first)
 
     def second(i):
         p = i + 1
-        ub[0, pl.ds(p, 1)], ub[1, pl.ds(p, 1)] = sweep_planes(ua, p, g, p, p, 1, coefs)
-
-    loop(half + 2 * HALO - 2, second)
+        own[0, pl.ds(i, 1)], own[1, pl.ds(i, 1)] = sweep_planes(ua, p, g, p, p, 1, coefs)
+
+    loop(pad - 2, second)
     for c in range(2):
-        own[c] = ub[c, pl.ds(HALO, half)]
-        up_gz[c] = ub[c, pl.ds(HALO + (1 - k) * (half - HALO), HALO)]
-        up_gx[c] = ub[c, pl.ds(HALO + k * (half - HALO), HALO)]
+        up_gz[c] = own[c, 2 + (1 - k) * (half - 3)]
+        up_gx[c] = own[c, 2 + k * (half - 3)]
 
     pairs = half // 2
 
     def down(q):
         p = HALO + 2 * q
-        ar, ai = resid_planes(ub, p, g, p, p, 1, coefs, dr, si)
-        br, bi = resid_planes(ub, p + 1, g, p + 1, p + 1, 1, coefs, dr, si)
+        ar, ai = resid_planes(own, p - 1, g, p, p, 1, coefs, dr, si)
+        br, bi = resid_planes(own, p, g, p + 1, p + 1, 1, coefs, dr, si)
         totals = (ar + br, ai + bi, rho[pl.ds(p + 1, 1)] + rho[pl.ds(p + 2, 1)], sr[pl.ds(p, 1)] + sr[pl.ds(p + 1, 1)], si[pl.ds(p, 1)] + si[pl.ds(p + 1, 1)])
         for j, v in enumerate(totals):
             sums[pl.ds(pl.multiple_of((j * pairs + q) * ny, ny), ny), :] = v[0]
@@ -314,10 +315,10 @@
 
 
 def coarse_kernel(
-    mine, other, own, from_gz, from_gx, g0, bx0, by0, bz0, wr0, wi0, out,
+    mine, other, out,
     rho1, sr1, si1, g1, bx1, by1, bz1, wr1, wi1, dr1, ua1, ub1,
     rho2, sr2, si2, g2, bx2, by2, bz2, wr2, wi2, dr2, ua2, ub2,
-    sums, narrow, wide, tall, ua0, ub0,
+    sums, narrow, wide, tall,
 ):
     k = lax.axis_index("gz")
     chip = lax.axis_index("gx")
@@ -339,7 +340,7 @@
             sr1[pl.ds(at, pairs)] = ref[s, 3]
             si1[pl.ds(at, pairs)] = ref[s, 4]
     step1 = 4
-    level_coefs(rho1, sr1, si1, 0.25, bx1, by1, bz1, wr1, wi1, dr1, step1)
+    level_coefs(rho1, sr1, si1, 0.25, bx1, by1, bz1, wr1, wi1, dr1, step1, 0, n1)
     coefs1 = (bx1, by1, bz1, wr1, wi1)
 
     def first(i):
@@ -381,7 +382,7 @@
     for j, ref in enumerate((g2.at[0], g2.at[1], rho2.at[pl.ds(1, n2)], sr2, si2)):
         at = 2 * n * j
         ref[...] = (narrow[pl.ds(at, n, 2), :] + narrow[pl.ds(at + 1, n, 2), :]).reshape(n2, ny2, nz)
-    level_coefs(rho2, sr2, si2, 0.0625, bx2, by2, bz2, wr2, wi2, dr2, n2)
+    level_coefs(rho2, sr2, si2, 0.0625, bx2, by2, bz2, wr2, wi2, dr2, n2, 0, n2)
     coefs2 = (bx2, by2, bz2, wr2, wi2)
     ua2[0, pl.ds(1, n2)], ua2[1, pl.ds(1, n2)] = weigh(g2[0], g2[1], 0, n2, wr2, wi2)
     src, dst = ua2, ub2
@@ -406,31 +407,25 @@
     sweep1(ub1, ua1)
     sweep1(ua1, ub1)
 
-    half = own.shape[1]
-    pad = half + 2 * HALO
-    quads = pad // 2
-    base = (2 * chip + k) * pairs
-    fine_z = own.shape[3]
-    fine_y = own.shape[2]
+    quads = out.shape[1]
+    out[...] = ub1[:, pl.ds((2 * chip + k) * pairs, quads)]
+
+
+def last_kernel(u1, own, from_gz, from_gx, g0, bx0, by0, bz0, wr0, wi0, out, ua0, ub0, tall):
+    k = lax.axis_index("gz")
+    quads, ny, nz = u1.shape[1:]
+    pad, fine_y, fine_z = ua0.shape[1:]
+    half = pad - 2 * HALO
     rows = quads * ny
-
-    @pl.when(k == 0)
-    def _():
-        ua0[:, pl.ds(0, HALO)] = from_gx[...]
-        ua0[:, pl.ds(HALO + half, HALO)] = from_gz[...]
-
-    @pl.when(k == 1)
-    def _():
-        ua0[:, pl.ds(0, HALO)] = from_gz[...]
-        ua0[:, pl.ds(HALO + half, HALO)] = from_gx[...]
-
-    ua0[:, pl.ds(HALO, half)] = own[...]
+    ua0[:, pl.ds(1, pad - 2)] = own[...]
+    ua0[:, k * (pad - 1)] = from_gx[...]
+    ua0[:, (1 - k) * (pad - 1)] = from_gz[...]
     for h in range(fine_z // nz):
         col = lax.broadcasted_iota(jnp.int32, (nz, nz), 1) + h * nz
         row = lax.broadcasted_iota(jnp.int32, (nz, nz), 0)
         widen = jnp.where(row == col // 2, 1.0, 0.0).astype(F32)
         for c in range(2):
-            v = dot(ub1[c, pl.ds(base, quads)].reshape(rows, nz), widen)
+            v = dot(u1[c].reshape(rows, nz), widen)
             tall[pl.ds(0, rows, 2), :] = v
             tall[pl.ds(1, rows, 2), :] = v
             for q in range(quads):
@@ -453,32 +448,31 @@
         for c, v in enumerate((r, m)):
             for d in range(dests):
                 for z in range(2):
-                    slot = jnp.where(k == z, 0, 1)
-                    out[d, slot, c, i] = v[0, d * drows : (d + 1) * drows, z * lanes : (z + 1) * lanes]
+                    out[d, z, c, i] = v[0, d * drows : (d + 1) * drows, z * lanes : (z + 1) * lanes]
 
     loop(half, fourth)
 
 
-def gather_kernel(kept, came, out):
-    half = kept.shape[3]
-    k = lax.axis_index("gz")
-    for r in range(kept.shape[0]):
-        for c in range(2):
-            out[c, r, pl.ds(k * half, half)] = kept[r, 0, c]
-            out[c, r, pl.ds((1 - k) * half, half)] = came[r, c]
-
-
-def call(kernel, outs, args, scratch=(), limit=24):
-    vm = pl.BlockSpec(memory_space=pltpu.VMEM)
+def gather_kernel(came, out):
+    half = came.shape[3]
+    for r in range(came.shape[0]):
+        for z in range(2):
+            for c in range(2):
+                out[c, r, z * half : (z + 1) * half] = came[r, z, c]
+
+
+def call(kernel, outs, args, scratch=(), limit=24, space=pltpu.VMEM, sems=None, cost=None, aliases=None):
     single = not isinstance(outs, list)
     shapes = [outs] if single else outs
     result = pl.pallas_call(
         kernel,
         out_shape=[jax.ShapeDtypeStruct(s, F32) for s in shapes],
-        in_specs=[vm] * len(args),
-        out_specs=[vm] * len(shapes),
-        scratch_shapes=[pltpu.VMEM(s, F32) for s in scratch],
+        in_specs=[pl.BlockSpec(memory_space=space)] * len(args),
+        out_specs=[pl.BlockSpec(memory_space=pltpu.VMEM)] * len(shapes),
+        scratch_shapes=[pltpu.VMEM(s, F32) for s in scratch] + ([pltpu.SemaphoreType.DMA((sems,))] if sems else []),
         compiler_params=pltpu.CompilerParams(vmem_limit_bytes=limit * MIB),
+        input_output_aliases=aliases or {},
+        cost_estimate=cost and pl.CostEstimate(flops=cost, bytes_accessed=0, transcendentals=0),
     )(*args)
     return result[0] if single else result
 
@@ -493,25 +487,28 @@
     ends = [p for c in range(chips - 1) for p in ((2 * c + 1, 2 * c + 2), (2 * c + 2, 2 * c + 1))]
     fields = (rhs, density, shift_real, shift_imag)
 
-    away = call(send_kernel, (2 * m + 3, half, rows, lanes), fields)
+    own_half = (2 * m + 3, half, rows, lanes)
+    away, kept = call(send_kernel, [own_half, own_half], tuple(pltpu.with_memory_space_constraint(f, pltpu.HBM) for f in fields), space=pltpu.HBM, sems=10)
     came = lax.ppermute(away, "gz", swap)
-    spread = call(spread_kernel, (m, 2, 5, half, rows, lanes), fields + (came,))
-    blocks = lax.all_to_all(spread, "gy", 0, 0, tiled=True)
-
     edges = (m, 2, 5 * HALO + 1, rows, lanes)
-    to_gz, to_gx = call(edge_kernel, [edges, edges], (blocks,))
-    from_gx = lax.ppermute(to_gx, ("gx", "gz"), ends)
+    close, far = call(spread_kernel, [edges, (m, 2, 5 * (half - HALO) - 1, rows, lanes)], (kept, came))
+    close = lax.all_to_all(close, "gy", 0, 0, tiled=True)
+    from_gx = lax.ppermute(close, ("gx", "gz"), ends)
+    far = lax.all_to_all(far, "gy", 0, 0, tiled=True)
+    to_gz = call(edge_kernel, edges, (close, far))
     from_gz = lax.ppermute(to_gz, "gz", swap)
 
     pairs = half // 2
     plane = (ny, nz)
-    own, up_gz, up_gx, packed, g, bx, by, bz, wr, wi = call(
+    laid = [(2, pad) + plane, (pad + 2,) + plane, (pad,) + plane, (pad,) + plane, (pad + 1,) + plane] + [(pad,) + plane] * 5
+    state = call(lay_kernel, laid, (close, far, from_gx), limit=24, cost=LAY_COST)
+    g, _, _, _, bx, by, bz, wr, wi, _, own, up_gz, up_gx, packed = call(
         fine_kernel,
-        [(2, half) + plane, (2, HALO) + plane, (2, HALO) + plane, (chips, 5, pairs, ny // 2, nz // 2), (2, pad) + plane, (pad + 1,) + plane]
-        + [(pad,) + plane] * 4,
-        (blocks, from_gz, from_gx),
-        scratch=[(pad + 2,) + plane] + [(pad,) + plane] * 3 + [(2, pad) + plane] * 2 + [(5 * pairs * ny, nz), (5 * pairs * ny, nz // 2)],
-        limit=40,
+        laid + [(2, pad - 2) + plane, (2,) + plane, (2,) + plane, (chips, 5, pairs, ny // 2, nz // 2)],
+        (from_gz, *state),
+        scratch=[(2, pad) + plane] + [(5 * pairs * ny, nz), (5 * pairs * ny, nz // 2)],
+        limit=24,
+        aliases={i + 1: i for i in range(len(laid))},
     )
     u_gx = lax.ppermute(up_gx, ("gx", "gz"), ends)
     u_gz = lax.ppermute(up_gz, "gz", swap)
@@ -524,20 +521,23 @@
     def level(n, p):
         return [(n + 2,) + p, (n,) + p, (n,) + p, (2, n) + p, (n + 1,) + p] + [(n,) + p] * 5 + [(2, n + 2) + p] * 2
 
-    tall = max(2 * n2 * p1[0], pad * ny // 2 * 2)
+    u1 = call(
+        coarse_kernel,
+        (2, pad // 2) + p1,
+        (mine, other),
+        scratch=level(n1, p1) + level(n2, p2) + [(5 * n2 * p1[0], p1[1])] * 2 + [(2 * n2 * p2[0], p1[1]), (2 * n2 * p1[0], p1[1])],
+        limit=32,
+        cost=COARSE_COST,
+    )
     result = call(
-        coarse_kernel,
+        last_kernel,
         (m, 2, 2, half, rows, lanes),
-        (mine, other, own, u_gz, u_gx, g, bx, by, bz, wr, wi),
-        scratch=level(n1, p1)
-        + level(n2, p2)
-        + [(5 * n2 * p1[0], p1[1])] * 2
-        + [(2 * n2 * p2[0], p1[1]), (tall, p1[1]), (2, pad) + plane, (2, pad) + plane],
-        limit=40,
+        (u1, own, u_gz, u_gx, g, bx, by, bz, wr, wi),
+        scratch=[(2, pad) + plane, (2, pad) + plane, (pad * ny // 2, p1[1])],
+        limit=32,
     )
-    back = lax.all_to_all(result, "gy", 0, 0, tiled=True)
-    last = lax.ppermute(back[:, 1], "gz", swap)
-    return call(gather_kernel, rhs.shape, (back, last))
+    back = lax.all_to_all(result.reshape((2 * m,) + result.shape[2:]), ("gy", "gz"), 0, 0, tiled=True)
+    return call(gather_kernel, rhs.shape, (back.reshape(result.shape),))
 
 
 def solution(mesh):
@@ -545,7 +545,7 @@
 
     def local(rhs, density, shift_real, shift_imag):
         _, m, xs, rows, lanes = rhs.shape
-        planes = sizes["gz"] == 2 and sizes["gy"] == m and xs % 8 == 0 and rows % 16 == 0 and lanes == 128
+        planes = sizes["gz"] == 2 and sizes["gy"] == m and xs == 8 and rows % 16 == 0 and lanes == 128
         return (local_planes if planes else local_general)(rhs, density, shift_real, shift_imag)
 
     placed = (

time: 94.1 us -> 83.3 us (0.89); the launches traced: 92.7 us -> 83 us
  local copies, waits for them, and re-layouts: 3.58 us -> 0 us
  starting transfers between devices: 7.1 us -> 4.33 us
  waiting for transfers between devices: 5.22 us -> 2.9 us
  blocking collectives: 63.7 us -> 62 us
    all_to_all x1, blocking collectives: 32 us -> 22.7 us  [local_planes(): mine = lax.all_to_all(packed, 'gx', 0, 0, tiled=True)]
    all_to_all x2 -> x3, blocking collectives: 31.7 us -> 39.3 us  [the longest x1 16 us: local_planes(): close = lax.all_to_all(close, 'gy', 0, 0, tiled=True)]
    ppermute x2 -> x1, starting transfers between devices: 5.34 us -> 0.7 us  [local_planes(): from_gx = lax.ppermute(close, ('gx', 'gz'), ends)]
    unnamed x8 -> x0, local copies, waits for them, and re-layouts: 3.56 us -> none
    ppermute x1, starting transfers between devices: 0.07 us -> 1.95 us  [local_planes(): from_gz = lax.ppermute(to_gz, 'gz', swap)]
    ppermute x1, waiting for transfers between devices: 1.29 us -> 0.01 us  [local_planes(): u_gz = lax.ppermute(up_gz, 'gz', swap)]
    ppermute x2 -> x1, waiting for transfers between devices: 1.16 us -> 0.01 us  [local_planes(): from_gx = lax.ppermute(close, ('gx', 'gz'), ends)]
    pallas_call x6 -> x8, Pallas kernels: 13 us -> 13.7 us  [call(): pl.pallas_call(kernel, out_shape=[jax.ShapeDtypeStruct(s, F32) for s in s...]
  transfers between devices with their start and end apart: 7 -> 6, of which waited for: 4 -> 3; matrix products, arithmetic and copies ran while one was open for 0% -> 0% of each run, Pallas kernels for 0% -> 8%
where the time goes in v2:
time: 83.3 us; the launch traced here: 83 us
  blocking collectives  62 us (74%)
  Pallas kernels  13.7 us (16%)
  starting transfers between devices  4.33 us (5%)
  waiting for transfers between devices  2.9 us (3%)
    all_to_all x1, blocking collectives, local_planes(): mine = lax.all_to_all(packed, 'gx', 0, 0, tiled=True)  22.7 us
    all_to_all x1, blocking collectives, local_planes(): close = lax.all_to_all(close, 'gy', 0, 0, tiled=True)  16 us
    pallas_call x8, Pallas kernels, call(): pl.pallas_call(kernel, out_shape=[jax.ShapeDtypeStruct(s, F32) for s in s...  13.7 us
    all_to_all x1, blocking collectives, local_planes(): lax.all_to_all(result.reshape((2 * m,) + result.shape[2:]), ('gy', 'gz'),...  12.2 us
    all_to_all x1, blocking collectives, local_planes(): far = lax.all_to_all(far, 'gy', 0, 0, tiled=True)  11.1 us
    ppermute x1, starting transfers between devices, local_planes(): from_gz = lax.ppermute(to_gz, 'gz', swap)  1.95 us
  transfers between devices with their start and end apart: 6, of which 3 were waited for; matrix products, arithmetic and copies ran while one was open for 0% of the time, Pallas kernels for 8%

profile of v2, /device:TPU:0, one launch (start us, length us, event | category | flops | bytes accessed | tf_op | source)
XLA Modules:
  0.0 83.0 jit_solution(2884159613459799137)
XLA Ops:
  0.0 1.2 %shard_map.46 = (f32[11,4,16,128]{3,2,1,0:T(8,128)S(1)}, f32[11,4,16,128]{3,2,1,0:T(8,128)S(1)}) custom-call(f32[2,4,8,16,128]{4,3,2,1,0:T(8,128)} %rhs.1, f32[8,16,128]{2,1,0:T(8,128)} %rho.1, f32[8,16,128]{2,1,0:T(8,128)} %sr.1, f32[8,16,128]{2,1,0:T(8,128)} %si.1), custom_call_target="tpu_custom_call" | custom-call | tf_op jit(solution)/shard_map/pallas_call | solution.py:467
  1.2 0.5 collective-permute-start
  1.8 1.3 %collective-permute-done.came = f32[11,4,16,128]{3,2,1,0:T(8,128)S(1)} collective-permute-done((f32[11,4,16,128]{3,2,1,0:T(8,128)S(1)}, f32[11,4,16,128]{3,2,1,0:T(8,128)S(1)}, u32[]{:S(2)}, u32[]{:S(2)}) %collective-permute-start) | collective-permute-done | bytes 360480 | tf_op jit(solution)/shard_map/ppermute | solution.py:492
  3.1 0.1 shard_map.47
  3.2 16.0 %all_to_all.20.close = f32[4,2,11,16,128]{4,3,2,1,0:T(8,128)S(1)} all-to-all(f32[4,2,11,16,128]{4,3,2,1,0:T(8,128)S(1)} %get-tuple-element.31), channel_id=1, replica_groups=mesh['gx'=4,'gy'=4,'gz'=2] {'gy'}, dimensions={0} | all-to-all | bytes 1441792 | tf_op jit(solution)/shard_map/all_to_all | solution.py:495
  19.1 0.7 collective-permute-start.2
  19.8 11.1 %all_to_all.21.far = f32[4,2,9,16,128]{4,3,2,1,0:T(8,128)S(1)} all-to-all(f32[4,2,9,16,128]{4,3,2,1,0:T(8,128)S(1)} %get-tuple-element.32), channel_id=1, replica_groups=mesh['gx'=4,'gy'=4,'gz'=2] {'gy'}, dimensions={0} | all-to-all | bytes 1179648 | tf_op jit(solution)/shard_map/all_to_all | solution.py:497
  31.0 0.1 shard_map.48
  31.0 1.9 %collective-permute-start.1 = (f32[4,2,11,16,128]{4,3,2,1,0:T(8,128)S(1)}, f32[4,2,11,16,128]{4,3,2,1,0:T(8,128)S(1)}, u32[]{:S(2)}, u32[]{:S(2)}) collective-permute-start(f32[4,2,11,16,128]{4,3,2,1,0:T(8,128)S(1)} %shard_map.48), channel_id=1, source_target_pairs={{0,1},{1,0},{2,3},{3,2},{4,5},{5,4},{6,7},{7,6},{8,9},{9,8},{10,11... | collective-permute-start | bytes 2162696 | tf_op jit(solution)/shard_map/ppermute | solution.py:499
  33.0 0.0 collective-permute-done.2.from_gx
  33.0 1.1 %shard_map.49 = (f32[2,8,64,256]{3,2,1,0:T(8,128)S(1)}, f32[10,64,256]{2,1,0:T(8,128)S(1)}, f32[8,64,256]{2,1,0:T(8,128)S(1)}, f32[8,64,256]{2,1,0:T(8,128)S(1)}...) custom-call(f32[4,2,11,16,128]{4,3,2,1,0:T(8,128)S(1)} %all_to_all.2, ...), custom_call_target="tpu_custom_call" | custom-call | flops 5000000000 | tf_op jit(solution)/shard_map/pallas_call | solution.py:467
  34.1 0.7 collective-permute-done.1.from_gz
  34.8 3.1 %shard_map.50 = (f32[2,8,64,256]{3,2,1,0:T(8,128)S(1)}, f32[10,64,256]{2,1,0:T(8,128)S(1)}, f32[8,64,256]{2,1,0:T(8,128)S(1)}, f32[8,64,256]{2,1,0:T(8,128)S(1)}...) custom-call(f32[4,2,11,16,128]{4,3,2,1,0:T(8,128)S(1)} %collective-p, ...), custom_call_target="tpu_custom_call", output_to_operand_aliasing={{0}: (1, {}), {1}: (2, {}), {2}: (3, {}), {3}: (4, {}), {4}... | custom-call | tf_op jit(solution)/shard_map/pallas_call | solution.py:467
  37.9 22.7 %all_to_all.22.mine = f32[4,5,2,32,128]{4,3,2,1,0:T(8,128)S(1)} all-to-all(f32[4,5,2,32,128]{4,3,2,1,0:T(8,128)S(1)} %get-tuple-element.43), channel_id=1, replica_groups=mesh['gx'=4,'gy'=4,'gz'=2] {'gx'}, dimensions={0} | all-to-all | bytes 1310720 | tf_op jit(solution)/shard_map/all_to_all | solution.py:515
  60.6 0.0 collective-permute-start.3
  60.7 0.5 collective-permute-start.4
  61.2 0.7 collective-permute-start.5
  61.8 0.9 %collective-permute-done.3.other = f32[4,5,2,32,128]{4,3,2,1,0:T(8,128)S(1)} collective-permute-done((f32[4,5,2,32,128]{4,3,2,1,0:T(8,128)S(1)}, f32[4,5,2,32,128]{4,3,2,1,0:T(8,128)S(1)}, u32[]{:S(2)}, u32[]{:S(2)}) %collective-permute-start.3) | collective-permute-done | bytes 655392 | tf_op jit(solution)/shard_map/ppermute | solution.py:516
  62.7 5.2 %shard_map.51.u1 = f32[2,4,32,128]{3,2,1,0:T(8,128)S(1)} custom-call(f32[4,5,2,32,128]{4,3,2,1,0:T(8,128)S(1)} %all_to_all.22.mine, f32[4,5,2,32,128]{4,3,2,1,0:T(8,128)S(1)} %collective-permute-done.3.other), custom_call_target="tpu_custom_call" | custom-call | flops 5000000000 | tf_op jit(solution)/shard_map/pallas_call | solution.py:467
  68.0 0.0 collective-permute-done.4.from_gz
  68.0 0.0 collective-permute-done.5.from_gx
  68.0 2.1 %shard_map.52 = f32[4,2,2,4,16,128]{5,4,3,2,1,0:T(8,128)S(1)} custom-call(f32[2,4,32,128]{3,2,1,0:T(8,128)S(1)} %shard_map.51.u1, f32[2,6,64,256]{3,2,1,0:T(8,128)S(1)} %get-tuple-element.44.own, f32[2,64,256]{2,1,0:T(8,128)S(1)} %collective-permute-done.4.from_gz, f32[2,64,256]{2,1,0:T(8,128)S(1)} %collective-permute-done.5.from_gx, ...), custom_call_target="tpu_custom_call" | custom-call | tf_op jit(solution)/shard_map/pallas_call | solution.py:467
  70.1 12.2 %all_to_all.23 = f32[8,2,4,16,128]{4,3,2,1,0:T(8,128)S(1)} all-to-all(f32[8,2,4,16,128]{4,3,2,1,0:T(8,128)S(1)} %bitcast.3), channel_id=1, replica_groups=mesh['gx'=4,'gy'=4,'gz'=2] {'gy','gz'}, dimensions={0} | all-to-all | bytes 1048576 | tf_op jit(solution)/shard_map/all_to_all | solution.py:539
  82.2 0.8 shard_map.53
Async XLA Ops:
  1.2 1.8 %collective-permute-start = (f32[11,4,16,128]{3,2,1,0:T(8,128)S(1)}, f32[11,4,16,128]{3,2,1,0:T(8,128)S(1)}, u32[]{:S(2)}, u32[]{:S(2)}) collective-permute-start(f32[11,4,16,128]{3,2,1,0:T(8,128)S(1)} %get-tuple-element.30), channel_id=1, source_target_pairs={{0,1},{1,0},{2,3},{3,2},{4,5},{5,4},{6,7},{7,6},{8,9},{9,8},{10,11... | collective-permute-start | bytes 1081352 | tf_op jit(solution)/shard_map/ppermute | solution.py:492
  19.1 13.8 %collective-permute-start.2 = (f32[4,2,11,16,128]{4,3,2,1,0:T(8,128)S(1)}, f32[4,2,11,16,128]{4,3,2,1,0:T(8,128)S(1)}, u32[]{:S(2)}, u32[]{:S(2)}) collective-permute-start(f32[4,2,11,16,128]{4,3,2,1,0:T(8,128)S(1)} %all_to_all.20.close), channel_id=1, source_target_pairs={{1,8},{8,1},{9,16},{16,9},{17,24},{24,17},{3,10},{10,3},{11,18},{1... | collective-permute-start | bytes 2162696 | tf_op jit(solution)/shard_map/ppermute | solution.py:496
  31.0 3.8 %collective-permute-start.1 = (f32[4,2,11,16,128]{4,3,2,1,0:T(8,128)S(1)}, f32[4,2,11,16,128]{4,3,2,1,0:T(8,128)S(1)}, u32[]{:S(2)}, u32[]{:S(2)}) collective-permute-start(f32[4,2,11,16,128]{4,3,2,1,0:T(8,128)S(1)} %shard_map.48), channel_id=1, source_target_pairs={{0,1},{1,0},{2,3},{3,2},{4,5},{5,4},{6,7},{7,6},{8,9},{9,8},{10,11... | collective-permute-start | bytes 2162696 | tf_op jit(solution)/shard_map/ppermute | solution.py:499
  60.6 2.1 %collective-permute-start.3 = (f32[4,5,2,32,128]{4,3,2,1,0:T(8,128)S(1)}, f32[4,5,2,32,128]{4,3,2,1,0:T(8,128)S(1)}, u32[]{:S(2)}, u32[]{:S(2)}) collective-permute-start(f32[4,5,2,32,128]{4,3,2,1,0:T(8,128)S(1)} %all_to_all.22.mine), channel_id=1, source_target_pairs={{0,1},{1,0},{2,3},{3,2},{4,5},{5,4},{6,7},{7,6},{8,9},{9,8},{10,11... | collective-permute-start | bytes 1966088 | tf_op jit(solution)/shard_map/ppermute | solution.py:516
  60.7 7.3 %collective-permute-start.4 = (f32[2,64,256]{2,1,0:T(8,128)S(1)}, f32[2,64,256]{2,1,0:T(8,128)S(1)}, u32[]{:S(2)}, u32[]{:S(2)}) collective-permute-start(f32[2,64,256]{2,1,0:T(8,128)S(1)} %get-tuple-element.45), channel_id=1, source_target_pairs={{0,1},{1,0},{2,3},{3,2},{4,5},{5,4},{6,7},{7,6},{8,9},{9,8},{10,11... | collective-permute-start | bytes 393224 | tf_op jit(solution)/shard_map/ppermute | solution.py:514
  61.2 6.8 %collective-permute-start.5 = (f32[2,64,256]{2,1,0:T(8,128)S(1)}, f32[2,64,256]{2,1,0:T(8,128)S(1)}, u32[]{:S(2)}, u32[]{:S(2)}) collective-permute-start(f32[2,64,256]{2,1,0:T(8,128)S(1)} %get-tuple-element.46), channel_id=1, source_target_pairs={{1,8},{8,1},{9,16},{16,9},{17,24},{24,17},{3,10},{10,3},{11,18},{1... | collective-permute-start | bytes 393224 | tf_op jit(solution)/shard_map/ppermute | solution.py:513

commit v3 on v2

--- a/solution.py
+++ b/solution.py
@@ -119,9 +119,9 @@
 
 
 HALO = 2
+SIDE = 4
 MIB = 1 << 20
 COARSE_COST = 5 * 10**9
-LAY_COST = 5 * 10**9
 F32 = jnp.float32
 
 
@@ -166,11 +166,11 @@
     loop(count // step, body)
 
 
-def near(u, at, c, p, step, bx, by, bz):
-    mid = u[c, pl.ds(at, step)]
+def near(u, f, at, p, step, bx, by, bz):
+    mid = u[f, pl.ds(at, step)]
     ny, nz = mid.shape[1:]
     b = by[pl.ds(p, step)]
-    total = bx[pl.ds(p, step)] * u[c, pl.ds(at - 1, step)] + bx[pl.ds(p + 1, step)] * u[c, pl.ds(at + 1, step)]
+    total = bx[pl.ds(p, step)] * u[f, pl.ds(at - 1, step)] + bx[pl.ds(p + 1, step)] * u[f, pl.ds(at + 1, step)]
     total = total + (b * pltpu.roll(mid, ny - 1, 1) + pltpu.roll(b * mid, 1, 1))
     b = bz[pl.ds(p, step)]
     return mid, total + (b * pltpu.roll(mid, nz - 1, 2) + pltpu.roll(b * mid, 1, 2))
@@ -181,21 +181,23 @@
     return a * tr - b * ti, a * ti + b * tr
 
 
-def sweep_planes(u, at, g, gat, p, step, coefs):
+def sweep_planes(u, fields, at, g, gat, p, step, coefs):
     bx, by, bz, wr, wi = coefs
-    mr, nr = near(u, at, 0, p, step, bx, by, bz)
-    mi, ni = near(u, at, 1, p, step, bx, by, bz)
-    vr, vi = weigh(g[0, pl.ds(gat, step)] + nr, g[1, pl.ds(gat, step)] + ni, p, step, wr, wi)
+    re, im = fields
+    mr, nr = near(u, re, at, p, step, bx, by, bz)
+    mi, ni = near(u, im, at, p, step, bx, by, bz)
+    vr, vi = weigh(g[re, pl.ds(gat, step)] + nr, g[im, pl.ds(gat, step)] + ni, p, step, wr, wi)
     rest = 1.0 - omega_damp
     return rest * mr + vr, rest * mi + vi
 
 
-def resid_planes(u, at, g, gat, p, step, coefs, dr, si):
+def resid_planes(u, fields, at, g, gat, p, step, coefs, dr, si):
     bx, by, bz = coefs[:3]
-    mr, nr = near(u, at, 0, p, step, bx, by, bz)
-    mi, ni = near(u, at, 1, p, step, bx, by, bz)
+    re, im = fields
+    mr, nr = near(u, re, at, p, step, bx, by, bz)
+    mi, ni = near(u, im, at, p, step, bx, by, bz)
     d, e = dr[pl.ds(p, step)], si[pl.ds(p, step)]
-    return g[0, pl.ds(gat, step)] + nr - (d * mr + e * mi), g[1, pl.ds(gat, step)] + ni - (d * mi - e * mr)
+    return g[re, pl.ds(gat, step)] + nr - (d * mr + e * mi), g[im, pl.ds(gat, step)] + ni - (d * mi - e * mr)
 
 
 def pick(nrow, ncol, down, value):
@@ -225,93 +227,122 @@
         copy.wait()
 
 
-def spread_kernel(kept, came, close, far):
+def rows_kernel(kept, came, out, ends):
+    y = lax.axis_index("gy")
+    fields, half, rows, _ = kept.shape
+    rho = fields - 3
+    for t, ref in enumerate((kept, came)):
+        for h in range(2):
+            at = 0
+            for f in range(fields):
+                n = HALO + 1 if f == rho else HALO
+                for i in range(half):
+                    ends[h, t, at : at + n, :] = ref[f, i, (rows - n if h else 0) : (rows if h else n), :]
+                    at += n
+    for d in range(out.shape[0]):
+        out[d] = ends[jnp.where(y < d, 1, 0)]
+
+
+def lay_kernel(kept, came, ends, g, rho, sr, si, to_gz, to_gx):
     k = lax.axis_index("gz")
-    m = close.shape[0]
-    half = kept.shape[1]
-    rest = half - HALO
-    for t, ref in enumerate((kept, came)):
+    y = lax.axis_index("gy")
+    fields, half, rows, lanes = kept.shape
+    m2 = fields - 3
+    arrays = [g.at[f] for f in range(m2)] + [rho, sr, si]
+    for f, ref in enumerate(arrays):
+        first = HALO + 1 if f == m2 else HALO
+        for i in range(half):
+            ref[first + i] = jnp.zeros(ref.shape[1:], F32)
+        for t, src in enumerate((kept, came)):
+            z = k if t == 0 else 1 - k
+            spot = pl.ds(pl.multiple_of(z * lanes, lanes), lanes)
+            for i in range(half):
+                ref[first + i, SIDE : SIDE + rows, spot] = src[f, i]
+    for high in range(2):
+        count = ends.shape[0]
+        there = jnp.where(y < count - 1, 1.0, 0.0) if high else jnp.where(y > 0, 1.0, 0.0)
+        peer = jnp.minimum(y + 1, count - 1) if high else jnp.maximum(y - 1, 0)
+        for z in range(2):
+            slot = jnp.where(k == z, 0, 1)
+            at = 0
+            for f, ref in enumerate(arrays):
+                n = HALO + 1 if f == m2 else HALO
+                row = SIDE + rows if high else SIDE - n
+                for i in range(half):
+                    ref[n + i, row : row + n, z * lanes : (z + 1) * lanes] = ends[peer, slot, at : at + n, :] * there
+                    at += n
+    for out, up in ((to_gz, 1 - k), (to_gx, k)):
+        two, three = HALO + up * (half - HALO), HALO + 1 + up * (half - HALO - 1)
+        for j, ref in enumerate(arrays[:m2] + [sr, si]):
+            out[HALO * j : HALO * (j + 1)] = ref[pl.ds(two, HALO)]
+        out[HALO * (m2 + 2) :] = rho[pl.ds(three, HALO + 1)]
+
+
+def fine_kernel(from_gz, from_gx, _g, _rho, _sr, _si, g, rho, sr, si, bx, by, bz, wr, wi, own, up_gz, up_gx, up_gy, packed, dr, ua, left, right, narrow):
+    k = lax.axis_index("gz")
+    m2, pad, ny, nz = g.shape
+    m = m2 // 2
+    half = pad - 2 * HALO
+    rows = ny - 2 * SIDE
+    for came, low in ((from_gx, k), (from_gz, 1 - k)):
+        two, three = low * (half + HALO), low * (half + HALO + 1)
+        for j, ref in enumerate([g.at[f] for f in range(m2)] + [sr, si]):
+            ref[pl.ds(two, HALO)] = came[HALO * j : HALO * (j + 1)]
+        rho[pl.ds(three, HALO + 1)] = came[HALO * (m2 + 2) :]
+    level_coefs(rho, sr, si, 1.0, bx, by, bz, wr, wi, dr, 1, 0, pad)
+    coefs = (bx, by, bz, wr, wi)
+
+    def first(p):
         for r in range(m):
-            for j, f in enumerate((r, m + r, 2 * m + 1, 2 * m + 2)):
-                close[r, t, HALO * j : HALO * (j + 1)] = ref[f, pl.ds(k * rest, HALO)]
-                far[r, t, rest * j : rest * (j + 1)] = ref[f, pl.ds((1 - k) * HALO, rest)]
-            close[r, t, 4 * HALO : 5 * HALO + 1] = ref[2 * m, pl.ds(k * (rest - 1), HALO + 1)]
-            far[r, t, 4 * rest : 5 * rest - 1] = ref[2 * m, pl.ds((1 - k) * (HALO + 1), rest - 1)]
-
-
-def edge_kernel(close, far, out):
-    k = lax.axis_index("gz")
-    for s in range(close.shape[0]):
-        for t in range(2):
-            out[s, t, 0 : 4 * HALO] = far[s, t, 0 : 4 * HALO]
-            out[s, t, pl.ds(4 * HALO + k, HALO)] = close[s, t, pl.ds(5 * HALO - 1 - k, HALO)]
-            out[s, t, 5 * HALO - k * HALO] = far[s, t, 4 * HALO]
-
-
-def put_planes(came, other, arrays, rho, first, first_rho):
-    k = lax.axis_index("gz")
-    rows, lanes = came.shape[3:]
-    count = came.shape[2] // 4
-    for s in range(came.shape[0]):
-        for t in range(2):
-            z = jnp.where(k == t, 1, 0) if other else jnp.where(k == t, 0, 1)
-            spot = (slice(s * rows, (s + 1) * rows), pl.ds(pl.multiple_of(z * lanes, lanes), lanes))
-            for j, ref in enumerate(arrays):
-                ref[(pl.ds(first, count), *spot)] = came[s, t, count * j : count * (j + 1)]
-            rho[(pl.ds(first_rho, came.shape[2] - 4 * count), *spot)] = came[s, t, 4 * count :]
-
-
-def lay_kernel(close, far, from_gx, g, rho, sr, si, bx, by, bz, wr, wi, dr):
-    k = lax.axis_index("gz")
-    pad = g.shape[1]
-    half = pad - 2 * HALO
-    rest = half - HALO
-    arrays = (g.at[0], g.at[1], sr, si)
-    put_planes(close, False, arrays, rho, HALO + k * rest, HALO + 1 + k * (rest - 1))
-    put_planes(far, False, arrays, rho, HALO + (1 - k) * HALO, HALO + 1 + (1 - k) * (HALO + 1))
-    put_planes(from_gx, True, arrays, rho, k * (half + HALO), k * (half + HALO + 1))
-    level_coefs(rho, sr, si, 1.0, bx, by, bz, wr, wi, dr, 1, k * (HALO + 1), pad - HALO - 1)
-
-
-def fine_kernel(from_gz, *refs):
-    g, rho, sr, si, bx, by, bz, wr, wi, dr, own, up_gz, up_gx, packed, ua, sums, narrow = refs[10:]
-    k = lax.axis_index("gz")
-    pad, ny, nz = g.shape[1:]
-    half = pad - 2 * HALO
-    put_planes(from_gz, True, (g.at[0], g.at[1], sr, si), rho, (1 - k) * (half + HALO), (1 - k) * (half + HALO + 1))
-    level_coefs(rho, sr, si, 1.0, bx, by, bz, wr, wi, dr, 1, (1 - k) * (pad - HALO - 1), HALO + 1)
-    coefs = (bx, by, bz, wr, wi)
-
-    def first(p):
-        ua[0, pl.ds(p, 1)], ua[1, pl.ds(p, 1)] = weigh(g[0, pl.ds(p, 1)], g[1, pl.ds(p, 1)], p, 1, wr, wi)
+            ua[r, pl.ds(p, 1)], ua[m + r, pl.ds(p, 1)] = weigh(g[r, pl.ds(p, 1)], g[m + r, pl.ds(p, 1)], p, 1, wr, wi)
 
     loop(pad, first)
 
     def second(i):
         p = i + 1
-        own[0, pl.ds(i, 1)], own[1, pl.ds(i, 1)] = sweep_planes(ua, p, g, p, p, 1, coefs)
+        for r in range(m):
+            own[r, pl.ds(i, 1)], own[m + r, pl.ds(i, 1)] = sweep_planes(ua, (r, m + r), p, g, p, p, 1, coefs)
 
     loop(pad - 2, second)
-    for c in range(2):
-        up_gz[c] = own[c, 2 + (1 - k) * (half - 3)]
-        up_gx[c] = own[c, 2 + k * (half - 3)]
-
+    lanes = nz // 2
+    for f in range(m2):
+        up_gz[f] = own[f, 2 + (1 - k) * (half - 3), SIDE : SIDE + rows, :]
+        up_gx[f] = own[f, 2 + k * (half - 3), SIDE : SIDE + rows, :]
+        for i in range(half):
+            for h, row in enumerate((SIDE + 1, SIDE + rows - 2)):
+                for z in range(2):
+                    at = z * m2 * half + f * half + i
+                    up_gy[h, at : at + 1, :] = own[f, i + 1, row : row + 1, z * lanes : (z + 1) * lanes]
     pairs = half // 2
 
     def down(q):
         p = HALO + 2 * q
-        ar, ai = resid_planes(own, p - 1, g, p, p, 1, coefs, dr, si)
-        br, bi = resid_planes(own, p, g, p + 1, p + 1, 1, coefs, dr, si)
-        totals = (ar + br, ai + bi, rho[pl.ds(p + 1, 1)] + rho[pl.ds(p + 2, 1)], sr[pl.ds(p, 1)] + sr[pl.ds(p + 1, 1)], si[pl.ds(p, 1)] + si[pl.ds(p + 1, 1)])
-        for j, v in enumerate(totals):
-            sums[pl.ds(pl.multiple_of((j * pairs + q) * ny, ny), ny), :] = v[0]
+        totals = {}
+        for r in range(m):
+            ar, ai = resid_planes(own, (r, m + r), p - 1, g, p, p, 1, coefs, dr, si)
+            br, bi = resid_planes(own, (r, m + r), p, g, p + 1, p + 1, 1, coefs, dr, si)
+            totals[r], totals[m + r] = ar + br, ai + bi
+        totals[m2] = rho[pl.ds(p + 1, 1)] + rho[pl.ds(p + 2, 1)]
+        for j, ref in ((m2 + 1, sr), (m2 + 2, si)):
+            totals[j] = ref[pl.ds(p, 1)] + ref[pl.ds(p + 1, 1)]
+        for j, v in totals.items():
+            spot = pl.ds(pl.multiple_of((j * pairs + q) * ny, ny), ny)
+            left[spot, :] = v[0, :, :lanes]
+            right[spot, :] = v[0, :, lanes:]
 
     loop(pairs, down)
-    narrow[...] = dot(sums[...], pick(nz, nz // 2, True, 0.125))
-    n = 5 * pairs * ny // 2
-    done = (narrow[pl.ds(0, n, 2), :] + narrow[pl.ds(1, n, 2), :]).reshape(5, pairs, ny // 2, nz // 2)
-    for d in range(packed.shape[0]):
-        packed[d] = done
+    n = (m2 + 3) * pairs * ny // 2
+    both = [ref[pl.ds(0, n, 2), :] + ref[pl.ds(1, n, 2), :] for ref in (left, right)]
+    narrow[...] = dot(jnp.concatenate(both, axis=1), pick(nz, lanes, True, 0.125))
+    for q in range(pairs):
+        done = []
+        for j in range(m2 + 3):
+            at = (j * pairs + q) * (ny // 2) + SIDE // 2
+            done.append(narrow[at : at + rows // 2, :])
+        for d in range(packed.shape[0]):
+            r = d % m
+            for a, j in enumerate((r, m + r, m2, m2 + 1, m2 + 2)):
+                packed[d, a, q] = done[j]
 
 
 def coarse_kernel(
@@ -322,8 +353,10 @@
 ):
     k = lax.axis_index("gz")
     chip = lax.axis_index("gx")
-    chips, _, pairs, ny, nz = mine.shape
-    n1 = sr1.shape[0]
+    _, _, pairs, rows, nz = mine.shape
+    n1, ny = sr1.shape[:2]
+    parts = ny // rows
+    chips = mine.shape[0] // parts
     zero = jnp.zeros((1, ny, nz), F32)
     rho1[pl.ds(0, 1)] = zero
     rho1[pl.ds(n1 + 1, 1)] = zero
@@ -334,11 +367,14 @@
     for s in range(chips):
         for ref, z in ((mine, k), (other, 1 - k)):
             at = 2 * pairs * s + pairs * z
-            for c in range(2):
-                g1[c, pl.ds(at, pairs)] = ref[s, c]
-            rho1[pl.ds(at + 1, pairs)] = ref[s, 2]
-            sr1[pl.ds(at, pairs)] = ref[s, 3]
-            si1[pl.ds(at, pairs)] = ref[s, 4]
+            for y in range(parts):
+                spot = slice(y * rows, (y + 1) * rows)
+                e = s * parts + y
+                for c in range(2):
+                    g1[c, pl.ds(at, pairs), spot] = ref[e, c]
+                rho1[pl.ds(at + 1, pairs), spot] = ref[e, 2]
+                sr1[pl.ds(at, pairs), spot] = ref[e, 3]
+                si1[pl.ds(at, pairs), spot] = ref[e, 4]
     step1 = 4
     level_coefs(rho1, sr1, si1, 0.25, bx1, by1, bz1, wr1, wi1, dr1, step1, 0, n1)
     coefs1 = (bx1, by1, bz1, wr1, wi1)
@@ -353,7 +389,7 @@
     def sweep1(src, dst):
         def body(i):
             p = i * step1
-            r, m = sweep_planes(src, p + 1, g1, p, p, step1, coefs1)
+            r, m = sweep_planes(src, (0, 1), p + 1, g1, p, p, step1, coefs1)
             dst[0, pl.ds(p + 1, step1)], dst[1, pl.ds(p + 1, step1)] = r, m
 
         loop(n1 // step1, body)
@@ -364,7 +400,7 @@
 
     def down(q):
         p = 2 * q
-        r, m = resid_planes(ub1, p + 1, g1, p, p, 2, coefs1, dr1, si1)
+        r, m = resid_planes(ub1, (0, 1), p + 1, g1, p, p, 2, coefs1, dr1, si1)
         totals = (r[0] + r[1], m[0] + m[1], rho1[p + 1] + rho1[p + 2], sr1[p] + sr1[p + 1], si1[p] + si1[p + 1])
         for j, v in enumerate(totals):
             sums[pl.ds(pl.multiple_of((j * n2 + q) * ny, ny), ny), :] = v
@@ -387,7 +423,7 @@
     ua2[0, pl.ds(1, n2)], ua2[1, pl.ds(1, n2)] = weigh(g2[0], g2[1], 0, n2, wr2, wi2)
     src, dst = ua2, ub2
     for _ in range(CSWEEPS - 1):
-        dst[0, pl.ds(1, n2)], dst[1, pl.ds(1, n2)] = sweep_planes(src, 1, g2, 0, 0, n2, coefs2)
+        dst[0, pl.ds(1, n2)], dst[1, pl.ds(1, n2)] = sweep_planes(src, (0, 1), 1, g2, 0, 0, n2, coefs2)
         src, dst = dst, src
 
     widen = pick(nz, nz, False, 1.0)
@@ -407,61 +443,106 @@
     sweep1(ub1, ua1)
     sweep1(ua1, ub1)
 
-    quads = out.shape[1]
-    out[...] = ub1[:, pl.ds((2 * chip + k) * pairs, quads)]
-
-
-def last_kernel(u1, own, from_gz, from_gx, g0, bx0, by0, bz0, wr0, wi0, out, ua0, ub0, tall):
+    out[...] = ub1[:, pl.ds((2 * chip + k) * pairs, 2 + pairs)]
+
+
+def pack_kernel(u1, up_gy, from_gz, from_gx, out, edges):
     k = lax.axis_index("gz")
-    quads, ny, nz = u1.shape[1:]
-    pad, fine_y, fine_z = ua0.shape[1:]
+    me = lax.axis_index("gy")
+    edges[k] = from_gz[...]
+    edges[1 - k] = from_gx[...]
+    _, quads, ny, nz = u1.shape
+    parts = out.shape[0]
+    rows = ny // parts
+    edge = SIDE // 2
+    tall_rows = rows + 2 * edge
+    for y in range(parts):
+        low, high = max(y * rows - edge, 0), min((y + 1) * rows + edge, ny)
+        for c in range(2):
+            for q in range(quads):
+                at = (c * quads + q) * tall_rows
+                skip = low - (y * rows - edge)
+                end = skip + high - low
+                if skip:
+                    out[y, at : at + skip, :] = jnp.zeros((skip, nz), F32)
+                out[y, at + skip : at + end, :] = u1[c, q, low:high, :]
+                if end < tall_rows:
+                    out[y, at + end : at + tall_rows, :] = jnp.zeros((tall_rows - end, nz), F32)
+        out[y, 2 * quads * tall_rows :, :] = up_gy[jnp.where(me < y, 1, 0)]
+
+
+def last_kernel(back, own, edges, g, bx, by, bz, wr, wi, out, ua, ub, tall):
+    k = lax.axis_index("gz")
+    y = lax.axis_index("gy")
+    m2, pad, ny, nz = ua.shape
+    m = m2 // 2
     half = pad - 2 * HALO
-    rows = quads * ny
-    ua0[:, pl.ds(1, pad - 2)] = own[...]
-    ua0[:, k * (pad - 1)] = from_gx[...]
-    ua0[:, (1 - k) * (pad - 1)] = from_gz[...]
-    for h in range(fine_z // nz):
-        col = lax.broadcasted_iota(jnp.int32, (nz, nz), 1) + h * nz
-        row = lax.broadcasted_iota(jnp.int32, (nz, nz), 0)
-        widen = jnp.where(row == col // 2, 1.0, 0.0).astype(F32)
-        for c in range(2):
-            v = dot(u1[c].reshape(rows, nz), widen)
-            tall[pl.ds(0, rows, 2), :] = v
-            tall[pl.ds(1, rows, 2), :] = v
-            for q in range(quads):
-                w = tall[pl.ds(q * fine_y, fine_y), :]
-                for j in range(2):
-                    p = 2 * q + j
-                    ua0[c, p, :, h * nz : (h + 1) * nz] = ua0[c, p, :, h * nz : (h + 1) * nz] + w
-    coefs0 = (bx0, by0, bz0, wr0, wi0)
+    rows = ny - 2 * SIDE
+    quads = pad // 2
+    lanes = nz // 2
+    ua[:, pl.ds(1, pad - 2)] = own[...]
+    parts = back.shape[0]
+    blank = jnp.zeros((m2, ny, nz), F32)
+    for p, side in ((0, 1), (pad - 1, 0)):
+        ua[:, p] = blank
+        ua[:, p, SIDE : SIDE + rows, :] = edges[side]
+    used = 2 * quads * ny // 2
+    for high in range(2):
+        there = jnp.where(y < parts - 1, 1.0, 0.0) if high else jnp.where(y > 0, 1.0, 0.0)
+        peer = jnp.minimum(y + 1, parts - 1) if high else jnp.maximum(y - 1, 0)
+        row = SIDE + rows + 1 if high else SIDE - 2
+        block = back[peer, used:, :] * there
+        for z in range(2):
+            for f in range(m2):
+                for i in range(half):
+                    at = z * m2 * half + f * half + i
+                    ua[f, HALO + i, row : row + 1, z * lanes : (z + 1) * lanes] = block[at : at + 1, :]
+    u1 = back[:, :used, :].reshape(m * used, lanes)
+    for h in range(2):
+        col = lax.broadcasted_iota(jnp.int32, (lanes, lanes), 1) + h * lanes
+        line = lax.broadcasted_iota(jnp.int32, (lanes, lanes), 0)
+        v = dot(u1, jnp.where(line == col // 2, 1.0, 0.0).astype(F32))
+        tall[pl.ds(0, m * used, 2), :] = v
+        tall[pl.ds(1, m * used, 2), :] = v
+        spot = slice(h * lanes, (h + 1) * lanes)
+        for r in range(m):
+            for c in range(2):
+                for q in range(quads):
+                    at = ((r * 2 + c) * quads + q) * ny
+                    w = tall[at : at + ny, :]
+                    f = c * m + r
+                    for j in range(2):
+                        ua[f, 2 * q + j, :, spot] = ua[f, 2 * q + j, :, spot] + w
+    coefs = (bx, by, bz, wr, wi)
 
     def third(i):
         p = i + 1
-        ub0[0, pl.ds(p, 1)], ub0[1, pl.ds(p, 1)] = sweep_planes(ua0, p, g0, p, p, 1, coefs0)
+        for r in range(m):
+            ub[r, pl.ds(p, 1)], ub[m + r, pl.ds(p, 1)] = sweep_planes(ua, (r, m + r), p, g, p, p, 1, coefs)
 
     loop(pad - 2, third)
-    dests, _, _, _, drows, lanes = out.shape
 
     def fourth(i):
         p = i + HALO
-        r, m = sweep_planes(ub0, p, g0, p, p, 1, coefs0)
-        for c, v in enumerate((r, m)):
-            for d in range(dests):
+        for r in range(m):
+            for c, v in enumerate(sweep_planes(ub, (r, m + r), p, g, p, p, 1, coefs)):
                 for z in range(2):
-                    out[d, z, c, i] = v[0, d * drows : (d + 1) * drows, z * lanes : (z + 1) * lanes]
+                    slot = jnp.where(k == z, 0, 1)
+                    out[slot, c, r, i] = v[0, SIDE : SIDE + rows, z * lanes : (z + 1) * lanes]
 
     loop(half, fourth)
 
 
-def gather_kernel(came, out):
-    half = came.shape[3]
-    for r in range(came.shape[0]):
-        for z in range(2):
-            for c in range(2):
-                out[c, r, z * half : (z + 1) * half] = came[r, z, c]
-
-
-def call(kernel, outs, args, scratch=(), limit=24, space=pltpu.VMEM, sems=None, cost=None, aliases=None):
+def gather_kernel(kept, came, out):
+    k = lax.axis_index("gz")
+    half = kept.shape[2]
+    for side, ref in ((k, kept), (1 - k, came)):
+        for c in range(2):
+            for r in range(kept.shape[1]):
+                out[c, r, pl.ds(side * half, half)] = ref[c, r]
+
+
+def call(kernel, outs, args, scratch=(), limit=14, space=pltpu.VMEM, sems=None, cost=None, aliases=None):
     single = not isinstance(outs, list)
     shapes = [outs] if single else outs
     result = pl.pallas_call(
@@ -488,31 +569,37 @@
     fields = (rhs, density, shift_real, shift_imag)
 
     own_half = (2 * m + 3, half, rows, lanes)
-    away, kept = call(send_kernel, [own_half, own_half], tuple(pltpu.with_memory_space_constraint(f, pltpu.HBM) for f in fields), space=pltpu.HBM, sems=10)
+    placed = tuple(pltpu.with_memory_space_constraint(f, pltpu.HBM) for f in fields)
+    away, kept = call(send_kernel, [own_half, own_half], placed, space=pltpu.HBM, sems=10)
     came = lax.ppermute(away, "gz", swap)
-    edges = (m, 2, 5 * HALO + 1, rows, lanes)
-    close, far = call(spread_kernel, [edges, (m, 2, 5 * (half - HALO) - 1, rows, lanes)], (kept, came))
-    close = lax.all_to_all(close, "gy", 0, 0, tiled=True)
-    from_gx = lax.ppermute(close, ("gx", "gz"), ends)
-    far = lax.all_to_all(far, "gy", 0, 0, tiled=True)
-    to_gz = call(edge_kernel, edges, (close, far))
+    rim = ((2 * m + 3) * HALO + 1) * half
+    rim = (m, 2, -(-rim // 8) * 8, lanes)
+    ends_y = call(rows_kernel, rim, (kept, came), scratch=[(2,) + rim[1:]])
+    ends_y = lax.all_to_all(ends_y, "gy", 0, 0, tiled=True)
+
+    plane = (rows + 2 * SIDE, nz)
+    laid = [(2 * m, pad) + plane, (pad + 2,) + plane, (pad,) + plane, (pad,) + plane]
+    edges = (HALO * (2 * m + 2) + HALO + 1,) + plane
+    *state, to_gz, to_gx = call(lay_kernel, laid + [edges, edges], (kept, came, ends_y))
+    from_gx = lax.ppermute(to_gx, ("gx", "gz"), ends)
     from_gz = lax.ppermute(to_gz, "gz", swap)
 
     pairs = half // 2
-    plane = (ny, nz)
-    laid = [(2, pad) + plane, (pad + 2,) + plane, (pad,) + plane, (pad,) + plane, (pad + 1,) + plane] + [(pad,) + plane] * 5
-    state = call(lay_kernel, laid, (close, far, from_gx), limit=24, cost=LAY_COST)
-    g, _, _, _, bx, by, bz, wr, wi, _, own, up_gz, up_gx, packed = call(
+    brow = (rows, nz)
+    tall0 = (2 * m + 3) * pairs * plane[0]
+    g, _, _, _, bx, by, bz, wr, wi, own, up_gz, up_gx, up_gy, packed = call(
         fine_kernel,
-        laid + [(2, pad - 2) + plane, (2,) + plane, (2,) + plane, (chips, 5, pairs, ny // 2, nz // 2)],
-        (from_gz, *state),
-        scratch=[(2, pad) + plane] + [(5 * pairs * ny, nz), (5 * pairs * ny, nz // 2)],
-        limit=24,
-        aliases={i + 1: i for i in range(len(laid))},
+        laid
+        + [(pad + 1,) + plane]
+        + [(pad,) + plane] * 4
+        + [(2 * m, pad - 2) + plane, (2 * m,) + brow, (2 * m,) + brow, (2, 4 * m * half, lanes), (chips * m, 5, pairs, rows // 2, lanes)],
+        (from_gz, from_gx, *state),
+        scratch=[(pad,) + plane, (2 * m, pad) + plane, (tall0, lanes), (tall0, lanes), (tall0 // 2, lanes)],
+        aliases={i + 2: i for i in range(len(laid))},
     )
     u_gx = lax.ppermute(up_gx, ("gx", "gz"), ends)
     u_gz = lax.ppermute(up_gz, "gz", swap)
-    mine = lax.all_to_all(packed, "gx", 0, 0, tiled=True)
+    mine = lax.all_to_all(packed, ("gx", "gy"), 0, 0, tiled=True)
     other = lax.ppermute(mine, "gz", swap)
 
     n1, n2 = chips * xs // 2, chips * xs // 4
@@ -521,23 +608,25 @@
     def level(n, p):
         return [(n + 2,) + p, (n,) + p, (n,) + p, (2, n) + p, (n + 1,) + p] + [(n,) + p] * 5 + [(2, n + 2) + p] * 2
 
+    used = (2 + pairs) * plane[0]
     u1 = call(
         coarse_kernel,
-        (2, pad // 2) + p1,
+        (2, 2 + pairs) + p1,
         (mine, other),
         scratch=level(n1, p1) + level(n2, p2) + [(5 * n2 * p1[0], p1[1])] * 2 + [(2 * n2 * p2[0], p1[1]), (2 * n2 * p1[0], p1[1])],
-        limit=32,
+        limit=14,
         cost=COARSE_COST,
     )
+    packed, halo = call(pack_kernel, [(m, used + 4 * m * half, lanes), (2, 2 * m) + brow], (u1, up_gy, u_gz, u_gx))
+    back = lax.all_to_all(packed, "gy", 0, 0, tiled=True)
     result = call(
         last_kernel,
-        (m, 2, 2, half, rows, lanes),
-        (u1, own, u_gz, u_gx, g, bx, by, bz, wr, wi),
-        scratch=[(2, pad) + plane, (2, pad) + plane, (pad * ny // 2, p1[1])],
-        limit=32,
+        (2, 2, m, half, rows, lanes),
+        (back, own, halo, g, bx, by, bz, wr, wi),
+        scratch=[(2 * m, pad) + plane, (2 * m, pad) + plane, (2 * m * used, lanes)],
     )
-    back = lax.all_to_all(result.reshape((2 * m,) + result.shape[2:]), ("gy", "gz"), 0, 0, tiled=True)
-    return call(gather_kernel, rhs.shape, (back.reshape(result.shape),))
+    last = lax.ppermute(result[1], "gz", swap)
+    return call(gather_kernel, rhs.shape, (result[0], last))
 
 
 def solution(mesh):

time: 83.3 us -> 77.5 us (0.930)
  blocking collectives: 62 us -> 54.8 us
  waiting for transfers between devices: 2.9 us -> 4.81 us
  starting transfers between devices: 4.33 us -> 2.72 us
  Pallas kernels: 13.7 us -> 14.8 us
    all_to_all x4 -> x3, blocking collectives: 62 us -> 54.8 us  [the longest x1 32.5 us: local_planes(): mine = lax.all_to_all(packed, ('gx', 'gy'), 0, 0, tiled=True)]
    ppermute x1, starting transfers between devices: 1.95 us -> 0.07 us  [local_planes(): from_gz = lax.ppermute(to_gz, 'gz', swap)]
    ppermute x1 -> x2, waiting for transfers between devices: 0.01 us -> 1.33 us  [the longest x1 1.33 us: local_planes(): last = lax.ppermute(result[1], 'gz', swap)]
    pallas_call x8, Pallas kernels: 13.7 us -> 14.8 us  [call(): pl.pallas_call(kernel, out_shape=[jax.ShapeDtypeStruct(s, F32) for s in s...]
  transfers between devices with their start and end apart: 6 -> 7, of which waited for: 3 -> 4; matrix products, arithmetic and copies ran while one was open for 0% -> 0% of each run, Pallas kernels for 8% -> 7%
where the time goes in v3:
time: 77.5 us; the launch traced here: 77.3 us
  blocking collectives  54.8 us (71%)
  Pallas kernels  14.8 us (19%)
  waiting for transfers between devices  4.81 us (6%)
  starting transfers between devices  2.72 us (4%)
    all_to_all x1, blocking collectives, local_planes(): mine = lax.all_to_all(packed, ('gx', 'gy'), 0, 0, tiled=True)  32.5 us
    pallas_call x8, Pallas kernels, call(): pl.pallas_call(kernel, out_shape=[jax.ShapeDtypeStruct(s, F32) for s in s...  14.8 us
    all_to_all x1, blocking collectives, local_planes(): ends_y = lax.all_to_all(ends_y, 'gy', 0, 0, tiled=True)  12.3 us
    all_to_all x1, blocking collectives, local_planes(): back = lax.all_to_all(packed, 'gy', 0, 0, tiled=True)  9.99 us
  transfers between devices with their start and end apart: 7, of which 4 were waited for; matrix products, arithmetic and copies ran while one was open for 0% of the time, Pallas kernels for 7%

profile of v3, /device:TPU:0, one launch (start us, length us, event | category | flops | bytes accessed | tf_op | source)
XLA Modules:
  0.0 77.3 jit_solution(2919927371299397237)
XLA Ops:
  0.0 1.2 %shard_map.46 = (f32[11,4,16,128]{3,2,1,0:T(8,128)S(1)}, f32[11,4,16,128]{3,2,1,0:T(8,128)S(1)}) custom-call(f32[2,4,8,16,128]{4,3,2,1,0:T(8,128)} %rhs.1, f32[8,16,128]{2,1,0:T(8,128)} %rho.1, f32[8,16,128]{2,1,0:T(8,128)} %sr.1, f32[8,16,128]{2,1,0:T(8,128)} %si.1), custom_call_target="tpu_custom_call" | custom-call | tf_op jit(solution)/shard_map/pallas_call | solution.py:548
  1.2 0.5 collective-permute-start
  1.8 1.3 %collective-permute-done.came = f32[11,4,16,128]{3,2,1,0:T(8,128)S(1)} collective-permute-done((f32[11,4,16,128]{3,2,1,0:T(8,128)S(1)}, f32[11,4,16,128]{3,2,1,0:T(8,128)S(1)}, u32[]{:S(2)}, u32[]{:S(2)}) %collective-permute-start) | collective-permute-done | bytes 360480 | tf_op jit(solution)/shard_map/ppermute | solution.py:574
  3.1 0.1 shard_map.47
  3.2 12.3 %all_to_all.15.ends = f32[4,2,96,128]{3,2,1,0:T(8,128)S(1)} all-to-all(f32[4,2,96,128]{3,2,1,0:T(8,128)S(1)} %shard_map.47), channel_id=1, replica_groups=mesh['gx'=4,'gy'=4,'gz'=2] {'gy'}, dimensions={0} | all-to-all | bytes 786432 | tf_op jit(solution)/shard_map/all_to_all | solution.py:578
  15.5 0.3 shard_map.48
  15.8 0.1 collective-permute-start.1
  15.8 0.7 collective-permute-start.2
  16.5 1.3 %collective-permute-done.1.from_gz = f32[23,24,256]{2,1,0:T(8,128)S(1)} collective-permute-done((f32[23,24,256]{2,1,0:T(8,128)S(1)}, f32[23,24,256]{2,1,0:T(8,128)S(1)}, u32[]{:S(2)}, u32[]{:S(2)}) %collective-permute-start.1) | collective-permute-done | bytes 565280 | tf_op jit(solution)/shard_map/ppermute | solution.py:585
  17.8 0.0 collective-permute-done.2.from_gx
  17.8 4.3 %shard_map.49 = (f32[8,8,24,256]{3,2,1,0:T(8,128)S(1)}, f32[10,24,256]{2,1,0:T(8,128)S(1)}, f32[8,24,256]{2,1,0:T(8,128)S(1)}, f32[8,24,256]{2,1,0:T(8,128)S(1)}...) custom-call(f32[23,24,256]{2,1,0:T(8,128)S(1)} %collective-permute-d, ...), custom_call_target="tpu_custom_call", output_to_operand_aliasing={{0}: (2, {}), {1}: (3, {}), {2}: (4, {}), {3}: (5, {})} | custom-call | tf_op jit(solution)/shard_map/pallas_call | solution.py:548
  22.1 32.5 %all_to_all.16.mine = f32[16,5,2,8,128]{4,3,2,1,0:T(8,128)S(1)} all-to-all(f32[16,5,2,8,128]{4,3,2,1,0:T(8,128)S(1)} %get-tuple-element.34), channel_id=1, replica_groups=mesh['gx'=4,'gy'=4,'gz'=2] {'gx','gy'}, dimensions={0} | all-to-all | bytes 1310720 | tf_op jit(solution)/shard_map/all_to_all | solution.py:602
  54.6 0.0 collective-permute-start.3
  54.6 0.5 collective-permute-start.4
  55.1 0.7 collective-permute-start.5
  55.7 0.9 %collective-permute-done.3.other = f32[16,5,2,8,128]{4,3,2,1,0:T(8,128)S(1)} collective-permute-done((f32[16,5,2,8,128]{4,3,2,1,0:T(8,128)S(1)}, f32[16,5,2,8,128]{4,3,2,1,0:T(8,128)S(1)}, u32[]{:S(2)}, u32[]{:S(2)}) %collective-permute-start.3) | collective-permute-done | bytes 655392 | tf_op jit(solution)/shard_map/ppermute | solution.py:603
  56.7 5.2 %shard_map.50.u1 = f32[2,4,32,128]{3,2,1,0:T(8,128)S(1)} custom-call(f32[16,5,2,8,128]{4,3,2,1,0:T(8,128)S(1)} %all_to_all.16.mine, f32[16,5,2,8,128]{4,3,2,1,0:T(8,128)S(1)} %collective-permute-done.3.other), custom_call_target="tpu_custom_call" | custom-call | flops 5000000000 | tf_op jit(solution)/shard_map/pallas_call | solution.py:548
  61.9 0.0 collective-permute-done.5.from_gx
  61.9 0.1 shard_map.51
  62.0 10.0 %all_to_all.17.back = f32[4,160,128]{2,1,0:T(8,128)S(1)} all-to-all(f32[4,160,128]{2,1,0:T(8,128)S(1)} %get-tuple-element.38), channel_id=1, replica_groups=mesh['gx'=4,'gy'=4,'gz'=2] {'gy'}, dimensions={0} | all-to-all | bytes 655360 | tf_op jit(solution)/shard_map/all_to_all | solution.py:621
  72.0 2.8 %shard_map.52 = f32[2,2,4,4,16,128]{5,4,3,2,1,0:T(8,128)S(1)} custom-call(f32[4,160,128]{2,1,0:T(8,128)S(1)} %all_to_all.17.back, f32[8,6,24,256]{3,2,1,0:T(8,128)S(1)} %get-tuple-element.39.own, f32[2,8,16,256]{3,2,1,0:T(8,128)S(1)} %get-tuple-element.40.edges, f32[8,8,24,256]{3,2,1,0:T(8,128)S(1)} %get-tuple-element.41.g, ...), custom_call_target="tpu_custom_call" | custom-call | tf_op jit(solution)/shard_map/pallas_call | solution.py:548
  74.9 0.3 collective-permute-start.6
  75.1 1.3 %collective-permute-done.6.came = f32[2,4,4,16,128]{4,3,2,1,0:T(8,128)S(1)} collective-permute-done((f32[2,4,4,16,128]{4,3,2,1,0:T(8,128)S(1)}, f32[2,4,4,16,128]{4,3,2,1,0:T(8,128)S(1)}, u32[]{:S(2)}, u32[]{:S(2)}) %collective-permute-start.6) | collective-permute-done | bytes 262176 | tf_op jit(solution)/shard_map/ppermute | solution.py:628
  76.5 0.8 %shard_map.53 = f32[2,4,8,16,128]{4,3,2,1,0:T(8,128)} custom-call(f32[2,4,4,16,128]{4,3,2,1,0:T(8,128)S(1)} %get-tuple-element.48.kept, f32[2,4,4,16,128]{4,3,2,1,0:T(8,128)S(1)} %collective-permute-done.6.came), custom_call_target="tpu_custom_call" | custom-call | tf_op jit(solution)/shard_map/pallas_call | solution.py:548
  (2 shorter events, 0.0 us)
Async XLA Ops:
  1.2 1.8 %collective-permute-start = (f32[11,4,16,128]{3,2,1,0:T(8,128)S(1)}, f32[11,4,16,128]{3,2,1,0:T(8,128)S(1)}, u32[]{:S(2)}, u32[]{:S(2)}) collective-permute-start(f32[11,4,16,128]{3,2,1,0:T(8,128)S(1)} %get-tuple-element.27), channel_id=1, source_target_pairs={{0,1},{1,0},{2,3},{3,2},{4,5},{5,4},{6,7},{7,6},{8,9},{9,8},{10,11... | collective-permute-start | bytes 1081352 | tf_op jit(solution)/shard_map/ppermute | solution.py:574
  15.8 2.0 %collective-permute-start.1 = (f32[23,24,256]{2,1,0:T(8,128)S(1)}, f32[23,24,256]{2,1,0:T(8,128)S(1)}, u32[]{:S(2)}, u32[]{:S(2)}) collective-permute-start(f32[23,24,256]{2,1,0:T(8,128)S(1)} %get-tuple-element.28), channel_id=1, source_target_pairs={{0,1},{1,0},{2,3},{3,2},{4,5},{5,4},{6,7},{7,6},{8,9},{9,8},{10,11... | collective-permute-start | bytes 1695752 | tf_op jit(solution)/shard_map/ppermute | solution.py:585
  15.8 2.0 %collective-permute-start.2 = (f32[23,24,256]{2,1,0:T(8,128)S(1)}, f32[23,24,256]{2,1,0:T(8,128)S(1)}, u32[]{:S(2)}, u32[]{:S(2)}) collective-permute-start(f32[23,24,256]{2,1,0:T(8,128)S(1)} %get-tuple-element.29), channel_id=1, source_target_pairs={{1,8},{8,1},{9,16},{16,9},{17,24},{24,17},{3,10},{10,3},{11,18},{1... | collective-permute-start | bytes 1695752 | tf_op jit(solution)/shard_map/ppermute | solution.py:584
  54.6 2.1 %collective-permute-start.3 = (f32[16,5,2,8,128]{4,3,2,1,0:T(8,128)S(1)}, f32[16,5,2,8,128]{4,3,2,1,0:T(8,128)S(1)}, u32[]{:S(2)}, u32[]{:S(2)}) collective-permute-start(f32[16,5,2,8,128]{4,3,2,1,0:T(8,128)S(1)} %all_to_all.16.mine), channel_id=1, source_target_pairs={{0,1},{1,0},{2,3},{3,2},{4,5},{5,4},{6,7},{7,6},{8,9},{9,8},{10,11... | collective-permute-start | bytes 1966088 | tf_op jit(solution)/shard_map/ppermute | solution.py:603
  54.6 7.3 %collective-permute-start.4 = (f32[8,16,256]{2,1,0:T(8,128)S(1)}, f32[8,16,256]{2,1,0:T(8,128)S(1)}, u32[]{:S(2)}, u32[]{:S(2)}) collective-permute-start(f32[8,16,256]{2,1,0:T(8,128)S(1)} %get-tuple-element.36), channel_id=1, source_target_pairs={{0,1},{1,0},{2,3},{3,2},{4,5},{5,4},{6,7},{7,6},{8,9},{9,8},{10,11... | collective-permute-start | bytes 393224 | tf_op jit(solution)/shard_map/ppermute | solution.py:601
  55.1 6.8 %collective-permute-start.5 = (f32[8,16,256]{2,1,0:T(8,128)S(1)}, f32[8,16,256]{2,1,0:T(8,128)S(1)}, u32[]{:S(2)}, u32[]{:S(2)}) collective-permute-start(f32[8,16,256]{2,1,0:T(8,128)S(1)} %get-tuple-element.37), channel_id=1, source_target_pairs={{1,8},{8,1},{9,16},{16,9},{17,24},{24,17},{3,10},{10,3},{11,18},{1... | collective-permute-start | bytes 393224 | tf_op jit(solution)/shard_map/ppermute | solution.py:600
  74.9 1.6 %collective-permute-start.6 = (f32[2,4,4,16,128]{4,3,2,1,0:T(8,128)S(1)}, f32[2,4,4,16,128]{4,3,2,1,0:T(8,128)S(1)}, u32[]{:S(2)}, u32[]{:S(2)}) collective-permute-start(f32[2,4,4,16,128]{4,3,2,1,0:T(8,128)S(1)} %get-tuple-element.47), channel_id=1, source_target_pairs={{0,1},{1,0},{2,3},{3,2},{4,5},{5,4},{6,7},{7,6},{8,9},{9,8},{10,11... | collective-permute-start | bytes 786440 | tf_op jit(solution)/shard_map/ppermute | solution.py:628

commit v4 on v3

--- a/solution.py
+++ b/solution.py
@@ -122,6 +122,7 @@
 SIDE = 4
 MIB = 1 << 20
 COARSE_COST = 5 * 10**9
+NEAR_COST = 2 * 10**9
 F32 = jnp.float32
 
 
@@ -227,7 +228,7 @@
         copy.wait()
 
 
-def rows_kernel(kept, came, out, ends):
+def rows_kernel(kept, came, to_even, to_odd, ends):
     y = lax.axis_index("gy")
     fields, half, rows, _ = kept.shape
     rho = fields - 3
@@ -239,11 +240,12 @@
                 for i in range(half):
                     ends[h, t, at : at + n, :] = ref[f, i, (rows - n if h else 0) : (rows if h else n), :]
                     at += n
-    for d in range(out.shape[0]):
-        out[d] = ends[jnp.where(y < d, 1, 0)]
-
-
-def lay_kernel(kept, came, ends, g, rho, sr, si, to_gz, to_gx):
+    even = lax.rem(y, 2)
+    to_even[...] = ends[1 - even]
+    to_odd[...] = ends[even]
+
+
+def lay_kernel(kept, came, even, odd, g, rho, sr, si, to_gz, to_gx, ends):
     k = lax.axis_index("gz")
     y = lax.axis_index("gy")
     fields, half, rows, lanes = kept.shape
@@ -258,10 +260,11 @@
             spot = pl.ds(pl.multiple_of(z * lanes, lanes), lanes)
             for i in range(half):
                 ref[first + i, SIDE : SIDE + rows, spot] = src[f, i]
+    ends[0] = even[...]
+    ends[1] = odd[...]
     for high in range(2):
-        count = ends.shape[0]
-        there = jnp.where(y < count - 1, 1.0, 0.0) if high else jnp.where(y > 0, 1.0, 0.0)
-        peer = jnp.minimum(y + 1, count - 1) if high else jnp.maximum(y - 1, 0)
+        there = jnp.where(y < lax.axis_size("gy") - 1, 1.0, 0.0) if high else jnp.where(y > 0, 1.0, 0.0)
+        peer = lax.rem(y, 2) if high else 1 - lax.rem(y, 2)
         for z in range(2):
             slot = jnp.where(k == z, 0, 1)
             at = 0
@@ -278,32 +281,49 @@
         out[HALO * (m2 + 2) :] = rho[pl.ds(three, HALO + 1)]
 
 
-def fine_kernel(from_gz, from_gx, _g, _rho, _sr, _si, g, rho, sr, si, bx, by, bz, wr, wi, own, up_gz, up_gx, up_gy, packed, dr, ua, left, right, narrow):
+def side_planes(came, low, g, rho, sr, si, bx, by, bz, wr, wi, dr, ua, own, rest):
+    m2, pad = g.shape[:2]
+    m = m2 // 2
+    half = pad - 2 * HALO
+    two, three = low * (half + HALO), low * (half + HALO + 1)
+    for j, ref in enumerate([g.at[f] for f in range(m2)] + [sr, si]):
+        ref[pl.ds(two, HALO)] = came[HALO * j : HALO * (j + 1)]
+    rho[pl.ds(three, HALO + 1)] = came[HALO * (m2 + 2) :]
+    count = HALO + 1 if rest else pad - HALO - 1
+    start = low * (pad - count)
+    level_coefs(rho, sr, si, 1.0, bx, by, bz, wr, wi, dr, 1, start, count)
+
+    def first(i):
+        p = start + i
+        for r in range(m):
+            ua[r, pl.ds(p, 1)], ua[m + r, pl.ds(p, 1)] = weigh(g[r, pl.ds(p, 1)], g[m + r, pl.ds(p, 1)], p, 1, wr, wi)
+
+    loop(count, first)
+    done = HALO + 1 if rest else half - 1
+    begin = low * (pad - 2 - done)
+
+    def second(i):
+        at = begin + i
+        p = at + 1
+        for r in range(m):
+            own[r, pl.ds(at, 1)], own[m + r, pl.ds(at, 1)] = sweep_planes(ua, (r, m + r), p, g, p, p, 1, (bx, by, bz, wr, wi))
+
+    loop(done, second)
+
+
+def near_kernel(from_gz, _g, _rho, _sr, _si, *state):
+    side_planes(from_gz, 1 - lax.axis_index("gz"), *state, False)
+
+
+def fine_kernel(from_gx, *refs):
+    g, rho, sr, si, bx, by, bz, wr, wi, dr, ua, own, up_gz, up_gx, up_gy, packed, left, right, narrow = refs[12:]
     k = lax.axis_index("gz")
+    side_planes(from_gx, k, g, rho, sr, si, bx, by, bz, wr, wi, dr, ua, own, True)
+    coefs = (bx, by, bz, wr, wi)
     m2, pad, ny, nz = g.shape
     m = m2 // 2
     half = pad - 2 * HALO
     rows = ny - 2 * SIDE
-    for came, low in ((from_gx, k), (from_gz, 1 - k)):
-        two, three = low * (half + HALO), low * (half + HALO + 1)
-        for j, ref in enumerate([g.at[f] for f in range(m2)] + [sr, si]):
-            ref[pl.ds(two, HALO)] = came[HALO * j : HALO * (j + 1)]
-        rho[pl.ds(three, HALO + 1)] = came[HALO * (m2 + 2) :]
-    level_coefs(rho, sr, si, 1.0, bx, by, bz, wr, wi, dr, 1, 0, pad)
-    coefs = (bx, by, bz, wr, wi)
-
-    def first(p):
-        for r in range(m):
-            ua[r, pl.ds(p, 1)], ua[m + r, pl.ds(p, 1)] = weigh(g[r, pl.ds(p, 1)], g[m + r, pl.ds(p, 1)], p, 1, wr, wi)
-
-    loop(pad, first)
-
-    def second(i):
-        p = i + 1
-        for r in range(m):
-            own[r, pl.ds(i, 1)], own[m + r, pl.ds(i, 1)] = sweep_planes(ua, (r, m + r), p, g, p, p, 1, coefs)
-
-    loop(pad - 2, second)
     lanes = nz // 2
     for f in range(m2):
         up_gz[f] = own[f, 2 + (1 - k) * (half - 3), SIDE : SIDE + rows, :]
@@ -446,13 +466,14 @@
     out[...] = ub1[:, pl.ds((2 * chip + k) * pairs, 2 + pairs)]
 
 
-def pack_kernel(u1, up_gy, from_gz, from_gx, out, edges):
+def pack_kernel(u1, up_gy, from_gz, from_gx, *refs):
+    *outs, edges, blocks = refs
     k = lax.axis_index("gz")
     me = lax.axis_index("gy")
     edges[k] = from_gz[...]
     edges[1 - k] = from_gx[...]
     _, quads, ny, nz = u1.shape
-    parts = out.shape[0]
+    parts = len(outs)
     rows = ny // parts
     edge = SIDE // 2
     tall_rows = rows + 2 * edge
@@ -464,14 +485,18 @@
                 skip = low - (y * rows - edge)
                 end = skip + high - low
                 if skip:
-                    out[y, at : at + skip, :] = jnp.zeros((skip, nz), F32)
-                out[y, at + skip : at + end, :] = u1[c, q, low:high, :]
+                    blocks[y, at : at + skip, :] = jnp.zeros((skip, nz), F32)
+                blocks[y, at + skip : at + end, :] = u1[c, q, low:high, :]
                 if end < tall_rows:
-                    out[y, at + end : at + tall_rows, :] = jnp.zeros((tall_rows - end, nz), F32)
-        out[y, 2 * quads * tall_rows :, :] = up_gy[jnp.where(me < y, 1, 0)]
-
-
-def last_kernel(back, own, edges, g, bx, by, bz, wr, wi, out, ua, ub, tall):
+                    blocks[y, at + end : at + tall_rows, :] = jnp.zeros((tall_rows - end, nz), F32)
+    used = 2 * quads * tall_rows
+    for v, out in enumerate(outs):
+        out[:used, :] = blocks[me ^ v]
+        out[used:, :] = up_gy[jnp.where(me < (me ^ v), 1, 0)]
+
+
+def last_kernel(*refs):
+    *back, own, edges, g, bx, by, bz, wr, wi, out, ua, ub, tall, flat = refs
     k = lax.axis_index("gz")
     y = lax.axis_index("gy")
     m2, pad, ny, nz = ua.shape
@@ -481,23 +506,24 @@
     quads = pad // 2
     lanes = nz // 2
     ua[:, pl.ds(1, pad - 2)] = own[...]
-    parts = back.shape[0]
     blank = jnp.zeros((m2, ny, nz), F32)
     for p, side in ((0, 1), (pad - 1, 0)):
         ua[:, p] = blank
         ua[:, p, SIDE : SIDE + rows, :] = edges[side]
     used = 2 * quads * ny // 2
+    for v, ref in enumerate(back):
+        flat[y ^ v] = ref[...]
     for high in range(2):
-        there = jnp.where(y < parts - 1, 1.0, 0.0) if high else jnp.where(y > 0, 1.0, 0.0)
-        peer = jnp.minimum(y + 1, parts - 1) if high else jnp.maximum(y - 1, 0)
+        there = jnp.where(y < m - 1, 1.0, 0.0) if high else jnp.where(y > 0, 1.0, 0.0)
+        peer = jnp.minimum(y + 1, m - 1) if high else jnp.maximum(y - 1, 0)
         row = SIDE + rows + 1 if high else SIDE - 2
-        block = back[peer, used:, :] * there
+        block = flat[peer, used:, :] * there
         for z in range(2):
             for f in range(m2):
                 for i in range(half):
                     at = z * m2 * half + f * half + i
                     ua[f, HALO + i, row : row + 1, z * lanes : (z + 1) * lanes] = block[at : at + 1, :]
-    u1 = back[:, :used, :].reshape(m * used, lanes)
+    u1 = flat[:, :used, :].reshape(m * used, lanes)
     for h in range(2):
         col = lax.broadcasted_iota(jnp.int32, (lanes, lanes), 1) + h * lanes
         line = lax.broadcasted_iota(jnp.int32, (lanes, lanes), 0)
@@ -573,29 +599,29 @@
     away, kept = call(send_kernel, [own_half, own_half], placed, space=pltpu.HBM, sems=10)
     came = lax.ppermute(away, "gz", swap)
     rim = ((2 * m + 3) * HALO + 1) * half
-    rim = (m, 2, -(-rim // 8) * 8, lanes)
-    ends_y = call(rows_kernel, rim, (kept, came), scratch=[(2,) + rim[1:]])
-    ends_y = lax.all_to_all(ends_y, "gy", 0, 0, tiled=True)
+    rim = (2, -(-rim // 8) * 8, lanes)
+    to_even, to_odd = call(rows_kernel, [rim, rim], (kept, came), scratch=[(2,) + rim])
+    even = lax.ppermute(to_even, "gy", [(i, i ^ 1) for i in range(m)])
+    odd = lax.ppermute(to_odd, "gy", [(i, (i + 2 * (i % 2) - 1) % m) for i in range(m)])
 
     plane = (rows + 2 * SIDE, nz)
     laid = [(2 * m, pad) + plane, (pad + 2,) + plane, (pad,) + plane, (pad,) + plane]
     edges = (HALO * (2 * m + 2) + HALO + 1,) + plane
-    *state, to_gz, to_gx = call(lay_kernel, laid + [edges, edges], (kept, came, ends_y))
+    *state, to_gz, to_gx = call(lay_kernel, laid + [edges, edges], (kept, came, even, odd), scratch=[(2,) + rim])
     from_gx = lax.ppermute(to_gx, ("gx", "gz"), ends)
     from_gz = lax.ppermute(to_gz, "gz", swap)
 
     pairs = half // 2
     brow = (rows, nz)
     tall0 = (2 * m + 3) * pairs * plane[0]
-    g, _, _, _, bx, by, bz, wr, wi, own, up_gz, up_gx, up_gy, packed = call(
+    full = laid + [(pad + 1,) + plane] + [(pad,) + plane] * 5 + [(2 * m, pad) + plane, (2 * m, pad - 2) + plane]
+    state = call(near_kernel, full, (from_gz, *state), aliases={i + 1: i for i in range(len(laid))}, cost=NEAR_COST)
+    g, _, _, _, bx, by, bz, wr, wi, _, _, own, up_gz, up_gx, up_gy, packed = call(
         fine_kernel,
-        laid
-        + [(pad + 1,) + plane]
-        + [(pad,) + plane] * 4
-        + [(2 * m, pad - 2) + plane, (2 * m,) + brow, (2 * m,) + brow, (2, 4 * m * half, lanes), (chips * m, 5, pairs, rows // 2, lanes)],
-        (from_gz, from_gx, *state),
-        scratch=[(pad,) + plane, (2 * m, pad) + plane, (tall0, lanes), (tall0, lanes), (tall0 // 2, lanes)],
-        aliases={i + 2: i for i in range(len(laid))},
+        full + [(2 * m,) + brow, (2 * m,) + brow, (2, 4 * m * half, lanes), (chips * m, 5, pairs, rows // 2, lanes)],
+        (from_gx, *state),
+        scratch=[(tall0, lanes), (tall0, lanes), (tall0 // 2, lanes)],
+        aliases={i + 1: i for i in range(len(full))},
     )
     u_gx = lax.ppermute(up_gx, ("gx", "gz"), ends)
     u_gz = lax.ppermute(up_gz, "gz", swap)
@@ -617,13 +643,14 @@
         limit=14,
         cost=COARSE_COST,
     )
-    packed, halo = call(pack_kernel, [(m, used + 4 * m * half, lanes), (2, 2 * m) + brow], (u1, up_gy, u_gz, u_gx))
-    back = lax.all_to_all(packed, "gy", 0, 0, tiled=True)
+    block = (used + 4 * m * half, lanes)
+    *blocks, halo = call(pack_kernel, [block] * m + [(2, 2 * m) + brow], (u1, up_gy, u_gz, u_gx), scratch=[(m, used, lanes)])
+    back = [lax.ppermute(b, "gy", [(i, i ^ v) for i in range(m)]) if v else b for v, b in enumerate(blocks)]
     result = call(
         last_kernel,
         (2, 2, m, half, rows, lanes),
-        (back, own, halo, g, bx, by, bz, wr, wi),
-        scratch=[(2 * m, pad) + plane, (2 * m, pad) + plane, (2 * m * used, lanes)],
+        (*back, own, halo, g, bx, by, bz, wr, wi),
+        scratch=[(2 * m, pad) + plane, (2 * m, pad) + plane, (2 * m * used, lanes), (m,) + block],
     )
     last = lax.ppermute(result[1], "gz", swap)
     return call(gather_kernel, rhs.shape, (result[0], last))
@@ -634,7 +661,7 @@
 
     def local(rhs, density, shift_real, shift_imag):
         _, m, xs, rows, lanes = rhs.shape
-        planes = sizes["gz"] == 2 and sizes["gy"] == m and xs == 8 and rows % 16 == 0 and lanes == 128
+        planes = sizes["gz"] == 2 and sizes["gy"] == m == 4 and xs == 8 and rows % 16 == 0 and lanes == 128
         return (local_planes if planes else local_general)(rhs, density, shift_real, shift_imag)
 
     placed = (

time: 77.5 us -> 71 us (0.916)
  blocking collectives: 54.8 us -> 31.4 us
  waiting for transfers between devices: 4.81 us -> 14 us
  starting transfers between devices: 2.72 us -> 10.5 us
    all_to_all x2 -> x0, blocking collectives: 22.3 us -> none  [the longest x1 12.3 us: local_planes(): ends_y = lax.all_to_all(ends_y, 'gy', 0, 0, tiled=True)]
    ppermute x0 -> x5, waiting for transfers between devices: none -> 9 us  [the longest x3 4.08 us: local_planes(): lax.ppermute(b, 'gy', [(i, i ^ v) for i in range(m)])]
    ppermute x0 -> x5, starting transfers between devices: none -> 7.97 us  [the longest x3 3.55 us: local_planes(): lax.ppermute(b, 'gy', [(i, i ^ v) for i in range(m)])]
    all_to_all x1, blocking collectives: 32.5 us -> 31.4 us  [local_planes(): mine = lax.all_to_all(packed, ('gx', 'gy'), 0, 0, tiled=True)]
    pallas_call x8 -> x9, Pallas kernels: 14.8 us -> 14.8 us  [call(): pl.pallas_call(kernel, out_shape=[jax.ShapeDtypeStruct(s, F32) for s in s...]
  transfers between devices with their start and end apart: 7 -> 12, of which waited for: 4 -> 8; matrix products, arithmetic and copies ran while one was open for 0% -> 0% of each run, Pallas kernels for 7% -> 10%
where the time goes in v4:
time: 71 us; the launch traced here: 70.8 us
  blocking collectives  31.4 us (44%)
  Pallas kernels  14.8 us (21%)
  waiting for transfers between devices  14 us (20%)
  starting transfers between devices  10.5 us (15%)
    all_to_all x1, blocking collectives, local_planes(): mine = lax.all_to_all(packed, ('gx', 'gy'), 0, 0, tiled=True)  31.4 us
    pallas_call x9, Pallas kernels, call(): pl.pallas_call(kernel, out_shape=[jax.ShapeDtypeStruct(s, F32) for s in s...  14.8 us
    ppermute x3, waiting for transfers between devices, local_planes(): lax.ppermute(b, 'gy', [(i, i ^ v) for i in range(m)])  4.08 us
    ppermute x3, starting transfers between devices, local_planes(): lax.ppermute(b, 'gy', [(i, i ^ v) for i in range(m)])  3.55 us
    ppermute x1, waiting for transfers between devices, local_planes(): lax.ppermute(to_odd, 'gy', [(i, (i + 2 * (i % 2) - 1) % m) for i in range...  3.25 us
    ppermute x1, starting transfers between devices, local_planes(): even = lax.ppermute(to_even, 'gy', [(i, i ^ 1) for i in range(m)])  2.92 us
    ppermute x1, waiting for transfers between devices, local_planes(): even = lax.ppermute(to_even, 'gy', [(i, i ^ 1) for i in range(m)])  1.66 us
    ppermute x1, starting transfers between devices, local_planes(): lax.ppermute(to_odd, 'gy', [(i, (i + 2 * (i % 2) - 1) % m) for i in range...  1.49 us
  transfers between devices with their start and end apart: 12, of which 8 were waited for; matrix products, arithmetic and copies ran while one was open for 0% of the time, Pallas kernels for 10%

profile of v4, /device:TPU:0, one launch (start us, length us, event | category | flops | bytes accessed | tf_op | source)
XLA Modules:
  0.0 70.8 jit_solution(907591258458054625)
XLA Ops:
  0.0 1.2 %shard_map.46 = (f32[11,4,16,128]{3,2,1,0:T(8,128)S(1)}, f32[11,4,16,128]{3,2,1,0:T(8,128)S(1)}) custom-call(f32[2,4,8,16,128]{4,3,2,1,0:T(8,128)} %rhs.1, f32[8,16,128]{2,1,0:T(8,128)} %rho.1, f32[8,16,128]{2,1,0:T(8,128)} %sr.1, f32[8,16,128]{2,1,0:T(8,128)} %si.1), custom_call_target="tpu_custom_call" | custom-call | tf_op jit(solution)/shard_map/pallas_call | solution.py:574
  1.2 0.5 collective-permute-start
  1.8 1.3 %collective-permute-done.came = f32[11,4,16,128]{3,2,1,0:T(8,128)S(1)} collective-permute-done((f32[11,4,16,128]{3,2,1,0:T(8,128)S(1)}, f32[11,4,16,128]{3,2,1,0:T(8,128)S(1)}, u32[]{:S(2)}, u32[]{:S(2)}) %collective-permute-start) | collective-permute-done | bytes 360480 | tf_op jit(solution)/shard_map/ppermute | solution.py:600
  3.1 2.9 %collective-permute-start.1 = (f32[2,96,128]{2,1,0:T(8,128)S(1)}, f32[2,96,128]{2,1,0:T(8,128)S(1)}, u32[]{:S(2)}, u32[]{:S(2)}) collective-permute-start(f32[2,96,128]{2,1,0:T(8,128)S(1)} %get-tuple-element.45), channel_id=1, source_target_pairs={{0,2},{2,0},{4,6},{6,4},{1,3},{3,1},{5,7},{7,5},{8,10},{10,8},{12,... | collective-permute-start | bytes 294920 | tf_op jit(solution)/shard_map/ppermute | solution.py:604
  6.1 1.5 %collective-permute-start.2 = (f32[2,96,128]{2,1,0:T(8,128)S(1)}, f32[2,96,128]{2,1,0:T(8,128)S(1)}, u32[]{:S(2)}, u32[]{:S(2)}) collective-permute-start(f32[2,96,128]{2,1,0:T(8,128)S(1)} %get-tuple-element.46), channel_id=1, source_target_pairs={{0,6},{2,4},{4,2},{6,0},{1,7},{3,5},{5,3},{7,1},{8,14},{10,12},{12... | collective-permute-start | bytes 294920 | tf_op jit(solution)/shard_map/ppermute | solution.py:605
  7.6 1.7 %collective-permute-done.1.even = f32[2,96,128]{2,1,0:T(8,128)S(1)} collective-permute-done((f32[2,96,128]{2,1,0:T(8,128)S(1)}, f32[2,96,128]{2,1,0:T(8,128)S(1)}, u32[]{:S(2)}, u32[]{:S(2)}) %collective-permute-start.1) | collective-permute-done | bytes 98336 | tf_op jit(solution)/shard_map/ppermute | solution.py:604
  9.2 3.3 %collective-permute-done.2.odd = f32[2,96,128]{2,1,0:T(8,128)S(1)} collective-permute-done((f32[2,96,128]{2,1,0:T(8,128)S(1)}, f32[2,96,128]{2,1,0:T(8,128)S(1)}, u32[]{:S(2)}, u32[]{:S(2)}) %collective-permute-start.2) | collective-permute-done | bytes 98336 | tf_op jit(solution)/shard_map/ppermute | solution.py:605
  12.9 0.7 collective-permute-start.3
  13.6 1.3 %collective-permute-done.4.from_gz = f32[23,24,256]{2,1,0:T(8,128)S(1)} collective-permute-done((f32[23,24,256]{2,1,0:T(8,128)S(1)}, f32[23,24,256]{2,1,0:T(8,128)S(1)}, u32[]{:S(2)}, u32[]{:S(2)}) %collective-permute-start.4) | collective-permute-done | bytes 565280 | tf_op jit(solution)/shard_map/ppermute | solution.py:612
  14.8 1.7 %shard_map.49 = (f32[8,8,24,256]{3,2,1,0:T(8,128)S(1)}, f32[10,24,256]{2,1,0:T(8,128)S(1)}, f32[8,24,256]{2,1,0:T(8,128)S(1)}, f32[8,24,256]{2,1,0:T(8,128)S(1)}...) custom-call(f32[23,24,256]{2,1,0:T(8,128)S(1)} %collective-permute-d, ...), custom_call_target="tpu_custom_call", output_to_operand_aliasing={{0}: (1, {}), {1}: (2, {}), {2}: (3, {}), {3}: (4, {})} | custom-call | flops 2000000000 | tf_op jit(solution)/shard_map/pallas_call | solution.py:574
  16.5 2.5 %shard_map.50 = (f32[8,8,24,256]{3,2,1,0:T(8,128)S(1)}, f32[10,24,256]{2,1,0:T(8,128)S(1)}, f32[8,24,256]{2,1,0:T(8,128)S(1)}, f32[8,24,256]{2,1,0:T(8,128)S(1)}...) custom-call(f32[23,24,256]{2,1,0:T(8,128)S(1)} %collective-permute-d, ...), custom_call_target="tpu_custom_call", output_to_operand_aliasing={{0}: (1, {}), {1}: (2, {}), {2}: (3, {}), {3}: (4, {}), {4}... | custom-call | tf_op jit(solution)/shard_map/pallas_call | solution.py:574
  19.1 31.4 %all_to_all.5.mine = f32[16,5,2,8,128]{4,3,2,1,0:T(8,128)S(1)} all-to-all(f32[16,5,2,8,128]{4,3,2,1,0:T(8,128)S(1)} %get-tuple-element.65), channel_id=1, replica_groups=mesh['gx'=4,'gy'=4,'gz'=2] {'gx','gy'}, dimensions={0} | all-to-all | bytes 1310720 | tf_op jit(solution)/shard_map/all_to_all | solution.py:628
  50.4 0.5 collective-permute-start.6
  50.9 0.7 collective-permute-start.7
  51.6 0.9 %collective-permute-done.5.other = f32[16,5,2,8,128]{4,3,2,1,0:T(8,128)S(1)} collective-permute-done((f32[16,5,2,8,128]{4,3,2,1,0:T(8,128)S(1)}, f32[16,5,2,8,128]{4,3,2,1,0:T(8,128)S(1)}, u32[]{:S(2)}, u32[]{:S(2)}) %collective-permute-start.5) | collective-permute-done | bytes 655392 | tf_op jit(solution)/shard_map/ppermute | solution.py:629
  52.5 5.2 %shard_map.51.u1 = f32[2,4,32,128]{3,2,1,0:T(8,128)S(1)} custom-call(f32[16,5,2,8,128]{4,3,2,1,0:T(8,128)S(1)} %all_to_all.5.mine, f32[16,5,2,8,128]{4,3,2,1,0:T(8,128)S(1)} %collective-permute-done.5.other), custom_call_target="tpu_custom_call" | custom-call | flops 5000000000 | tf_op jit(solution)/shard_map/pallas_call | solution.py:574
  57.8 0.6 collective-permute-start.8
  58.5 0.7 collective-permute-start.9
  59.1 2.3 %collective-permute-start.10 = (f32[160,128]{1,0:T(8,128)S(1)}, f32[160,128]{1,0:T(8,128)S(1)}, u32[]{:S(2)}, u32[]{:S(2)}) collective-permute-start(f32[160,128]{1,0:T(8,128)S(1)} %get-tuple-element.72), channel_id=1, source_target_pairs={{0,6},{2,4},{4,2},{6,0},{1,7},{3,5},{5,3},{7,1},{8,14},{10,12},{12... | collective-permute-start | bytes 245768 | tf_op jit(solution)/shard_map/ppermute | solution.py:648
  61.4 1.6 %collective-permute-done.8.refs_1_ = f32[160,128]{1,0:T(8,128)S(1)} collective-permute-done((f32[160,128]{1,0:T(8,128)S(1)}, f32[160,128]{1,0:T(8,128)S(1)}, u32[]{:S(2)}, u32[]{:S(2)}) %collective-permute-start.8) | collective-permute-done | bytes 81952 | tf_op jit(solution)/shard_map/ppermute | solution.py:648
  63.0 2.5 %collective-permute-done.9.refs_2_ = f32[160,128]{1,0:T(8,128)S(1)} collective-permute-done((f32[160,128]{1,0:T(8,128)S(1)}, f32[160,128]{1,0:T(8,128)S(1)}, u32[]{:S(2)}, u32[]{:S(2)}) %collective-permute-start.9) | collective-permute-done | bytes 81952 | tf_op jit(solution)/shard_map/ppermute | solution.py:648
  65.5 2.8 %shard_map.53 = f32[2,2,4,4,16,128]{5,4,3,2,1,0:T(8,128)S(1)} custom-call(f32[160,128]{1,0:T(8,128)S(1)} %get-tuple-element.69.refs_0_, f32[160,128]{1,0:T(8,128)S(1)} %collective-permute-done.8.refs_1_, f32[160,128]{1,0:T(8,128)S(1)} %collective-permute-done.9.refs_2_, f32[160,128]{1,0:T(8,128)S(1)} %collective-permute-done.10.refs_3_, ...), custom_call_target="tpu_custom_call" | custom-call | tf_op jit(solution)/shard_map/pallas_call | solution.py:574
  68.5 1.5 %collective-permute-done.11.came = f32[2,4,4,16,128]{4,3,2,1,0:T(8,128)S(1)} collective-permute-done((f32[2,4,4,16,128]{4,3,2,1,0:T(8,128)S(1)}, f32[2,4,4,16,128]{4,3,2,1,0:T(8,128)S(1)}, u32[]{:S(2)}, u32[]{:S(2)}) %collective-permute-start.11) | collective-permute-done | bytes 262176 | tf_op jit(solution)/shard_map/ppermute | solution.py:655
  70.0 0.8 %shard_map.54 = f32[2,4,8,16,128]{4,3,2,1,0:T(8,128)} custom-call(f32[2,4,4,16,128]{4,3,2,1,0:T(8,128)S(1)} %get-tuple-element.82.kept, f32[2,4,4,16,128]{4,3,2,1,0:T(8,128)S(1)} %collective-permute-done.11.came), custom_call_target="tpu_custom_call" | custom-call | tf_op jit(solution)/shard_map/pallas_call | solution.py:574
  (11 shorter events, 0.7 us)
Async XLA Ops:
  1.2 1.8 %collective-permute-start = (f32[11,4,16,128]{3,2,1,0:T(8,128)S(1)}, f32[11,4,16,128]{3,2,1,0:T(8,128)S(1)}, u32[]{:S(2)}, u32[]{:S(2)}) collective-permute-start(f32[11,4,16,128]{3,2,1,0:T(8,128)S(1)} %get-tuple-element.44), channel_id=1, source_target_pairs={{0,1},{1,0},{2,3},{3,2},{4,5},{5,4},{6,7},{7,6},{8,9},{9,8},{10,11... | collective-permute-start | bytes 1081352 | tf_op jit(solution)/shard_map/ppermute | solution.py:600
  3.1 6.1 %collective-permute-start.1 = (f32[2,96,128]{2,1,0:T(8,128)S(1)}, f32[2,96,128]{2,1,0:T(8,128)S(1)}, u32[]{:S(2)}, u32[]{:S(2)}) collective-permute-start(f32[2,96,128]{2,1,0:T(8,128)S(1)} %get-tuple-element.45), channel_id=1, source_target_pairs={{0,2},{2,0},{4,6},{6,4},{1,3},{3,1},{5,7},{7,5},{8,10},{10,8},{12,... | collective-permute-start | bytes 294920 | tf_op jit(solution)/shard_map/ppermute | solution.py:604
  6.1 6.4 %collective-permute-start.2 = (f32[2,96,128]{2,1,0:T(8,128)S(1)}, f32[2,96,128]{2,1,0:T(8,128)S(1)}, u32[]{:S(2)}, u32[]{:S(2)}) collective-permute-start(f32[2,96,128]{2,1,0:T(8,128)S(1)} %get-tuple-element.46), channel_id=1, source_target_pairs={{0,6},{2,4},{4,2},{6,0},{1,7},{3,5},{5,3},{7,1},{8,14},{10,12},{12... | collective-permute-start | bytes 294920 | tf_op jit(solution)/shard_map/ppermute | solution.py:605
  12.8 2.0 %collective-permute-start.4 = (f32[23,24,256]{2,1,0:T(8,128)S(1)}, f32[23,24,256]{2,1,0:T(8,128)S(1)}, u32[]{:S(2)}, u32[]{:S(2)}) collective-permute-start(f32[23,24,256]{2,1,0:T(8,128)S(1)} %get-tuple-element.48), channel_id=1, source_target_pairs={{0,1},{1,0},{2,3},{3,2},{4,5},{5,4},{6,7},{7,6},{8,9},{9,8},{10,11... | collective-permute-start | bytes 1695752 | tf_op jit(solution)/shard_map/ppermute | solution.py:612
  12.9 3.7 %collective-permute-start.3 = (f32[23,24,256]{2,1,0:T(8,128)S(1)}, f32[23,24,256]{2,1,0:T(8,128)S(1)}, u32[]{:S(2)}, u32[]{:S(2)}) collective-permute-start(f32[23,24,256]{2,1,0:T(8,128)S(1)} %get-tuple-element.47), channel_id=1, source_target_pairs={{1,8},{8,1},{9,16},{16,9},{17,24},{24,17},{3,10},{10,3},{11,18},{1... | collective-permute-start | bytes 1695752 | tf_op jit(solution)/shard_map/ppermute | solution.py:611
  50.4 2.1 %collective-permute-start.5 = (f32[16,5,2,8,128]{4,3,2,1,0:T(8,128)S(1)}, f32[16,5,2,8,128]{4,3,2,1,0:T(8,128)S(1)}, u32[]{:S(2)}, u32[]{:S(2)}) collective-permute-start(f32[16,5,2,8,128]{4,3,2,1,0:T(8,128)S(1)} %all_to_all.5.mine), channel_id=1, source_target_pairs={{0,1},{1,0},{2,3},{3,2},{4,5},{5,4},{6,7},{7,6},{8,9},{9,8},{10,11... | collective-permute-start | bytes 1966088 | tf_op jit(solution)/shard_map/ppermute | solution.py:629
  50.4 7.3 %collective-permute-start.6 = (f32[8,16,256]{2,1,0:T(8,128)S(1)}, f32[8,16,256]{2,1,0:T(8,128)S(1)}, u32[]{:S(2)}, u32[]{:S(2)}) collective-permute-start(f32[8,16,256]{2,1,0:T(8,128)S(1)} %get-tuple-element.67), channel_id=1, source_target_pairs={{0,1},{1,0},{2,3},{3,2},{4,5},{5,4},{6,7},{7,6},{8,9},{9,8},{10,11... | collective-permute-start | bytes 393224 | tf_op jit(solution)/shard_map/ppermute | solution.py:627
  50.9 6.8 %collective-permute-start.7 = (f32[8,16,256]{2,1,0:T(8,128)S(1)}, f32[8,16,256]{2,1,0:T(8,128)S(1)}, u32[]{:S(2)}, u32[]{:S(2)}) collective-permute-start(f32[8,16,256]{2,1,0:T(8,128)S(1)} %get-tuple-element.68), channel_id=1, source_target_pairs={{1,8},{8,1},{9,16},{16,9},{17,24},{24,17},{3,10},{10,3},{11,18},{1... | collective-permute-start | bytes 393224 | tf_op jit(solution)/shard_map/ppermute | solution.py:626
  57.8 5.2 %collective-permute-start.8 = (f32[160,128]{1,0:T(8,128)S(1)}, f32[160,128]{1,0:T(8,128)S(1)}, u32[]{:S(2)}, u32[]{:S(2)}) collective-permute-start(f32[160,128]{1,0:T(8,128)S(1)} %get-tuple-element.70), channel_id=1, source_target_pairs={{0,2},{2,0},{4,6},{6,4},{1,3},{3,1},{5,7},{7,5},{8,10},{10,8},{12,... | collective-permute-start | bytes 245768 | tf_op jit(solution)/shard_map/ppermute | solution.py:648
  58.5 7.0 %collective-permute-start.9 = (f32[160,128]{1,0:T(8,128)S(1)}, f32[160,128]{1,0:T(8,128)S(1)}, u32[]{:S(2)}, u32[]{:S(2)}) collective-permute-start(f32[160,128]{1,0:T(8,128)S(1)} %get-tuple-element.71), channel_id=1, source_target_pairs={{0,4},{2,6},{4,0},{6,2},{1,5},{3,7},{5,1},{7,3},{8,12},{10,14},{12... | collective-permute-start | bytes 245768 | tf_op jit(solution)/shard_map/ppermute | solution.py:648
  59.1 6.4 %collective-permute-start.10 = (f32[160,128]{1,0:T(8,128)S(1)}, f32[160,128]{1,0:T(8,128)S(1)}, u32[]{:S(2)}, u32[]{:S(2)}) collective-permute-start(f32[160,128]{1,0:T(8,128)S(1)} %get-tuple-element.72), channel_id=1, source_target_pairs={{0,6},{2,4},{4,2},{6,0},{1,7},{3,5},{5,3},{7,1},{8,14},{10,12},{12... | collective-permute-start | bytes 245768 | tf_op jit(solution)/shard_map/ppermute | solution.py:648
  68.4 1.6 %collective-permute-start.11 = (f32[2,4,4,16,128]{4,3,2,1,0:T(8,128)S(1)}, f32[2,4,4,16,128]{4,3,2,1,0:T(8,128)S(1)}, u32[]{:S(2)}, u32[]{:S(2)}) collective-permute-start(f32[2,4,4,16,128]{4,3,2,1,0:T(8,128)S(1)} %get-tuple-element.81), channel_id=1, source_target_pairs={{0,1},{1,0},{2,3},{3,2},{4,5},{5,4},{6,7},{7,6},{8,9},{9,8},{10,11... | collective-permute-start | bytes 786440 | tf_op jit(solution)/shard_map/ppermute | solution.py:655

commit v5 on v4

--- a/solution.py
+++ b/solution.py
@@ -1,3 +1,5 @@
+import functools
+
 import jax
 import jax.numpy as jnp
 from jax import lax
@@ -245,7 +247,31 @@
     to_odd[...] = ends[even]
 
 
-def lay_kernel(kept, came, even, odd, g, rho, sr, si, to_gz, to_gx, ends):
+def means_kernel(kept, came, out, slots, sums):
+    k = lax.axis_index("gz")
+    fields, half, rows, lanes = kept.shape
+    pairs = half // 2
+    for t, ref in enumerate((kept, came)):
+        for j in range(3):
+            for q in range(pairs):
+                at = (j * pairs + q) * rows
+                slots[at : at + rows, :] = ref[fields - 3 + j, 2 * q] + ref[fields - 3 + j, 2 * q + 1]
+        n = 3 * pairs * rows // 2
+        sums[t] = slots[pl.ds(0, n, 2), :] + slots[pl.ds(1, n, 2), :]
+    done = dot(jnp.concatenate([sums[k], sums[1 - k]], axis=1), pick(2 * lanes, lanes, True, 0.125))
+    out[...] = done.reshape(3, pairs, rows // 2, lanes)
+
+
+def join(axis, parts, out):
+    me = lax.axis_index(axis)
+    n = out.shape[0] // len(parts)
+    for v, ref in enumerate(parts):
+        out[pl.ds((me ^ v) * n, n)] = ref[...].reshape((n,) + out.shape[1:])
+
+
+def lay_kernel(kept, came, even, odd, *refs):
+    *means, g, rho, sr, si, to_gz, to_gx, joined, ends = refs
+    join("gx", means, joined)
     k = lax.axis_index("gz")
     y = lax.axis_index("gy")
     fields, half, rows, lanes = kept.shape
@@ -311,12 +337,15 @@
     loop(done, second)
 
 
-def near_kernel(from_gz, _g, _rho, _sr, _si, *state):
+def near_kernel(from_gz, _g, _rho, _sr, _si, *refs):
+    means, *state, out = refs
+    out[...] = means[...]
     side_planes(from_gz, 1 - lax.axis_index("gz"), *state, False)
 
 
 def fine_kernel(from_gx, *refs):
-    g, rho, sr, si, bx, by, bz, wr, wi, dr, ua, own, up_gz, up_gx, up_gy, packed, left, right, narrow = refs[12:]
+    g, rho, sr, si, bx, by, bz, wr, wi, dr, ua, own, up_gz, up_gx, up_gy, packed, joined, left, right, narrow = refs[-20:]
+    join("gy", refs[12:-20], joined)
     k = lax.axis_index("gz")
     side_planes(from_gx, k, g, rho, sr, si, bx, by, bz, wr, wi, dr, ua, own, True)
     coefs = (bx, by, bz, wr, wi)
@@ -342,61 +371,86 @@
             ar, ai = resid_planes(own, (r, m + r), p - 1, g, p, p, 1, coefs, dr, si)
             br, bi = resid_planes(own, (r, m + r), p, g, p + 1, p + 1, 1, coefs, dr, si)
             totals[r], totals[m + r] = ar + br, ai + bi
-        totals[m2] = rho[pl.ds(p + 1, 1)] + rho[pl.ds(p + 2, 1)]
-        for j, ref in ((m2 + 1, sr), (m2 + 2, si)):
-            totals[j] = ref[pl.ds(p, 1)] + ref[pl.ds(p + 1, 1)]
         for j, v in totals.items():
             spot = pl.ds(pl.multiple_of((j * pairs + q) * ny, ny), ny)
             left[spot, :] = v[0, :, :lanes]
             right[spot, :] = v[0, :, lanes:]
 
     loop(pairs, down)
-    n = (m2 + 3) * pairs * ny // 2
+    n = m2 * pairs * ny // 2
     both = [ref[pl.ds(0, n, 2), :] + ref[pl.ds(1, n, 2), :] for ref in (left, right)]
     narrow[...] = dot(jnp.concatenate(both, axis=1), pick(nz, lanes, True, 0.125))
     for q in range(pairs):
         done = []
-        for j in range(m2 + 3):
+        for j in range(m2):
             at = (j * pairs + q) * (ny // 2) + SIDE // 2
             done.append(narrow[at : at + rows // 2, :])
         for d in range(packed.shape[0]):
-            r = d % m
-            for a, j in enumerate((r, m + r, m2, m2 + 1, m2 + 2)):
-                packed[d, a, q] = done[j]
-
-
-def coarse_kernel(
-    mine, other, out,
-    rho1, sr1, si1, g1, bx1, by1, bz1, wr1, wi1, dr1, ua1, ub1,
-    rho2, sr2, si2, g2, bx2, by2, bz2, wr2, wi2, dr2, ua2, ub2,
-    sums, narrow, wide, tall,
-):
-    k = lax.axis_index("gz")
-    chip = lax.axis_index("gx")
-    _, _, pairs, rows, nz = mine.shape
-    n1, ny = sr1.shape[:2]
-    parts = ny // rows
-    chips = mine.shape[0] // parts
+            for c in range(2):
+                packed[d, c, q] = done[c * m + d % m]
+
+
+def merge_kernel(chips, fields, means, out):
+    parts = fields.shape[0] // chips
+    for e in range(fields.shape[0]):
+        x, y = divmod(e, parts)
+        out[e, :2] = fields[e]
+        out[e, 2:] = means[y * chips + x]
+
+
+def put_coarse(mine, other, refs, offsets, parts, skip):
+    k = lax.axis_index("gz")
+    _, _, pairs, rows, _ = mine.shape
+    for e in range(mine.shape[0]):
+        s, y = divmod(e, parts)
+        for came, z in ((mine, k), (other, 1 - k)):
+            for j, ref in enumerate(refs):
+                ref[pl.ds(2 * pairs * s + pairs * z + offsets[j], pairs), y * rows : (y + 1) * rows] = came[e, skip + j]
+
+
+def halve(sums, narrow, ny, count, total, values):
+    nz = sums.shape[1]
+
+    def body(q):
+        for j, v in enumerate(values(q)):
+            sums[pl.ds(pl.multiple_of((j * total + q) * ny, ny), ny), :] = v
+
+    loop(total, body)
+    n = count * total * ny // 2
+    narrow[pl.ds(0, n), :] = dot(sums[pl.ds(0, n, 2), :] + sums[pl.ds(1, n, 2), :], pick(nz, nz, True, 0.125))
+
+
+def levels(mine, other, si1, bx1, by1, bz1, wr1, wi1, dr1, bx2, by2, bz2, wr2, wi2, rho1, sr1, rho2, sr2, si2, dr2, sums, narrow):
+    n1, ny, nz = si1.shape
     zero = jnp.zeros((1, ny, nz), F32)
     rho1[pl.ds(0, 1)] = zero
     rho1[pl.ds(n1 + 1, 1)] = zero
+    put_coarse(mine, other, (rho1, sr1, si1), (1, 0, 0), ny // mine.shape[3], 2)
+    level_coefs(rho1, sr1, si1, 0.25, bx1, by1, bz1, wr1, wi1, dr1, 4, 0, n1)
+    n2, ny2 = sr2.shape[:2]
+    halve(sums, narrow, ny, 3, n2, lambda q: (rho1[2 * q + 1] + rho1[2 * q + 2], sr1[2 * q] + sr1[2 * q + 1], si1[2 * q] + si1[2 * q + 1]))
+    zero2 = jnp.zeros((1, ny2, nz), F32)
+    rho2[pl.ds(0, 1)] = zero2
+    rho2[pl.ds(n2 + 1, 1)] = zero2
+    n = n2 * ny2
+    for j, ref in enumerate((rho2.at[pl.ds(1, n2)], sr2, si2)):
+        ref[...] = narrow[j * n : (j + 1) * n, :].reshape(n2, ny2, nz)
+    level_coefs(rho2, sr2, si2, 0.0625, bx2, by2, bz2, wr2, wi2, dr2, n2, 0, n2)
+
+
+def coarse_kernel(mine, other, out, si1, bx1, by1, bz1, wr1, wi1, dr1, bx2, by2, bz2, wr2, wi2, rho1, sr1, rho2, sr2, si2, dr2, sums, narrow, g1, ua1, ub1, g2, ua2, ub2, wide, tall):
+    levels(mine, other, si1, bx1, by1, bz1, wr1, wi1, dr1, bx2, by2, bz2, wr2, wi2, rho1, sr1, rho2, sr2, si2, dr2, sums, narrow)
+    k = lax.axis_index("gz")
+    chip = lax.axis_index("gx")
+    pairs = mine.shape[2]
+    n1, ny, nz = si1.shape
+    zero = jnp.zeros((1, ny, nz), F32)
     for u in (ua1, ub1):
         for c in range(2):
             u[c, pl.ds(0, 1)] = zero
             u[c, pl.ds(n1 + 1, 1)] = zero
-    for s in range(chips):
-        for ref, z in ((mine, k), (other, 1 - k)):
-            at = 2 * pairs * s + pairs * z
-            for y in range(parts):
-                spot = slice(y * rows, (y + 1) * rows)
-                e = s * parts + y
-                for c in range(2):
-                    g1[c, pl.ds(at, pairs), spot] = ref[e, c]
-                rho1[pl.ds(at + 1, pairs), spot] = ref[e, 2]
-                sr1[pl.ds(at, pairs), spot] = ref[e, 3]
-                si1[pl.ds(at, pairs), spot] = ref[e, 4]
+    put_coarse(mine, other, (g1.at[0], g1.at[1]), (0, 0), ny // mine.shape[3], 0)
     step1 = 4
-    level_coefs(rho1, sr1, si1, 0.25, bx1, by1, bz1, wr1, wi1, dr1, step1, 0, n1)
     coefs1 = (bx1, by1, bz1, wr1, wi1)
 
     def first(i):
@@ -415,30 +469,20 @@
         loop(n1 // step1, body)
 
     sweep1(ua1, ub1)
-    n2 = n1 // 2
-    ny2 = ny // 2
+    n2, ny2 = n1 // 2, ny // 2
 
     def down(q):
-        p = 2 * q
-        r, m = resid_planes(ub1, (0, 1), p + 1, g1, p, p, 2, coefs1, dr1, si1)
-        totals = (r[0] + r[1], m[0] + m[1], rho1[p + 1] + rho1[p + 2], sr1[p] + sr1[p + 1], si1[p] + si1[p + 1])
-        for j, v in enumerate(totals):
-            sums[pl.ds(pl.multiple_of((j * n2 + q) * ny, ny), ny), :] = v
-
-    loop(n2, down)
-    narrow[...] = dot(sums[...], pick(nz, nz, True, 0.125))
+        r, m = resid_planes(ub1, (0, 1), 2 * q + 1, g1, 2 * q, 2 * q, 2, coefs1, dr1, si1)
+        return r[0] + r[1], m[0] + m[1]
+
+    halve(sums, narrow, ny, 2, n2, down)
+    zero2 = jnp.zeros((1, ny2, nz), F32)
     n = n2 * ny2
-    zero2 = jnp.zeros((1, ny2, nz), F32)
-    rho2[pl.ds(0, 1)] = zero2
-    rho2[pl.ds(n2 + 1, 1)] = zero2
-    for u in (ua2, ub2):
-        for c in range(2):
+    for c in range(2):
+        g2[c] = narrow[c * n : (c + 1) * n, :].reshape(n2, ny2, nz)
+        for u in (ua2, ub2):
             u[c, pl.ds(0, 1)] = zero2
             u[c, pl.ds(n2 + 1, 1)] = zero2
-    for j, ref in enumerate((g2.at[0], g2.at[1], rho2.at[pl.ds(1, n2)], sr2, si2)):
-        at = 2 * n * j
-        ref[...] = (narrow[pl.ds(at, n, 2), :] + narrow[pl.ds(at + 1, n, 2), :]).reshape(n2, ny2, nz)
-    level_coefs(rho2, sr2, si2, 0.0625, bx2, by2, bz2, wr2, wi2, dr2, n2, 0, n2)
     coefs2 = (bx2, by2, bz2, wr2, wi2)
     ua2[0, pl.ds(1, n2)], ua2[1, pl.ds(1, n2)] = weigh(g2[0], g2[1], 0, n2, wr2, wi2)
     src, dst = ua2, ub2
@@ -462,7 +506,6 @@
     loop(n2, lift)
     sweep1(ub1, ua1)
     sweep1(ua1, ub1)
-
     out[...] = ub1[:, pl.ds((2 * chip + k) * pairs, 2 + pairs)]
 
 
@@ -598,6 +641,16 @@
     placed = tuple(pltpu.with_memory_space_constraint(f, pltpu.HBM) for f in fields)
     away, kept = call(send_kernel, [own_half, own_half], placed, space=pltpu.HBM, sems=10)
     came = lax.ppermute(away, "gz", swap)
+    pairs = half // 2
+    means = (3, pairs, rows // 2, lanes)
+    n = 3 * pairs * rows
+    coarse = call(means_kernel, means, (kept, came), scratch=[(n, lanes), (2, n // 2, lanes)])
+
+    def spread(array, axis, count):
+        return [lax.ppermute(array, axis, [(i, i ^ v) for i in range(count)]) if v else array for v in range(count)]
+
+    coarse = spread(coarse, "gx", chips)
+
     rim = ((2 * m + 3) * HALO + 1) * half
     rim = (2, -(-rim // 8) * 8, lanes)
     to_even, to_odd = call(rows_kernel, [rim, rim], (kept, came), scratch=[(2,) + rim])
@@ -607,42 +660,45 @@
     plane = (rows + 2 * SIDE, nz)
     laid = [(2 * m, pad) + plane, (pad + 2,) + plane, (pad,) + plane, (pad,) + plane]
     edges = (HALO * (2 * m + 2) + HALO + 1,) + plane
-    *state, to_gz, to_gx = call(lay_kernel, laid + [edges, edges], (kept, came, even, odd), scratch=[(2,) + rim])
+    *state, to_gz, to_gx, coarse = call(lay_kernel, laid + [edges, edges, (chips, *means)], (kept, came, even, odd, *coarse), scratch=[(2,) + rim])
     from_gx = lax.ppermute(to_gx, ("gx", "gz"), ends)
     from_gz = lax.ppermute(to_gz, "gz", swap)
 
-    pairs = half // 2
     brow = (rows, nz)
-    tall0 = (2 * m + 3) * pairs * plane[0]
+    tall0 = 2 * m * pairs * plane[0]
     full = laid + [(pad + 1,) + plane] + [(pad,) + plane] * 5 + [(2 * m, pad) + plane, (2 * m, pad - 2) + plane]
-    state = call(near_kernel, full, (from_gz, *state), aliases={i + 1: i for i in range(len(laid))}, cost=NEAR_COST)
-    g, _, _, _, bx, by, bz, wr, wi, _, _, own, up_gz, up_gx, up_gy, packed = call(
+    *state, coarse = call(near_kernel, full + [(chips, *means)], (from_gz, *state, coarse), aliases={i + 1: i for i in range(len(laid))}, cost=NEAR_COST)
+    coarse = spread(coarse, "gy", m)
+    g, _, _, _, bx, by, bz, wr, wi, _, _, own, up_gz, up_gx, up_gy, packed, coarse = call(
         fine_kernel,
-        full + [(2 * m,) + brow, (2 * m,) + brow, (2, 4 * m * half, lanes), (chips * m, 5, pairs, rows // 2, lanes)],
-        (from_gx, *state),
+        full + [(2 * m,) + brow, (2 * m,) + brow, (2, 4 * m * half, lanes), (chips * m, 2, pairs, rows // 2, lanes), (m * chips, *means)],
+        (from_gx, *state, *coarse),
         scratch=[(tall0, lanes), (tall0, lanes), (tall0 // 2, lanes)],
         aliases={i + 1: i for i in range(len(full))},
     )
     u_gx = lax.ppermute(up_gx, ("gx", "gz"), ends)
     u_gz = lax.ppermute(up_gz, "gz", swap)
     mine = lax.all_to_all(packed, ("gx", "gy"), 0, 0, tiled=True)
+    mine = call(functools.partial(merge_kernel, chips), (chips * m, 5) + packed.shape[2:], (mine, coarse))
     other = lax.ppermute(mine, "gz", swap)
 
     n1, n2 = chips * xs // 2, chips * xs // 4
     p1, p2 = (ny // 2, nz // 2), (ny // 4, nz // 2)
 
-    def level(n, p):
-        return [(n + 2,) + p, (n,) + p, (n,) + p, (2, n) + p, (n + 1,) + p] + [(n,) + p] * 5 + [(2, n + 2) + p] * 2
-
-    used = (2 + pairs) * plane[0]
     u1 = call(
         coarse_kernel,
         (2, 2 + pairs) + p1,
         (mine, other),
-        scratch=level(n1, p1) + level(n2, p2) + [(5 * n2 * p1[0], p1[1])] * 2 + [(2 * n2 * p2[0], p1[1]), (2 * n2 * p1[0], p1[1])],
-        limit=14,
+        scratch=[(n1,) + p1, (n1 + 1,) + p1]
+        + [(n1,) + p1] * 5
+        + [(n2 + 1,) + p2]
+        + [(n2,) + p2] * 4
+        + [(n1 + 2,) + p1, (n1,) + p1, (n2 + 2,) + p2, (n2,) + p2, (n2,) + p2, (n2,) + p2, (3 * n2 * p1[0], lanes), (3 * n2 * p2[0], lanes)]
+        + [(2, n1) + p1, (2, n1 + 2) + p1, (2, n1 + 2) + p1, (2, n2) + p2, (2, n2 + 2) + p2, (2, n2 + 2) + p2]
+        + [(2 * n2 * p2[0], lanes), (2 * n2 * p1[0], lanes)],
         cost=COARSE_COST,
     )
+    used = (2 + pairs) * plane[0]
     block = (used + 4 * m * half, lanes)
     *blocks, halo = call(pack_kernel, [block] * m + [(2, 2 * m) + brow], (u1, up_gy, u_gz, u_gx), scratch=[(m, used, lanes)])
     back = [lax.ppermute(b, "gy", [(i, i ^ v) for i in range(m)]) if v else b for v, b in enumerate(blocks)]
@@ -661,7 +717,7 @@
 
     def local(rhs, density, shift_real, shift_imag):
         _, m, xs, rows, lanes = rhs.shape
-        planes = sizes["gz"] == 2 and sizes["gy"] == m == 4 and xs == 8 and rows % 16 == 0 and lanes == 128
+        planes = sizes["gz"] == 2 and sizes["gy"] == m == 4 and sizes["gx"] in (2, 4, 8) and xs == 8 and rows % 16 == 0 and lanes == 128
         return (local_planes if planes else local_general)(rhs, density, shift_real, shift_imag)
 
     placed = (

time: 71 us -> 66.3 us (0.934)
  blocking collectives: 31.4 us -> 14.3 us
  starting transfers between devices: 10.5 us -> 18.7 us
  waiting for transfers between devices: 14 us -> 17.8 us
    all_to_all x1, blocking collectives: 31.4 us -> 14.3 us  [local_planes(): mine = lax.all_to_all(packed, ('gx', 'gy'), 0, 0, tiled=True)]
    ppermute x0 -> x6, waiting for transfers between devices: none -> 8.61 us  [spread(): lax.ppermute(array, axis, [(i, i ^ v) for i in range(count)])]
    ppermute x0 -> x6, starting transfers between devices: none -> 8.01 us  [spread(): lax.ppermute(array, axis, [(i, i ^ v) for i in range(count)])]
    ppermute x1, waiting for transfers between devices: 3.25 us -> 0.01 us  [local_planes(): lax.ppermute(to_odd, 'gy', [(i, (i + 2 * (i % 2) - 1) % m) for i in range...]
    ppermute x1, waiting for transfers between devices: 1.66 us -> 0.01 us  [local_planes(): even = lax.ppermute(to_even, 'gy', [(i, i ^ 1) for i in range(m)])]
    pallas_call x9 -> x11, Pallas kernels: 14.8 us -> 15.1 us  [call(): pl.pallas_call(kernel, out_shape=[jax.ShapeDtypeStruct(s, F32) for s in s...]
  transfers between devices with their start and end apart: 12 -> 18, of which waited for: 8 -> 10; matrix products, arithmetic and copies ran while one was open for 0% -> 0% of each run, Pallas kernels for 10% -> 11%
where the time goes in v5:
time: 66.3 us; the launch traced here: 66.1 us
  starting transfers between devices  18.7 us (28%)
  waiting for transfers between devices  17.8 us (27%)
  Pallas kernels  15.1 us (23%)
  blocking collectives  14.3 us (22%)
    pallas_call x11, Pallas kernels, call(): pl.pallas_call(kernel, out_shape=[jax.ShapeDtypeStruct(s, F32) for s in s...  15.1 us
    all_to_all x1, blocking collectives, local_planes(): mine = lax.all_to_all(packed, ('gx', 'gy'), 0, 0, tiled=True)  14.3 us
    ppermute x6, waiting for transfers between devices, spread(): lax.ppermute(array, axis, [(i, i ^ v) for i in range(count)])  8.61 us
    ppermute x6, starting transfers between devices, spread(): lax.ppermute(array, axis, [(i, i ^ v) for i in range(count)])  8.01 us
    ppermute x3, waiting for transfers between devices, local_planes(): lax.ppermute(b, 'gy', [(i, i ^ v) for i in range(m)])  4.27 us
    ppermute x3, starting transfers between devices, local_planes(): lax.ppermute(b, 'gy', [(i, i ^ v) for i in range(m)])  3.55 us
    ppermute x1, starting transfers between devices, local_planes(): even = lax.ppermute(to_even, 'gy', [(i, i ^ 1) for i in range(m)])  2.92 us
    ppermute x1, starting transfers between devices, local_planes(): lax.ppermute(to_odd, 'gy', [(i, (i + 2 * (i % 2) - 1) % m) for i in range...  1.49 us
  transfers between devices with their start and end apart: 18, of which 10 were waited for; matrix products, arithmetic and copies ran while one was open for 0% of the time, Pallas kernels for 11%

profile of v5, /device:TPU:0, one launch (start us, length us, event | category | flops | bytes accessed | tf_op | source)
XLA Modules:
  0.0 66.1 jit_solution(4203635206088248074)
XLA Ops:
  0.0 1.2 %shard_map.46 = (f32[11,4,16,128]{3,2,1,0:T(8,128)S(1)}, f32[11,4,16,128]{3,2,1,0:T(8,128)S(1)}) custom-call(f32[2,4,8,16,128]{4,3,2,1,0:T(8,128)} %rhs.1, f32[8,16,128]{2,1,0:T(8,128)} %rho.1, f32[8,16,128]{2,1,0:T(8,128)} %sr.1, f32[8,16,128]{2,1,0:T(8,128)} %si.1), custom_call_target="tpu_custom_call" | custom-call | tf_op jit(solution)/shard_map/pallas_call | solution.py:617
  1.8 1.3 %collective-permute-done.came = f32[11,4,16,128]{3,2,1,0:T(8,128)S(1)} collective-permute-done((f32[11,4,16,128]{3,2,1,0:T(8,128)S(1)}, f32[11,4,16,128]{3,2,1,0:T(8,128)S(1)}, u32[]{:S(2)}, u32[]{:S(2)}) %collective-permute-start) | collective-permute-done | bytes 360480 | tf_op jit(solution)/shard_map/ppermute | solution.py:643
  3.1 2.9 %collective-permute-start.1 = (f32[2,96,128]{2,1,0:T(8,128)S(1)}, f32[2,96,128]{2,1,0:T(8,128)S(1)}, u32[]{:S(2)}, u32[]{:S(2)}) collective-permute-start(f32[2,96,128]{2,1,0:T(8,128)S(1)} %get-tuple-element.48), channel_id=1, source_target_pairs={{0,2},{2,0},{4,6},{6,4},{1,3},{3,1},{5,7},{7,5},{8,10},{10,8},{12,... | collective-permute-start | bytes 294920 | tf_op jit(solution)/shard_map/ppermute | solution.py:657
  6.1 1.5 %collective-permute-start.2 = (f32[2,96,128]{2,1,0:T(8,128)S(1)}, f32[2,96,128]{2,1,0:T(8,128)S(1)}, u32[]{:S(2)}, u32[]{:S(2)}) collective-permute-start(f32[2,96,128]{2,1,0:T(8,128)S(1)} %get-tuple-element.49), channel_id=1, source_target_pairs={{0,6},{2,4},{4,2},{6,0},{1,7},{3,5},{5,3},{7,1},{8,14},{10,12},{12... | collective-permute-start | bytes 294920 | tf_op jit(solution)/shard_map/ppermute | solution.py:658
  7.8 3.7 %collective-permute-start.5 = (f32[3,2,8,128]{3,2,1,0:T(8,128)S(1)}, f32[3,2,8,128]{3,2,1,0:T(8,128)S(1)}, u32[]{:S(2)}, u32[]{:S(2)}) collective-permute-start(f32[3,2,8,128]{3,2,1,0:T(8,128)S(1)} %shard_map.48.refs_0_), channel_id=1, source_target_pairs={{0,24},{8,16},{16,8},{24,0},{1,25},{9,17},{17,9},{25,1},{2,26},{10... | collective-permute-start | bytes 73736 | tf_op jit(solution)/shard_map/ppermute | solution.py:650
  12.3 1.5 %collective-permute-done.5.refs_3_ = f32[3,2,8,128]{3,2,1,0:T(8,128)S(1)} collective-permute-done((f32[3,2,8,128]{3,2,1,0:T(8,128)S(1)}, f32[3,2,8,128]{3,2,1,0:T(8,128)S(1)}, u32[]{:S(2)}, u32[]{:S(2)}) %collective-permute-start.5) | collective-permute-done | bytes 24608 | tf_op jit(solution)/shard_map/ppermute | solution.py:650
  13.7 2.5 %collective-permute-done.4.refs_2_ = f32[3,2,8,128]{3,2,1,0:T(8,128)S(1)} collective-permute-done((f32[3,2,8,128]{3,2,1,0:T(8,128)S(1)}, f32[3,2,8,128]{3,2,1,0:T(8,128)S(1)}, u32[]{:S(2)}, u32[]{:S(2)}) %collective-permute-start.4) | collective-permute-done | bytes 24608 | tf_op jit(solution)/shard_map/ppermute | solution.py:650
  17.3 1.3 %collective-permute-done.7.from_gz = f32[23,24,256]{2,1,0:T(8,128)S(1)} collective-permute-done((f32[23,24,256]{2,1,0:T(8,128)S(1)}, f32[23,24,256]{2,1,0:T(8,128)S(1)}, u32[]{:S(2)}, u32[]{:S(2)}) %collective-permute-start.7) | collective-permute-done | bytes 565280 | tf_op jit(solution)/shard_map/ppermute | solution.py:665
  18.6 1.7 %shard_map.50 = (f32[8,8,24,256]{3,2,1,0:T(8,128)S(1)}, f32[10,24,256]{2,1,0:T(8,128)S(1)}, f32[8,24,256]{2,1,0:T(8,128)S(1)}, f32[8,24,256]{2,1,0:T(8,128)S(1)}...) custom-call(f32[23,24,256]{2,1,0:T(8,128)S(1)} %collective-permute-d, ...), custom_call_target="tpu_custom_call", output_to_operand_aliasing={{0}: (1, {}), {1}: (2, {}), {2}: (3, {}), {3}: (4, {})} | custom-call | flops 2000000000 | tf_op jit(solution)/shard_map/pallas_call | solution.py:617
  20.3 1.5 %collective-permute-start.10 = (f32[4,3,2,8,128]{4,3,2,1,0:T(8,128)S(1)}, f32[4,3,2,8,128]{4,3,2,1,0:T(8,128)S(1)}, u32[]{:S(2)}, u32[]{:S(2)}) collective-permute-start(f32[4,3,2,8,128]{4,3,2,1,0:T(8,128)S(1)} %get-tuple-element.69.refs_12_), channel_id=1, source_target_pairs={{0,6},{2,4},{4,2},{6,0},{1,7},{3,5},{5,3},{7,1},{8,14},{10,12},{12... | collective-permute-start | bytes 294920 | tf_op jit(solution)/shard_map/ppermute | solution.py:650
  21.8 1.5 %collective-permute-start.9 = (f32[4,3,2,8,128]{4,3,2,1,0:T(8,128)S(1)}, f32[4,3,2,8,128]{4,3,2,1,0:T(8,128)S(1)}, u32[]{:S(2)}, u32[]{:S(2)}) collective-permute-start(f32[4,3,2,8,128]{4,3,2,1,0:T(8,128)S(1)} %get-tuple-element.69.refs_12_), channel_id=1, source_target_pairs={{0,4},{2,6},{4,0},{6,2},{1,5},{3,7},{5,1},{7,3},{8,12},{10,14},{12... | collective-permute-start | bytes 294920 | tf_op jit(solution)/shard_map/ppermute | solution.py:650
  23.8 3.0 %collective-permute-done.10.refs_15_ = f32[4,3,2,8,128]{4,3,2,1,0:T(8,128)S(1)} collective-permute-done((f32[4,3,2,8,128]{4,3,2,1,0:T(8,128)S(1)}, f32[4,3,2,8,128]{4,3,2,1,0:T(8,128)S(1)}, u32[]{:S(2)}, u32[]{:S(2)}) %collective-permute-start.10) | collective-permute-done | bytes 98336 | tf_op jit(solution)/shard_map/ppermute | solution.py:650
  26.8 1.7 %collective-permute-done.9.refs_14_ = f32[4,3,2,8,128]{4,3,2,1,0:T(8,128)S(1)} collective-permute-done((f32[4,3,2,8,128]{4,3,2,1,0:T(8,128)S(1)}, f32[4,3,2,8,128]{4,3,2,1,0:T(8,128)S(1)}, u32[]{:S(2)}, u32[]{:S(2)}) %collective-permute-start.9) | collective-permute-done | bytes 98336 | tf_op jit(solution)/shard_map/ppermute | solution.py:650
  28.5 2.4 %shard_map.51 = (f32[8,8,24,256]{3,2,1,0:T(8,128)S(1)}, f32[10,24,256]{2,1,0:T(8,128)S(1)}, f32[8,24,256]{2,1,0:T(8,128)S(1)}, f32[8,24,256]{2,1,0:T(8,128)S(1)}...) custom-call(f32[23,24,256]{2,1,0:T(8,128)S(1)} %collective-permute-d, ...), custom_call_target="tpu_custom_call", output_to_operand_aliasing={{0}: (1, {}), {1}: (2, {}), {2}: (3, {}), {3}: (4, {}), {4}... | custom-call | tf_op jit(solution)/shard_map/pallas_call | solution.py:617
  31.0 14.3 %all_to_all.5.fields = f32[16,2,2,8,128]{4,3,2,1,0:T(8,128)S(1)} all-to-all(f32[16,2,2,8,128]{4,3,2,1,0:T(8,128)S(1)} %get-tuple-element.70), channel_id=1, replica_groups=mesh['gx'=4,'gy'=4,'gz'=2] {'gx','gy'}, dimensions={0} | all-to-all | bytes 524288 | tf_op jit(solution)/shard_map/all_to_all | solution.py:681
  46.6 0.9 %collective-permute-done.11.other = f32[16,5,2,8,128]{4,3,2,1,0:T(8,128)S(1)} collective-permute-done((f32[16,5,2,8,128]{4,3,2,1,0:T(8,128)S(1)}, f32[16,5,2,8,128]{4,3,2,1,0:T(8,128)S(1)}, u32[]{:S(2)}, u32[]{:S(2)}) %collective-permute-start.11) | collective-permute-done | bytes 655392 | tf_op jit(solution)/shard_map/ppermute | solution.py:683
  47.5 5.3 %shard_map.53.u1 = f32[2,4,32,128]{3,2,1,0:T(8,128)S(1)} custom-call(f32[16,5,2,8,128]{4,3,2,1,0:T(8,128)S(1)} %shard_map.52.mine, f32[16,5,2,8,128]{4,3,2,1,0:T(8,128)S(1)} %collective-permute-done.11.other), custom_call_target="tpu_custom_call" | custom-call | flops 5000000000 | tf_op jit(solution)/shard_map/pallas_call | solution.py:617
  52.9 0.8 %collective-permute-start.14 = (f32[160,128]{1,0:T(8,128)S(1)}, f32[160,128]{1,0:T(8,128)S(1)}, u32[]{:S(2)}, u32[]{:S(2)}) collective-permute-start(f32[160,128]{1,0:T(8,128)S(1)} %get-tuple-element.76), channel_id=1, source_target_pairs={{0,2},{2,0},{4,6},{6,4},{1,3},{3,1},{5,7},{7,5},{8,10},{10,8},{12,... | collective-permute-start | bytes 245768 | tf_op jit(solution)/shard_map/ppermute | solution.py:704
  54.5 2.0 %collective-permute-start.16 = (f32[160,128]{1,0:T(8,128)S(1)}, f32[160,128]{1,0:T(8,128)S(1)}, u32[]{:S(2)}, u32[]{:S(2)}) collective-permute-start(f32[160,128]{1,0:T(8,128)S(1)} %get-tuple-element.78), channel_id=1, source_target_pairs={{0,6},{2,4},{4,2},{6,0},{1,7},{3,5},{5,3},{7,1},{8,14},{10,12},{12... | collective-permute-start | bytes 245768 | tf_op jit(solution)/shard_map/ppermute | solution.py:704
  56.5 1.3 %collective-permute-done.14.refs_1_ = f32[160,128]{1,0:T(8,128)S(1)} collective-permute-done((f32[160,128]{1,0:T(8,128)S(1)}, f32[160,128]{1,0:T(8,128)S(1)}, u32[]{:S(2)}, u32[]{:S(2)}) %collective-permute-start.14) | collective-permute-done | bytes 81952 | tf_op jit(solution)/shard_map/ppermute | solution.py:704
  57.8 2.9 %collective-permute-done.15.refs_2_ = f32[160,128]{1,0:T(8,128)S(1)} collective-permute-done((f32[160,128]{1,0:T(8,128)S(1)}, f32[160,128]{1,0:T(8,128)S(1)}, u32[]{:S(2)}, u32[]{:S(2)}) %collective-permute-start.15) | collective-permute-done | bytes 81952 | tf_op jit(solution)/shard_map/ppermute | solution.py:704
  60.8 2.8 %shard_map.55 = f32[2,2,4,4,16,128]{5,4,3,2,1,0:T(8,128)S(1)} custom-call(f32[160,128]{1,0:T(8,128)S(1)} %get-tuple-element.75.refs_0_, f32[160,128]{1,0:T(8,128)S(1)} %collective-permute-done.14.refs_1_, f32[160,128]{1,0:T(8,128)S(1)} %collective-permute-done.15.refs_2_, f32[160,128]{1,0:T(8,128)S(1)} %collective-permute-done.16.refs_3_, ...), custom_call_target="tpu_custom_call" | custom-call | tf_op jit(solution)/shard_map/pallas_call | solution.py:617
  63.8 1.4 %collective-permute-done.17.came = f32[2,4,4,16,128]{4,3,2,1,0:T(8,128)S(1)} collective-permute-done((f32[2,4,4,16,128]{4,3,2,1,0:T(8,128)S(1)}, f32[2,4,4,16,128]{4,3,2,1,0:T(8,128)S(1)}, u32[]{:S(2)}, u32[]{:S(2)}) %collective-permute-start.17) | collective-permute-done | bytes 262176 | tf_op jit(solution)/shard_map/ppermute | solution.py:711
  65.2 0.8 %shard_map.56 = f32[2,4,8,16,128]{4,3,2,1,0:T(8,128)} custom-call(f32[2,4,4,16,128]{4,3,2,1,0:T(8,128)S(1)} %get-tuple-element.88.kept, f32[2,4,4,16,128]{4,3,2,1,0:T(8,128)S(1)} %collective-permute-done.17.came), custom_call_target="tpu_custom_call" | custom-call | tf_op jit(solution)/shard_map/pallas_call | solution.py:617
  (25 shorter events, 5.5 us)
Async XLA Ops:
  1.2 1.8 %collective-permute-start = (f32[11,4,16,128]{3,2,1,0:T(8,128)S(1)}, f32[11,4,16,128]{3,2,1,0:T(8,128)S(1)}, u32[]{:S(2)}, u32[]{:S(2)}) collective-permute-start(f32[11,4,16,128]{3,2,1,0:T(8,128)S(1)} %get-tuple-element.47), channel_id=1, source_target_pairs={{0,1},{1,0},{2,3},{3,2},{4,5},{5,4},{6,7},{7,6},{8,9},{9,8},{10,11... | collective-permute-start | bytes 1081352 | tf_op jit(solution)/shard_map/ppermute | solution.py:643
  3.1 13.1 %collective-permute-start.1 = (f32[2,96,128]{2,1,0:T(8,128)S(1)}, f32[2,96,128]{2,1,0:T(8,128)S(1)}, u32[]{:S(2)}, u32[]{:S(2)}) collective-permute-start(f32[2,96,128]{2,1,0:T(8,128)S(1)} %get-tuple-element.48), channel_id=1, source_target_pairs={{0,2},{2,0},{4,6},{6,4},{1,3},{3,1},{5,7},{7,5},{8,10},{10,8},{12,... | collective-permute-start | bytes 294920 | tf_op jit(solution)/shard_map/ppermute | solution.py:657
  6.1 10.1 %collective-permute-start.2 = (f32[2,96,128]{2,1,0:T(8,128)S(1)}, f32[2,96,128]{2,1,0:T(8,128)S(1)}, u32[]{:S(2)}, u32[]{:S(2)}) collective-permute-start(f32[2,96,128]{2,1,0:T(8,128)S(1)} %get-tuple-element.49), channel_id=1, source_target_pairs={{0,6},{2,4},{4,2},{6,0},{1,7},{3,5},{5,3},{7,1},{8,14},{10,12},{12... | collective-permute-start | bytes 294920 | tf_op jit(solution)/shard_map/ppermute | solution.py:658
  7.8 5.9 %collective-permute-start.5 = (f32[3,2,8,128]{3,2,1,0:T(8,128)S(1)}, f32[3,2,8,128]{3,2,1,0:T(8,128)S(1)}, u32[]{:S(2)}, u32[]{:S(2)}) collective-permute-start(f32[3,2,8,128]{3,2,1,0:T(8,128)S(1)} %shard_map.48.refs_0_), channel_id=1, source_target_pairs={{0,24},{8,16},{16,8},{24,0},{1,25},{9,17},{17,9},{25,1},{2,26},{10... | collective-permute-start | bytes 73736 | tf_op jit(solution)/shard_map/ppermute | solution.py:650
  11.5 4.7 %collective-permute-start.4 = (f32[3,2,8,128]{3,2,1,0:T(8,128)S(1)}, f32[3,2,8,128]{3,2,1,0:T(8,128)S(1)}, u32[]{:S(2)}, u32[]{:S(2)}) collective-permute-start(f32[3,2,8,128]{3,2,1,0:T(8,128)S(1)} %shard_map.48.refs_0_), channel_id=1, source_target_pairs={{0,16},{8,24},{16,0},{24,8},{1,17},{9,25},{17,1},{25,9},{2,18},{10... | collective-permute-start | bytes 73736 | tf_op jit(solution)/shard_map/ppermute | solution.py:650
  11.5 4.7 %collective-permute-start.3 = (f32[3,2,8,128]{3,2,1,0:T(8,128)S(1)}, f32[3,2,8,128]{3,2,1,0:T(8,128)S(1)}, u32[]{:S(2)}, u32[]{:S(2)}) collective-permute-start(f32[3,2,8,128]{3,2,1,0:T(8,128)S(1)} %shard_map.48.refs_0_), channel_id=1, source_target_pairs={{0,8},{8,0},{16,24},{24,16},{1,9},{9,1},{17,25},{25,17},{2,10},{10... | collective-permute-start | bytes 73736 | tf_op jit(solution)/shard_map/ppermute | solution.py:650
  16.5 2.0 %collective-permute-start.7 = (f32[23,24,256]{2,1,0:T(8,128)S(1)}, f32[23,24,256]{2,1,0:T(8,128)S(1)}, u32[]{:S(2)}, u32[]{:S(2)}) collective-permute-start(f32[23,24,256]{2,1,0:T(8,128)S(1)} %get-tuple-element.51), channel_id=1, source_target_pairs={{0,1},{1,0},{2,3},{3,2},{4,5},{5,4},{6,7},{7,6},{8,9},{9,8},{10,11... | collective-permute-start | bytes 1695752 | tf_op jit(solution)/shard_map/ppermute | solution.py:665
  16.6 7.2 %collective-permute-start.6 = (f32[23,24,256]{2,1,0:T(8,128)S(1)}, f32[23,24,256]{2,1,0:T(8,128)S(1)}, u32[]{:S(2)}, u32[]{:S(2)}) collective-permute-start(f32[23,24,256]{2,1,0:T(8,128)S(1)} %get-tuple-element.50), channel_id=1, source_target_pairs={{1,8},{8,1},{9,16},{16,9},{17,24},{24,17},{3,10},{10,3},{11,18},{1... | collective-permute-start | bytes 1695752 | tf_op jit(solution)/shard_map/ppermute | solution.py:664
  20.3 6.6 %collective-permute-start.10 = (f32[4,3,2,8,128]{4,3,2,1,0:T(8,128)S(1)}, f32[4,3,2,8,128]{4,3,2,1,0:T(8,128)S(1)}, u32[]{:S(2)}, u32[]{:S(2)}) collective-permute-start(f32[4,3,2,8,128]{4,3,2,1,0:T(8,128)S(1)} %get-tuple-element.69.refs_12_), channel_id=1, source_target_pairs={{0,6},{2,4},{4,2},{6,0},{1,7},{3,5},{5,3},{7,1},{8,14},{10,12},{12... | collective-permute-start | bytes 294920 | tf_op jit(solution)/shard_map/ppermute | solution.py:650
  21.8 6.7 %collective-permute-start.9 = (f32[4,3,2,8,128]{4,3,2,1,0:T(8,128)S(1)}, f32[4,3,2,8,128]{4,3,2,1,0:T(8,128)S(1)}, u32[]{:S(2)}, u32[]{:S(2)}) collective-permute-start(f32[4,3,2,8,128]{4,3,2,1,0:T(8,128)S(1)} %get-tuple-element.69.refs_12_), channel_id=1, source_target_pairs={{0,4},{2,6},{4,0},{6,2},{1,5},{3,7},{5,1},{7,3},{8,12},{10,14},{12... | collective-permute-start | bytes 294920 | tf_op jit(solution)/shard_map/ppermute | solution.py:650
  23.3 5.2 %collective-permute-start.8 = (f32[4,3,2,8,128]{4,3,2,1,0:T(8,128)S(1)}, f32[4,3,2,8,128]{4,3,2,1,0:T(8,128)S(1)}, u32[]{:S(2)}, u32[]{:S(2)}) collective-permute-start(f32[4,3,2,8,128]{4,3,2,1,0:T(8,128)S(1)} %get-tuple-element.69.refs_12_), channel_id=1, source_target_pairs={{0,2},{2,0},{4,6},{6,4},{1,3},{3,1},{5,7},{7,5},{8,10},{10,8},{12,... | collective-permute-start | bytes 294920 | tf_op jit(solution)/shard_map/ppermute | solution.py:650
  45.4 2.2 %collective-permute-start.11 = (f32[16,5,2,8,128]{4,3,2,1,0:T(8,128)S(1)}, f32[16,5,2,8,128]{4,3,2,1,0:T(8,128)S(1)}, u32[]{:S(2)}, u32[]{:S(2)}) collective-permute-start(f32[16,5,2,8,128]{4,3,2,1,0:T(8,128)S(1)} %shard_map.52.mine), channel_id=1, source_target_pairs={{0,1},{1,0},{2,3},{3,2},{4,5},{5,4},{6,7},{7,6},{8,9},{9,8},{10,11... | collective-permute-start | bytes 1966088 | tf_op jit(solution)/shard_map/ppermute | solution.py:683
  45.4 7.4 %collective-permute-start.12 = (f32[8,16,256]{2,1,0:T(8,128)S(1)}, f32[8,16,256]{2,1,0:T(8,128)S(1)}, u32[]{:S(2)}, u32[]{:S(2)}) collective-permute-start(f32[8,16,256]{2,1,0:T(8,128)S(1)} %get-tuple-element.73), channel_id=1, source_target_pairs={{0,1},{1,0},{2,3},{3,2},{4,5},{5,4},{6,7},{7,6},{8,9},{9,8},{10,11... | collective-permute-start | bytes 393224 | tf_op jit(solution)/shard_map/ppermute | solution.py:680
  45.9 6.9 %collective-permute-start.13 = (f32[8,16,256]{2,1,0:T(8,128)S(1)}, f32[8,16,256]{2,1,0:T(8,128)S(1)}, u32[]{:S(2)}, u32[]{:S(2)}) collective-permute-start(f32[8,16,256]{2,1,0:T(8,128)S(1)} %get-tuple-element.74), channel_id=1, source_target_pairs={{1,8},{8,1},{9,16},{16,9},{17,24},{24,17},{3,10},{10,3},{11,18},{1... | collective-permute-start | bytes 393224 | tf_op jit(solution)/shard_map/ppermute | solution.py:679
  52.9 4.9 %collective-permute-start.14 = (f32[160,128]{1,0:T(8,128)S(1)}, f32[160,128]{1,0:T(8,128)S(1)}, u32[]{:S(2)}, u32[]{:S(2)}) collective-permute-start(f32[160,128]{1,0:T(8,128)S(1)} %get-tuple-element.76), channel_id=1, source_target_pairs={{0,2},{2,0},{4,6},{6,4},{1,3},{3,1},{5,7},{7,5},{8,10},{10,8},{12,... | collective-permute-start | bytes 245768 | tf_op jit(solution)/shard_map/ppermute | solution.py:704
  53.8 7.0 %collective-permute-start.15 = (f32[160,128]{1,0:T(8,128)S(1)}, f32[160,128]{1,0:T(8,128)S(1)}, u32[]{:S(2)}, u32[]{:S(2)}) collective-permute-start(f32[160,128]{1,0:T(8,128)S(1)} %get-tuple-element.77), channel_id=1, source_target_pairs={{0,4},{2,6},{4,0},{6,2},{1,5},{3,7},{5,1},{7,3},{8,12},{10,14},{12... | collective-permute-start | bytes 245768 | tf_op jit(solution)/shard_map/ppermute | solution.py:704
  54.5 6.3 %collective-permute-start.16 = (f32[160,128]{1,0:T(8,128)S(1)}, f32[160,128]{1,0:T(8,128)S(1)}, u32[]{:S(2)}, u32[]{:S(2)}) collective-permute-start(f32[160,128]{1,0:T(8,128)S(1)} %get-tuple-element.78), channel_id=1, source_target_pairs={{0,6},{2,4},{4,2},{6,0},{1,7},{3,5},{5,3},{7,1},{8,14},{10,12},{12... | collective-permute-start | bytes 245768 | tf_op jit(solution)/shard_map/ppermute | solution.py:704
  63.6 1.6 %collective-permute-start.17 = (f32[2,4,4,16,128]{4,3,2,1,0:T(8,128)S(1)}, f32[2,4,4,16,128]{4,3,2,1,0:T(8,128)S(1)}, u32[]{:S(2)}, u32[]{:S(2)}) collective-permute-start(f32[2,4,4,16,128]{4,3,2,1,0:T(8,128)S(1)} %get-tuple-element.87), channel_id=1, source_target_pairs={{0,1},{1,0},{2,3},{3,2},{4,5},{5,4},{6,7},{7,6},{8,9},{9,8},{10,11... | collective-permute-start | bytes 786440 | tf_op jit(solution)/shard_map/ppermute | solution.py:711

commit v6 on v5

--- a/solution.py
+++ b/solution.py
@@ -129,7 +129,8 @@
 
 
 def loop(count, body):
-    lax.fori_loop(0, count, lambda i, c: (body(i), c)[1], 0)
+    for i in range(count):
+        body(i)
 
 
 def safe(total):
@@ -146,19 +147,23 @@
         r = rho[pl.ds(p + 1, step)]
         row = lax.broadcasted_iota(jnp.int32, r.shape, 1)
         lane = lax.broadcasted_iota(jnp.int32, r.shape, 2)
-        bx[pl.ds(p + 1, step)] = two / safe(r + rho[pl.ds(p + 2, step)])
-        edge = two / safe(r)
+        last_y, last_z = row == ny - 1, lane == nz - 1
+        tx = safe(r + rho[pl.ds(p + 2, step)])
+        ty = safe(r + jnp.where(last_y, 0.0, pltpu.roll(r, ny - 1, 1)))
+        tz = safe(r + jnp.where(last_z, 0.0, pltpu.roll(r, nz - 1, 2)))
+        te = safe(r)
+        pair, other = tx * ty, tz * te
+        whole = two / (pair * other)
+        per_pair, per_other = whole * other, whole * pair
+        bx[pl.ds(p + 1, step)] = per_pair * ty
+        edge = per_other * tz
         bsum = bx[pl.ds(p, step)] + bx[pl.ds(p + 1, step)]
-        last = row == ny - 1
-        up = jnp.where(last, 0.0, pltpu.roll(r, ny - 1, 1))
-        face = two / safe(r + up)
+        face = per_pair * tx
         bsum = bsum + face + jnp.where(row == 0, edge, pltpu.roll(face, 1, 1))
-        by[pl.ds(p, step)] = jnp.where(last, 0.0, face)
-        last = lane == nz - 1
-        up = jnp.where(last, 0.0, pltpu.roll(r, nz - 1, 2))
-        face = two / safe(r + up)
+        by[pl.ds(p, step)] = jnp.where(last_y, 0.0, face)
+        face = per_other * te
         bsum = bsum + face + jnp.where(lane == 0, edge, pltpu.roll(face, 1, 2))
-        bz[pl.ds(p, step)] = jnp.where(last, 0.0, face)
+        bz[pl.ds(p, step)] = jnp.where(last_z, 0.0, face)
         d = bsum - sr[pl.ds(p, step)]
         e = si[pl.ds(p, step)]
         w = jnp.where(r > 0.0, omega_damp, 0.0) / (d * d + e * e)
@@ -211,7 +216,13 @@
 
 
 def dot(a, b):
-    return jnp.dot(a, b, precision=lax.Precision.HIGHEST, preferred_element_type=F32)
+    b = b.astype(jnp.bfloat16)
+    high = a.astype(jnp.bfloat16)
+    a = a - high.astype(F32)
+    middle = a.astype(jnp.bfloat16)
+    low = (a - middle.astype(F32)).astype(jnp.bfloat16)
+    parts = [jnp.dot(part, b, preferred_element_type=F32) for part in (low, middle, high)]
+    return parts[0] + parts[1] + parts[2]
 
 
 def send_kernel(rhs, rho, sr, si, away, kept, sems):
@@ -302,22 +313,40 @@
                     at += n
     for out, up in ((to_gz, 1 - k), (to_gx, k)):
         two, three = HALO + up * (half - HALO), HALO + 1 + up * (half - HALO - 1)
+        rows, ny = ref.shape[1] - 2 * (SIDE - HALO), ref.shape[1]
         for j, ref in enumerate(arrays[:m2] + [sr, si]):
-            out[HALO * j : HALO * (j + 1)] = ref[pl.ds(two, HALO)]
-        out[HALO * (m2 + 2) :] = rho[pl.ds(three, HALO + 1)]
-
-
-def side_planes(came, low, g, rho, sr, si, bx, by, bz, wr, wi, dr, ua, own, rest):
+            for i in range(HALO):
+                at = (HALO * j + i) * rows
+                out[at : at + rows, :] = ref[two + i, SIDE - HALO : SIDE - HALO + rows, :]
+        for i in range(HALO + 1):
+            at = HALO * (m2 + 2) * rows + i * ny
+            out[at : at + ny, :] = rho[three + i]
+
+
+def lay_side(came, low, g, rho, sr, si):
+    m2, pad = g.shape[:2]
+    half = pad - 2 * HALO
+    two, three = low * (half + HALO), low * (half + HALO + 1)
+    ny, nz = sr.shape[1:]
+    rows = ny - 2 * (SIDE - HALO)
+    blank = jnp.zeros((ny, nz), F32)
+    for j, ref in enumerate([g.at[f] for f in range(m2)] + [sr, si]):
+        for i in range(HALO):
+            at = (HALO * j + i) * rows
+            ref[two + i] = blank
+            ref[two + i, SIDE - HALO : SIDE - HALO + rows, :] = came[at : at + rows, :]
+    for i in range(HALO + 1):
+        at = HALO * (m2 + 2) * rows + i * ny
+        rho[three + i] = came[at : at + ny, :]
+
+
+def side_planes(low, g, rho, sr, si, bx, by, bz, wr, wi, dr, ua, own, rest):
     m2, pad = g.shape[:2]
     m = m2 // 2
     half = pad - 2 * HALO
-    two, three = low * (half + HALO), low * (half + HALO + 1)
-    for j, ref in enumerate([g.at[f] for f in range(m2)] + [sr, si]):
-        ref[pl.ds(two, HALO)] = came[HALO * j : HALO * (j + 1)]
-    rho[pl.ds(three, HALO + 1)] = came[HALO * (m2 + 2) :]
     count = HALO + 1 if rest else pad - HALO - 1
     start = low * (pad - count)
-    level_coefs(rho, sr, si, 1.0, bx, by, bz, wr, wi, dr, 1, start, count)
+    level_coefs(rho, sr, si, 1.0, bx, by, bz, wr, wi, dr, count, start, count)
 
     def first(i):
         p = start + i
@@ -337,17 +366,21 @@
     loop(done, second)
 
 
-def near_kernel(from_gz, _g, _rho, _sr, _si, *refs):
-    means, *state, out = refs
+def beside_kernel(from_gz, _g, _rho, _sr, _si, means, g, rho, sr, si, out):
+    lay_side(from_gz, 1 - lax.axis_index("gz"), g, rho, sr, si)
     out[...] = means[...]
-    side_planes(from_gz, 1 - lax.axis_index("gz"), *state, False)
+
+
+def near_kernel(_g, _rho, _sr, _si, *state):
+    side_planes(1 - lax.axis_index("gz"), *state, False)
 
 
 def fine_kernel(from_gx, *refs):
     g, rho, sr, si, bx, by, bz, wr, wi, dr, ua, own, up_gz, up_gx, up_gy, packed, joined, left, right, narrow = refs[-20:]
     join("gy", refs[12:-20], joined)
     k = lax.axis_index("gz")
-    side_planes(from_gx, k, g, rho, sr, si, bx, by, bz, wr, wi, dr, ua, own, True)
+    lay_side(from_gx, k, g, rho, sr, si)
+    side_planes(k, g, rho, sr, si, bx, by, bz, wr, wi, dr, ua, own, True)
     coefs = (bx, by, bz, wr, wi)
     m2, pad, ny, nz = g.shape
     m = m2 // 2
@@ -372,7 +405,7 @@
             br, bi = resid_planes(own, (r, m + r), p, g, p + 1, p + 1, 1, coefs, dr, si)
             totals[r], totals[m + r] = ar + br, ai + bi
         for j, v in totals.items():
-            spot = pl.ds(pl.multiple_of((j * pairs + q) * ny, ny), ny)
+            spot = pl.ds((j * pairs + q) * ny, ny)
             left[spot, :] = v[0, :, :lanes]
             right[spot, :] = v[0, :, lanes:]
 
@@ -413,7 +446,7 @@
 
     def body(q):
         for j, v in enumerate(values(q)):
-            sums[pl.ds(pl.multiple_of((j * total + q) * ny, ny), ny), :] = v
+            sums[pl.ds((j * total + q) * ny, ny), :] = v
 
     loop(total, body)
     n = count * total * ny // 2
@@ -426,7 +459,7 @@
     rho1[pl.ds(0, 1)] = zero
     rho1[pl.ds(n1 + 1, 1)] = zero
     put_coarse(mine, other, (rho1, sr1, si1), (1, 0, 0), ny // mine.shape[3], 2)
-    level_coefs(rho1, sr1, si1, 0.25, bx1, by1, bz1, wr1, wi1, dr1, 4, 0, n1)
+    level_coefs(rho1, sr1, si1, 0.25, bx1, by1, bz1, wr1, wi1, dr1, 8, 0, n1)
     n2, ny2 = sr2.shape[:2]
     halve(sums, narrow, ny, 3, n2, lambda q: (rho1[2 * q + 1] + rho1[2 * q + 2], sr1[2 * q] + sr1[2 * q + 1], si1[2 * q] + si1[2 * q + 1]))
     zero2 = jnp.zeros((1, ny2, nz), F32)
@@ -499,7 +532,7 @@
 
     def lift(q):
         for c in range(2):
-            v = tall[pl.ds(pl.multiple_of((c * n2 + q) * ny, ny), ny), :]
+            v = tall[pl.ds((c * n2 + q) * ny, ny), :]
             for j in range(2):
                 ub1[c, 2 * q + j + 1] = ub1[c, 2 * q + j + 1] + v
 
@@ -659,7 +692,7 @@
 
     plane = (rows + 2 * SIDE, nz)
     laid = [(2 * m, pad) + plane, (pad + 2,) + plane, (pad,) + plane, (pad,) + plane]
-    edges = (HALO * (2 * m + 2) + HALO + 1,) + plane
+    edges = (HALO * (2 * m + 2) * (rows + 2 * HALO) + (HALO + 1) * plane[0], nz)
     *state, to_gz, to_gx, coarse = call(lay_kernel, laid + [edges, edges, (chips, *means)], (kept, came, even, odd, *coarse), scratch=[(2,) + rim])
     from_gx = lax.ppermute(to_gx, ("gx", "gz"), ends)
     from_gz = lax.ppermute(to_gz, "gz", swap)
@@ -667,8 +700,9 @@
     brow = (rows, nz)
     tall0 = 2 * m * pairs * plane[0]
     full = laid + [(pad + 1,) + plane] + [(pad,) + plane] * 5 + [(2 * m, pad) + plane, (2 * m, pad - 2) + plane]
-    *state, coarse = call(near_kernel, full + [(chips, *means)], (from_gz, *state, coarse), aliases={i + 1: i for i in range(len(laid))}, cost=NEAR_COST)
+    *state, coarse = call(beside_kernel, laid + [(chips, *means)], (from_gz, *state, coarse), aliases={i + 1: i for i in range(len(laid))})
     coarse = spread(coarse, "gy", m)
+    state = call(near_kernel, full, tuple(state), aliases={i: i for i in range(len(laid))}, cost=NEAR_COST)
     g, _, _, _, bx, by, bz, wr, wi, _, _, own, up_gz, up_gx, up_gy, packed, coarse = call(
         fine_kernel,
         full + [(2 * m,) + brow, (2 * m,) + brow, (2, 4 * m * half, lanes), (chips * m, 2, pairs, rows // 2, lanes), (m * chips, *means)],

time: 66.3 us -> 62 us (0.935)
  Pallas kernels: 15.1 us -> 11.8 us
  waiting for transfers between devices: 17.8 us -> 16.8 us
    pallas_call x11 -> x12, Pallas kernels: 15.1 us -> 11.8 us  [call(): pl.pallas_call(kernel, out_shape=[jax.ShapeDtypeStruct(s, F32) for s in s...]
    ppermute x6, waiting for transfers between devices: 8.61 us -> 7.65 us  [spread(): lax.ppermute(array, axis, [(i, i ^ v) for i in range(count)])]
  transfers between devices with their start and end apart: 18 -> 18, of which waited for: 10 -> 11; matrix products, arithmetic and copies ran while one was open for 0% -> 0% of each run, Pallas kernels for 11% -> 7%
where the time goes in v6:
time: 62 us; the launch traced here: 61.8 us
  starting transfers between devices  18.6 us (30%)
  waiting for transfers between devices  16.8 us (27%)
  blocking collectives  14.5 us (23%)
  Pallas kernels  11.8 us (19%)
    all_to_all x1, blocking collectives, local_planes(): mine = lax.all_to_all(packed, ('gx', 'gy'), 0, 0, tiled=True)  14.5 us
    pallas_call x12, Pallas kernels, call(): pl.pallas_call(kernel, out_shape=[jax.ShapeDtypeStruct(s, F32) for s in s...  11.8 us
    ppermute x6, starting transfers between devices, spread(): lax.ppermute(array, axis, [(i, i ^ v) for i in range(count)])  8 us
    ppermute x6, waiting for transfers between devices, spread(): lax.ppermute(array, axis, [(i, i ^ v) for i in range(count)])  7.65 us
    ppermute x3, waiting for transfers between devices, local_planes(): lax.ppermute(b, 'gy', [(i, i ^ v) for i in range(m)])  4.27 us
    ppermute x3, starting transfers between devices, local_planes(): lax.ppermute(b, 'gy', [(i, i ^ v) for i in range(m)])  3.55 us
    ppermute x1, starting transfers between devices, local_planes(): even = lax.ppermute(to_even, 'gy', [(i, i ^ 1) for i in range(m)])  2.92 us
    ppermute x1, starting transfers between devices, local_planes(): lax.ppermute(to_odd, 'gy', [(i, (i + 2 * (i % 2) - 1) % m) for i in range...  1.49 us
  transfers between devices with their start and end apart: 18, of which 11 were waited for; matrix products, arithmetic and copies ran while one was open for 0% of the time, Pallas kernels for 7%

profile of v6, /device:TPU:0, one launch (start us, length us, event | category | flops | bytes accessed | tf_op | source)
XLA Modules:
  0.0 61.8 jit_solution(15676761560670376163)
XLA Ops:
  0.0 1.2 %shard_map.46 = (f32[11,4,16,128]{3,2,1,0:T(8,128)S(1)}, f32[11,4,16,128]{3,2,1,0:T(8,128)S(1)}) custom-call(f32[2,4,8,16,128]{4,3,2,1,0:T(8,128)} %rhs.1, f32[8,16,128]{2,1,0:T(8,128)} %rho.1, f32[8,16,128]{2,1,0:T(8,128)} %sr.1, f32[8,16,128]{2,1,0:T(8,128)} %si.1), custom_call_target="tpu_custom_call" | custom-call | tf_op jit(solution)/shard_map/pallas_call | solution.py:650
  1.8 1.3 %collective-permute-done.came = f32[11,4,16,128]{3,2,1,0:T(8,128)S(1)} collective-permute-done((f32[11,4,16,128]{3,2,1,0:T(8,128)S(1)}, f32[11,4,16,128]{3,2,1,0:T(8,128)S(1)}, u32[]{:S(2)}, u32[]{:S(2)}) %collective-permute-start) | collective-permute-done | bytes 360480 | tf_op jit(solution)/shard_map/ppermute | solution.py:676
  3.1 2.9 %collective-permute-start.1 = (f32[2,96,128]{2,1,0:T(8,128)S(1)}, f32[2,96,128]{2,1,0:T(8,128)S(1)}, u32[]{:S(2)}, u32[]{:S(2)}) collective-permute-start(f32[2,96,128]{2,1,0:T(8,128)S(1)} %get-tuple-element.52), channel_id=1, source_target_pairs={{0,2},{2,0},{4,6},{6,4},{1,3},{3,1},{5,7},{7,5},{8,10},{10,8},{12,... | collective-permute-start | bytes 294920 | tf_op jit(solution)/shard_map/ppermute | solution.py:690
  6.1 1.5 %collective-permute-start.2 = (f32[2,96,128]{2,1,0:T(8,128)S(1)}, f32[2,96,128]{2,1,0:T(8,128)S(1)}, u32[]{:S(2)}, u32[]{:S(2)}) collective-permute-start(f32[2,96,128]{2,1,0:T(8,128)S(1)} %get-tuple-element.53), channel_id=1, source_target_pairs={{0,6},{2,4},{4,2},{6,0},{1,7},{3,5},{5,3},{7,1},{8,14},{10,12},{12... | collective-permute-start | bytes 294920 | tf_op jit(solution)/shard_map/ppermute | solution.py:691
  7.8 3.7 %collective-permute-start.5 = (f32[3,2,8,128]{3,2,1,0:T(8,128)S(1)}, f32[3,2,8,128]{3,2,1,0:T(8,128)S(1)}, u32[]{:S(2)}, u32[]{:S(2)}) collective-permute-start(f32[3,2,8,128]{3,2,1,0:T(8,128)S(1)} %shard_map.48.refs_0_), channel_id=1, source_target_pairs={{0,24},{8,16},{16,8},{24,0},{1,25},{9,17},{17,9},{25,1},{2,26},{10... | collective-permute-start | bytes 73736 | tf_op jit(solution)/shard_map/ppermute | solution.py:683
  12.2 1.5 %collective-permute-done.5.refs_3_ = f32[3,2,8,128]{3,2,1,0:T(8,128)S(1)} collective-permute-done((f32[3,2,8,128]{3,2,1,0:T(8,128)S(1)}, f32[3,2,8,128]{3,2,1,0:T(8,128)S(1)}, u32[]{:S(2)}, u32[]{:S(2)}) %collective-permute-start.5) | collective-permute-done | bytes 24608 | tf_op jit(solution)/shard_map/ppermute | solution.py:683
  13.7 2.5 %collective-permute-done.4.refs_2_ = f32[3,2,8,128]{3,2,1,0:T(8,128)S(1)} collective-permute-done((f32[3,2,8,128]{3,2,1,0:T(8,128)S(1)}, f32[3,2,8,128]{3,2,1,0:T(8,128)S(1)}, u32[]{:S(2)}, u32[]{:S(2)}) %collective-permute-start.4) | collective-permute-done | bytes 24608 | tf_op jit(solution)/shard_map/ppermute | solution.py:683
  17.3 1.1 %collective-permute-done.7.from_gz = f32[472,256]{1,0:T(8,128)S(1)} collective-permute-done((f32[472,256]{1,0:T(8,128)S(1)}, f32[472,256]{1,0:T(8,128)S(1)}, u32[]{:S(2)}, u32[]{:S(2)}) %collective-permute-start.7) | collective-permute-done | bytes 483360 | tf_op jit(solution)/shard_map/ppermute | solution.py:698
  18.5 1.5 %collective-permute-start.10 = (f32[4,3,2,8,128]{4,3,2,1,0:T(8,128)S(1)}, f32[4,3,2,8,128]{4,3,2,1,0:T(8,128)S(1)}, u32[]{:S(2)}, u32[]{:S(2)}) collective-permute-start(f32[4,3,2,8,128]{4,3,2,1,0:T(8,128)S(1)} %get-tuple-element.77.refs_12_), channel_id=1, source_target_pairs={{0,6},{2,4},{4,2},{6,0},{1,7},{3,5},{5,3},{7,1},{8,14},{10,12},{12... | collective-permute-start | bytes 294920 | tf_op jit(solution)/shard_map/ppermute | solution.py:683
  20.0 1.5 %collective-permute-start.9 = (f32[4,3,2,8,128]{4,3,2,1,0:T(8,128)S(1)}, f32[4,3,2,8,128]{4,3,2,1,0:T(8,128)S(1)}, u32[]{:S(2)}, u32[]{:S(2)}) collective-permute-start(f32[4,3,2,8,128]{4,3,2,1,0:T(8,128)S(1)} %get-tuple-element.77.refs_12_), channel_id=1, source_target_pairs={{0,4},{2,6},{4,0},{6,2},{1,5},{3,7},{5,1},{7,3},{8,12},{10,14},{12... | collective-permute-start | bytes 294920 | tf_op jit(solution)/shard_map/ppermute | solution.py:683
  22.1 1.1 %shard_map.51 = (f32[8,8,24,256]{3,2,1,0:T(8,128)S(1)}, f32[10,24,256]{2,1,0:T(8,128)S(1)}, f32[8,24,256]{2,1,0:T(8,128)S(1)}, f32[8,24,256]{2,1,0:T(8,128)S(1)}...) custom-call(f32[8,8,24,256]{3,2,1,0:T(8,128)S(1)} %get-tuple-element, ...), custom_call_target="tpu_custom_call", output_to_operand_aliasing={{0}: (0, {}), {1}: (1, {}), {2}: (2, {}), {3}: (3, {})} | custom-call | flops 2000000000 | tf_op jit(solution)/shard_map/pallas_call | solution.py:650
  23.2 1.9 %collective-permute-done.10.refs_15_ = f32[4,3,2,8,128]{4,3,2,1,0:T(8,128)S(1)} collective-permute-done((f32[4,3,2,8,128]{4,3,2,1,0:T(8,128)S(1)}, f32[4,3,2,8,128]{4,3,2,1,0:T(8,128)S(1)}, u32[]{:S(2)}, u32[]{:S(2)}) %collective-permute-start.10) | collective-permute-done | bytes 98336 | tf_op jit(solution)/shard_map/ppermute | solution.py:683
  25.1 1.8 %collective-permute-done.9.refs_14_ = f32[4,3,2,8,128]{4,3,2,1,0:T(8,128)S(1)} collective-permute-done((f32[4,3,2,8,128]{4,3,2,1,0:T(8,128)S(1)}, f32[4,3,2,8,128]{4,3,2,1,0:T(8,128)S(1)}, u32[]{:S(2)}, u32[]{:S(2)}) %collective-permute-start.9) | collective-permute-done | bytes 98336 | tf_op jit(solution)/shard_map/ppermute | solution.py:683
  26.9 2.0 %shard_map.52 = (f32[8,8,24,256]{3,2,1,0:T(8,128)S(1)}, f32[10,24,256]{2,1,0:T(8,128)S(1)}, f32[8,24,256]{2,1,0:T(8,128)S(1)}, f32[8,24,256]{2,1,0:T(8,128)S(1)}...) custom-call(f32[472,256]{1,0:T(8,128)S(1)} %collective-permute-done., ...), custom_call_target="tpu_custom_call", output_to_operand_aliasing={{0}: (1, {}), {1}: (2, {}), {2}: (3, {}), {3}: (4, {}), {4}... | custom-call | tf_op jit(solution)/shard_map/pallas_call | solution.py:650
  28.9 14.5 %all_to_all.5.fields = f32[16,2,2,8,128]{4,3,2,1,0:T(8,128)S(1)} all-to-all(f32[16,2,2,8,128]{4,3,2,1,0:T(8,128)S(1)} %get-tuple-element.78), channel_id=1, replica_groups=mesh['gx'=4,'gy'=4,'gz'=2] {'gx','gy'}, dimensions={0} | all-to-all | bytes 524288 | tf_op jit(solution)/shard_map/all_to_all | solution.py:715
  44.7 0.9 %collective-permute-done.11.other = f32[16,5,2,8,128]{4,3,2,1,0:T(8,128)S(1)} collective-permute-done((f32[16,5,2,8,128]{4,3,2,1,0:T(8,128)S(1)}, f32[16,5,2,8,128]{4,3,2,1,0:T(8,128)S(1)}, u32[]{:S(2)}, u32[]{:S(2)}) %collective-permute-start.11) | collective-permute-done | bytes 655392 | tf_op jit(solution)/shard_map/ppermute | solution.py:717
  45.6 3.2 %shard_map.54.u1 = f32[2,4,32,128]{3,2,1,0:T(8,128)S(1)} custom-call(f32[16,5,2,8,128]{4,3,2,1,0:T(8,128)S(1)} %shard_map.53.mine, f32[16,5,2,8,128]{4,3,2,1,0:T(8,128)S(1)} %collective-permute-done.11.other), custom_call_target="tpu_custom_call" | custom-call | flops 5000000000 | tf_op jit(solution)/shard_map/pallas_call | solution.py:650
  50.5 2.0 %collective-permute-start.16 = (f32[160,128]{1,0:T(8,128)S(1)}, f32[160,128]{1,0:T(8,128)S(1)}, u32[]{:S(2)}, u32[]{:S(2)}) collective-permute-start(f32[160,128]{1,0:T(8,128)S(1)} %get-tuple-element.86), channel_id=1, source_target_pairs={{0,6},{2,4},{4,2},{6,0},{1,7},{3,5},{5,3},{7,1},{8,14},{10,12},{12... | collective-permute-start | bytes 245768 | tf_op jit(solution)/shard_map/ppermute | solution.py:738
  52.5 1.3 %collective-permute-done.14.refs_1_ = f32[160,128]{1,0:T(8,128)S(1)} collective-permute-done((f32[160,128]{1,0:T(8,128)S(1)}, f32[160,128]{1,0:T(8,128)S(1)}, u32[]{:S(2)}, u32[]{:S(2)}) %collective-permute-start.14) | collective-permute-done | bytes 81952 | tf_op jit(solution)/shard_map/ppermute | solution.py:738
  53.9 1.0 %collective-permute-done.15.refs_2_ = f32[160,128]{1,0:T(8,128)S(1)} collective-permute-done((f32[160,128]{1,0:T(8,128)S(1)}, f32[160,128]{1,0:T(8,128)S(1)}, u32[]{:S(2)}, u32[]{:S(2)}) %collective-permute-start.15) | collective-permute-done | bytes 81952 | tf_op jit(solution)/shard_map/ppermute | solution.py:738
  54.9 1.9 %collective-permute-done.16.refs_3_ = f32[160,128]{1,0:T(8,128)S(1)} collective-permute-done((f32[160,128]{1,0:T(8,128)S(1)}, f32[160,128]{1,0:T(8,128)S(1)}, u32[]{:S(2)}, u32[]{:S(2)}) %collective-permute-start.16) | collective-permute-done | bytes 81952 | tf_op jit(solution)/shard_map/ppermute | solution.py:738
  56.8 2.5 %shard_map.56 = f32[2,2,4,4,16,128]{5,4,3,2,1,0:T(8,128)S(1)} custom-call(f32[160,128]{1,0:T(8,128)S(1)} %get-tuple-element.83.refs_0_, f32[160,128]{1,0:T(8,128)S(1)} %collective-permute-done.14.refs_1_, f32[160,128]{1,0:T(8,128)S(1)} %collective-permute-done.15.refs_2_, f32[160,128]{1,0:T(8,128)S(1)} %collective-permute-done.16.refs_3_, ...), custom_call_target="tpu_custom_call" | custom-call | tf_op jit(solution)/shard_map/pallas_call | solution.py:650
  59.5 1.5 %collective-permute-done.17.came = f32[2,4,4,16,128]{4,3,2,1,0:T(8,128)S(1)} collective-permute-done((f32[2,4,4,16,128]{4,3,2,1,0:T(8,128)S(1)}, f32[2,4,4,16,128]{4,3,2,1,0:T(8,128)S(1)}, u32[]{:S(2)}, u32[]{:S(2)}) %collective-permute-start.17) | collective-permute-done | bytes 262176 | tf_op jit(solution)/shard_map/ppermute | solution.py:745
  61.0 0.8 %shard_map.57 = f32[2,4,8,16,128]{4,3,2,1,0:T(8,128)} custom-call(f32[2,4,4,16,128]{4,3,2,1,0:T(8,128)S(1)} %get-tuple-element.96.kept, f32[2,4,4,16,128]{4,3,2,1,0:T(8,128)S(1)} %collective-permute-done.17.came), custom_call_target="tpu_custom_call" | custom-call | tf_op jit(solution)/shard_map/pallas_call | solution.py:650
  (26 shorter events, 6.3 us)
Async XLA Ops:
  1.2 1.8 %collective-permute-start = (f32[11,4,16,128]{3,2,1,0:T(8,128)S(1)}, f32[11,4,16,128]{3,2,1,0:T(8,128)S(1)}, u32[]{:S(2)}, u32[]{:S(2)}) collective-permute-start(f32[11,4,16,128]{3,2,1,0:T(8,128)S(1)} %get-tuple-element.51), channel_id=1, source_target_pairs={{0,1},{1,0},{2,3},{3,2},{4,5},{5,4},{6,7},{7,6},{8,9},{9,8},{10,11... | collective-permute-start | bytes 1081352 | tf_op jit(solution)/shard_map/ppermute | solution.py:676
  3.1 13.0 %collective-permute-start.1 = (f32[2,96,128]{2,1,0:T(8,128)S(1)}, f32[2,96,128]{2,1,0:T(8,128)S(1)}, u32[]{:S(2)}, u32[]{:S(2)}) collective-permute-start(f32[2,96,128]{2,1,0:T(8,128)S(1)} %get-tuple-element.52), channel_id=1, source_target_pairs={{0,2},{2,0},{4,6},{6,4},{1,3},{3,1},{5,7},{7,5},{8,10},{10,8},{12,... | collective-permute-start | bytes 294920 | tf_op jit(solution)/shard_map/ppermute | solution.py:690
  6.1 10.1 %collective-permute-start.2 = (f32[2,96,128]{2,1,0:T(8,128)S(1)}, f32[2,96,128]{2,1,0:T(8,128)S(1)}, u32[]{:S(2)}, u32[]{:S(2)}) collective-permute-start(f32[2,96,128]{2,1,0:T(8,128)S(1)} %get-tuple-element.53), channel_id=1, source_target_pairs={{0,6},{2,4},{4,2},{6,0},{1,7},{3,5},{5,3},{7,1},{8,14},{10,12},{12... | collective-permute-start | bytes 294920 | tf_op jit(solution)/shard_map/ppermute | solution.py:691
  7.8 5.9 %collective-permute-start.5 = (f32[3,2,8,128]{3,2,1,0:T(8,128)S(1)}, f32[3,2,8,128]{3,2,1,0:T(8,128)S(1)}, u32[]{:S(2)}, u32[]{:S(2)}) collective-permute-start(f32[3,2,8,128]{3,2,1,0:T(8,128)S(1)} %shard_map.48.refs_0_), channel_id=1, source_target_pairs={{0,24},{8,16},{16,8},{24,0},{1,25},{9,17},{17,9},{25,1},{2,26},{10... | collective-permute-start | bytes 73736 | tf_op jit(solution)/shard_map/ppermute | solution.py:683
  11.4 4.7 %collective-permute-start.4 = (f32[3,2,8,128]{3,2,1,0:T(8,128)S(1)}, f32[3,2,8,128]{3,2,1,0:T(8,128)S(1)}, u32[]{:S(2)}, u32[]{:S(2)}) collective-permute-start(f32[3,2,8,128]{3,2,1,0:T(8,128)S(1)} %shard_map.48.refs_0_), channel_id=1, source_target_pairs={{0,16},{8,24},{16,0},{24,8},{1,17},{9,25},{17,1},{25,9},{2,18},{10... | collective-permute-start | bytes 73736 | tf_op jit(solution)/shard_map/ppermute | solution.py:683
  11.4 4.7 %collective-permute-start.3 = (f32[3,2,8,128]{3,2,1,0:T(8,128)S(1)}, f32[3,2,8,128]{3,2,1,0:T(8,128)S(1)}, u32[]{:S(2)}, u32[]{:S(2)}) collective-permute-start(f32[3,2,8,128]{3,2,1,0:T(8,128)S(1)} %shard_map.48.refs_0_), channel_id=1, source_target_pairs={{0,8},{8,0},{16,24},{24,16},{1,9},{9,1},{17,25},{25,17},{2,10},{10... | collective-permute-start | bytes 73736 | tf_op jit(solution)/shard_map/ppermute | solution.py:683
  16.5 1.9 %collective-permute-start.7 = (f32[472,256]{1,0:T(8,128)S(1)}, f32[472,256]{1,0:T(8,128)S(1)}, u32[]{:S(2)}, u32[]{:S(2)}) collective-permute-start(f32[472,256]{1,0:T(8,128)S(1)} %get-tuple-element.55), channel_id=1, source_target_pairs={{0,1},{1,0},{2,3},{3,2},{4,5},{5,4},{6,7},{7,6},{8,9},{9,8},{10,11... | collective-permute-start | bytes 1449992 | tf_op jit(solution)/shard_map/ppermute | solution.py:698
  16.6 6.6 %collective-permute-start.6 = (f32[472,256]{1,0:T(8,128)S(1)}, f32[472,256]{1,0:T(8,128)S(1)}, u32[]{:S(2)}, u32[]{:S(2)}) collective-permute-start(f32[472,256]{1,0:T(8,128)S(1)} %get-tuple-element.54), channel_id=1, source_target_pairs={{1,8},{8,1},{9,16},{16,9},{17,24},{24,17},{3,10},{10,3},{11,18},{1... | collective-permute-start | bytes 1449992 | tf_op jit(solution)/shard_map/ppermute | solution.py:697
  18.5 6.6 %collective-permute-start.10 = (f32[4,3,2,8,128]{4,3,2,1,0:T(8,128)S(1)}, f32[4,3,2,8,128]{4,3,2,1,0:T(8,128)S(1)}, u32[]{:S(2)}, u32[]{:S(2)}) collective-permute-start(f32[4,3,2,8,128]{4,3,2,1,0:T(8,128)S(1)} %get-tuple-element.77.refs_12_), channel_id=1, source_target_pairs={{0,6},{2,4},{4,2},{6,0},{1,7},{3,5},{5,3},{7,1},{8,14},{10,12},{12... | collective-permute-start | bytes 294920 | tf_op jit(solution)/shard_map/ppermute | solution.py:683
  20.0 6.9 %collective-permute-start.9 = (f32[4,3,2,8,128]{4,3,2,1,0:T(8,128)S(1)}, f32[4,3,2,8,128]{4,3,2,1,0:T(8,128)S(1)}, u32[]{:S(2)}, u32[]{:S(2)}) collective-permute-start(f32[4,3,2,8,128]{4,3,2,1,0:T(8,128)S(1)} %get-tuple-element.77.refs_12_), channel_id=1, source_target_pairs={{0,4},{2,6},{4,0},{6,2},{1,5},{3,7},{5,1},{7,3},{8,12},{10,14},{12... | collective-permute-start | bytes 294920 | tf_op jit(solution)/shard_map/ppermute | solution.py:683
  21.5 5.3 %collective-permute-start.8 = (f32[4,3,2,8,128]{4,3,2,1,0:T(8,128)S(1)}, f32[4,3,2,8,128]{4,3,2,1,0:T(8,128)S(1)}, u32[]{:S(2)}, u32[]{:S(2)}) collective-permute-start(f32[4,3,2,8,128]{4,3,2,1,0:T(8,128)S(1)} %get-tuple-element.77.refs_12_), channel_id=1, source_target_pairs={{0,2},{2,0},{4,6},{6,4},{1,3},{3,1},{5,7},{7,5},{8,10},{10,8},{12,... | collective-permute-start | bytes 294920 | tf_op jit(solution)/shard_map/ppermute | solution.py:683
  43.5 2.2 %collective-permute-start.11 = (f32[16,5,2,8,128]{4,3,2,1,0:T(8,128)S(1)}, f32[16,5,2,8,128]{4,3,2,1,0:T(8,128)S(1)}, u32[]{:S(2)}, u32[]{:S(2)}) collective-permute-start(f32[16,5,2,8,128]{4,3,2,1,0:T(8,128)S(1)} %shard_map.53.mine), channel_id=1, source_target_pairs={{0,1},{1,0},{2,3},{3,2},{4,5},{5,4},{6,7},{7,6},{8,9},{9,8},{10,11... | collective-permute-start | bytes 1966088 | tf_op jit(solution)/shard_map/ppermute | solution.py:717
  43.5 5.3 %collective-permute-start.12 = (f32[8,16,256]{2,1,0:T(8,128)S(1)}, f32[8,16,256]{2,1,0:T(8,128)S(1)}, u32[]{:S(2)}, u32[]{:S(2)}) collective-permute-start(f32[8,16,256]{2,1,0:T(8,128)S(1)} %get-tuple-element.81), channel_id=1, source_target_pairs={{0,1},{1,0},{2,3},{3,2},{4,5},{5,4},{6,7},{7,6},{8,9},{9,8},{10,11... | collective-permute-start | bytes 393224 | tf_op jit(solution)/shard_map/ppermute | solution.py:714
  44.0 4.9 %collective-permute-start.13 = (f32[8,16,256]{2,1,0:T(8,128)S(1)}, f32[8,16,256]{2,1,0:T(8,128)S(1)}, u32[]{:S(2)}, u32[]{:S(2)}) collective-permute-start(f32[8,16,256]{2,1,0:T(8,128)S(1)} %get-tuple-element.82), channel_id=1, source_target_pairs={{1,8},{8,1},{9,16},{16,9},{17,24},{24,17},{3,10},{10,3},{11,18},{1... | collective-permute-start | bytes 393224 | tf_op jit(solution)/shard_map/ppermute | solution.py:713
  49.0 4.9 %collective-permute-start.14 = (f32[160,128]{1,0:T(8,128)S(1)}, f32[160,128]{1,0:T(8,128)S(1)}, u32[]{:S(2)}, u32[]{:S(2)}) collective-permute-start(f32[160,128]{1,0:T(8,128)S(1)} %get-tuple-element.84), channel_id=1, source_target_pairs={{0,2},{2,0},{4,6},{6,4},{1,3},{3,1},{5,7},{7,5},{8,10},{10,8},{12,... | collective-permute-start | bytes 245768 | tf_op jit(solution)/shard_map/ppermute | solution.py:738
  49.8 5.1 %collective-permute-start.15 = (f32[160,128]{1,0:T(8,128)S(1)}, f32[160,128]{1,0:T(8,128)S(1)}, u32[]{:S(2)}, u32[]{:S(2)}) collective-permute-start(f32[160,128]{1,0:T(8,128)S(1)} %get-tuple-element.85), channel_id=1, source_target_pairs={{0,4},{2,6},{4,0},{6,2},{1,5},{3,7},{5,1},{7,3},{8,12},{10,14},{12... | collective-permute-start | bytes 245768 | tf_op jit(solution)/shard_map/ppermute | solution.py:738
  50.5 6.3 %collective-permute-start.16 = (f32[160,128]{1,0:T(8,128)S(1)}, f32[160,128]{1,0:T(8,128)S(1)}, u32[]{:S(2)}, u32[]{:S(2)}) collective-permute-start(f32[160,128]{1,0:T(8,128)S(1)} %get-tuple-element.86), channel_id=1, source_target_pairs={{0,6},{2,4},{4,2},{6,0},{1,7},{3,5},{5,3},{7,1},{8,14},{10,12},{12... | collective-permute-start | bytes 245768 | tf_op jit(solution)/shard_map/ppermute | solution.py:738
  59.4 1.6 %collective-permute-start.17 = (f32[2,4,4,16,128]{4,3,2,1,0:T(8,128)S(1)}, f32[2,4,4,16,128]{4,3,2,1,0:T(8,128)S(1)}, u32[]{:S(2)}, u32[]{:S(2)}) collective-permute-start(f32[2,4,4,16,128]{4,3,2,1,0:T(8,128)S(1)} %get-tuple-element.95), channel_id=1, source_target_pairs={{0,1},{1,0},{2,3},{3,2},{4,5},{5,4},{6,7},{7,6},{8,9},{9,8},{10,11... | collective-permute-start | bytes 786440 | tf_op jit(solution)/shard_map/ppermute | solution.py:745

commit v7 on v6

--- a/solution.py
+++ b/solution.py
@@ -125,6 +125,7 @@
 MIB = 1 << 20
 COARSE_COST = 5 * 10**9
 NEAR_COST = 2 * 10**9
+JOIN_COST = 10**9
 F32 = jnp.float32
 
 
@@ -258,11 +259,11 @@
     to_odd[...] = ends[even]
 
 
-def means_kernel(kept, came, out, slots, sums):
+def means_kernel(kept, away, out, slots, sums):
     k = lax.axis_index("gz")
     fields, half, rows, lanes = kept.shape
     pairs = half // 2
-    for t, ref in enumerate((kept, came)):
+    for t, ref in enumerate((kept, away)):
         for j in range(3):
             for q in range(pairs):
                 at = (j * pairs + q) * rows
@@ -280,9 +281,15 @@
         out[pl.ds((me ^ v) * n, n)] = ref[...].reshape((n,) + out.shape[1:])
 
 
+def double_kernel(level, mine, other, out):
+    bit = lax.rem(lax.axis_index("gx") // level, 2)
+    out[pl.ds(bit * level, level)] = mine[...].reshape((level,) + out.shape[1:])
+    out[pl.ds((1 - bit) * level, level)] = other[...].reshape((level,) + out.shape[1:])
+
+
 def lay_kernel(kept, came, even, odd, *refs):
-    *means, g, rho, sr, si, to_gz, to_gx, joined, ends = refs
-    join("gx", means, joined)
+    means, other, g, rho, sr, si, to_gz, to_gx, joined, ends = refs
+    double_kernel(joined.shape[0] // 2, means, other, joined)
     k = lax.axis_index("gz")
     y = lax.axis_index("gy")
     fields, half, rows, lanes = kept.shape
@@ -431,14 +438,28 @@
         out[e, 2:] = means[y * chips + x]
 
 
-def put_coarse(mine, other, refs, offsets, parts, skip):
+def put_means(mine, other, refs, offsets, parts, skip):
+    k = lax.axis_index("gz")
+    _, _, pairs, rows, lanes = mine.shape
+    first = lax.broadcasted_iota(jnp.int32, (pairs, rows, lanes), 2) < lanes // 2
+    for e in range(mine.shape[0]):
+        s, y = divmod(e, parts)
+        for j, ref in enumerate(refs):
+            a, b = mine[e, skip + j], other[e, skip + j]
+            low, high = jnp.where(k == 0, a, b), jnp.where(k == 0, b, a)
+            for h, whole in enumerate((jnp.where(first, low, pltpu.roll(high, lanes // 2, 2)), jnp.where(first, pltpu.roll(low, lanes // 2, 2), high))):
+                at = 2 * pairs * s + pairs * h + offsets[j]
+                ref[at : at + pairs, y * rows : (y + 1) * rows] = whole
+
+
+def put_coarse(mine, other, refs, offsets, parts):
     k = lax.axis_index("gz")
     _, _, pairs, rows, _ = mine.shape
     for e in range(mine.shape[0]):
         s, y = divmod(e, parts)
         for came, z in ((mine, k), (other, 1 - k)):
             for j, ref in enumerate(refs):
-                ref[pl.ds(2 * pairs * s + pairs * z + offsets[j], pairs), y * rows : (y + 1) * rows] = came[e, skip + j]
+                ref[pl.ds(2 * pairs * s + pairs * z + offsets[j], pairs), y * rows : (y + 1) * rows] = came[e, j]
 
 
 def halve(sums, narrow, ny, count, total, values):
@@ -458,7 +479,7 @@
     zero = jnp.zeros((1, ny, nz), F32)
     rho1[pl.ds(0, 1)] = zero
     rho1[pl.ds(n1 + 1, 1)] = zero
-    put_coarse(mine, other, (rho1, sr1, si1), (1, 0, 0), ny // mine.shape[3], 2)
+    put_means(mine, other, (rho1, sr1, si1), (1, 0, 0), ny // mine.shape[3], 2)
     level_coefs(rho1, sr1, si1, 0.25, bx1, by1, bz1, wr1, wi1, dr1, 8, 0, n1)
     n2, ny2 = sr2.shape[:2]
     halve(sums, narrow, ny, 3, n2, lambda q: (rho1[2 * q + 1] + rho1[2 * q + 2], sr1[2 * q] + sr1[2 * q + 1], si1[2 * q] + si1[2 * q + 1]))
@@ -482,7 +503,7 @@
         for c in range(2):
             u[c, pl.ds(0, 1)] = zero
             u[c, pl.ds(n1 + 1, 1)] = zero
-    put_coarse(mine, other, (g1.at[0], g1.at[1]), (0, 0), ny // mine.shape[3], 0)
+    put_coarse(mine, other, (g1.at[0], g1.at[1]), (0, 0), ny // mine.shape[3])
     step1 = 4
     coefs1 = (bx1, by1, bz1, wr1, wi1)
 
@@ -677,12 +698,17 @@
     pairs = half // 2
     means = (3, pairs, rows // 2, lanes)
     n = 3 * pairs * rows
-    coarse = call(means_kernel, means, (kept, came), scratch=[(n, lanes), (2, n // 2, lanes)])
+    coarse = call(means_kernel, means, (kept, away), scratch=[(n, lanes), (2, n // 2, lanes)])
 
     def spread(array, axis, count):
         return [lax.ppermute(array, axis, [(i, i ^ v) for i in range(count)]) if v else array for v in range(count)]
 
-    coarse = spread(coarse, "gx", chips)
+    level = 1
+    while level < chips:
+        coarse = (coarse, lax.ppermute(coarse, "gx", [(i, i ^ level) for i in range(chips)]))
+        level *= 2
+        if level < chips:
+            coarse = call(functools.partial(double_kernel, level // 2), (level, *means), coarse, cost=JOIN_COST)
 
     rim = ((2 * m + 3) * HALO + 1) * half
     rim = (2, -(-rim // 8) * 8, lanes)

time: 62 us -> 60 us (0.968)
  waiting for transfers between devices: 16.8 us -> 14.2 us
  blocking collectives: 14.5 us -> 15.5 us
    ppermute x0 -> x2, starting transfers between devices: none -> 5.3 us  [local_planes(): lax.ppermute(coarse, 'gx', [(i, i ^ level) for i in range(chips)])]
    ppermute x6 -> x3, starting transfers between devices: 8 us -> 3.55 us  [spread(): lax.ppermute(array, axis, [(i, i ^ v) for i in range(count)])]
    ppermute x6 -> x3, waiting for transfers between devices: 7.65 us -> 4.04 us  [spread(): lax.ppermute(array, axis, [(i, i ^ v) for i in range(count)])]
    ppermute x0 -> x2, waiting for transfers between devices: none -> 2.4 us  [local_planes(): lax.ppermute(coarse, 'gx', [(i, i ^ level) for i in range(chips)])]
    ppermute x1, starting transfers between devices: 2.92 us -> 1.56 us  [local_planes(): even = lax.ppermute(to_even, 'gy', [(i, i ^ 1) for i in range(m)])]
    ppermute x1, waiting for transfers between devices: 1.3 us -> 0.01 us  [local_planes(): came = lax.ppermute(away, 'gz', swap)]
    all_to_all x1, blocking collectives: 14.5 us -> 15.5 us  [local_planes(): mine = lax.all_to_all(packed, ('gx', 'gy'), 0, 0, tiled=True)]
    pallas_call x12 -> x13, Pallas kernels: 11.8 us -> 11.8 us  [call(): pl.pallas_call(kernel, out_shape=[jax.ShapeDtypeStruct(s, F32) for s in s...]
  transfers between devices with their start and end apart: 18 -> 17, of which waited for: 11 -> 9; matrix products, arithmetic and copies ran while one was open for 0% -> 0% of each run, Pallas kernels for 7% -> 8%
where the time goes in v7:
time: 60 us; the launch traced here: 59.8 us
  starting transfers between devices  18.1 us (30%)
  blocking collectives  15.5 us (26%)
  waiting for transfers between devices  14.2 us (24%)
  Pallas kernels  11.8 us (20%)
    all_to_all x1, blocking collectives, local_planes(): mine = lax.all_to_all(packed, ('gx', 'gy'), 0, 0, tiled=True)  15.5 us
    pallas_call x13, Pallas kernels, call(): pl.pallas_call(kernel, out_shape=[jax.ShapeDtypeStruct(s, F32) for s in s...  11.8 us
    ppermute x2, starting transfers between devices, local_planes(): lax.ppermute(coarse, 'gx', [(i, i ^ level) for i in range(chips)])  5.3 us
    ppermute x3, waiting for transfers between devices, local_planes(): lax.ppermute(b, 'gy', [(i, i ^ v) for i in range(m)])  4.22 us
    ppermute x3, waiting for transfers between devices, spread(): lax.ppermute(array, axis, [(i, i ^ v) for i in range(count)])  4.04 us
    ppermute x3, starting transfers between devices, spread(): lax.ppermute(array, axis, [(i, i ^ v) for i in range(count)])  3.55 us
    ppermute x3, starting transfers between devices, local_planes(): lax.ppermute(b, 'gy', [(i, i ^ v) for i in range(m)])  3.55 us
    ppermute x2, waiting for transfers between devices, local_planes(): lax.ppermute(coarse, 'gx', [(i, i ^ level) for i in range(chips)])  2.4 us
  transfers between devices with their start and end apart: 17, of which 9 were waited for; matrix products, arithmetic and copies ran while one was open for 0% of the time, Pallas kernels for 8%

profile of v7, /device:TPU:0, one launch (start us, length us, event | category | flops | bytes accessed | tf_op | source)
XLA Modules:
  0.0 59.8 jit_solution(2578034764842316137)
XLA Ops:
  0.0 1.2 %shard_map.46 = (f32[11,4,16,128]{3,2,1,0:T(8,128)S(1)}, f32[11,4,16,128]{3,2,1,0:T(8,128)S(1)}) custom-call(f32[2,4,8,16,128]{4,3,2,1,0:T(8,128)} %rhs.1, f32[8,16,128]{2,1,0:T(8,128)} %rho.1, f32[8,16,128]{2,1,0:T(8,128)} %sr.1, f32[8,16,128]{2,1,0:T(8,128)} %si.1), custom_call_target="tpu_custom_call" | custom-call | tf_op jit(solution)/shard_map/pallas_call | solution.py:671
  1.9 2.6 %collective-permute-start.3 = (f32[3,2,8,128]{3,2,1,0:T(8,128)S(1)}, f32[3,2,8,128]{3,2,1,0:T(8,128)S(1)}, u32[]{:S(2)}, u32[]{:S(2)}) collective-permute-start(f32[3,2,8,128]{3,2,1,0:T(8,128)S(1)} %shard_map.48.mine), channel_id=1, source_target_pairs={{0,8},{8,0},{16,24},{24,16},{1,9},{9,1},{17,25},{25,17},{2,10},{10... | collective-permute-start | bytes 73736 | tf_op jit(solution)/shard_map/ppermute | solution.py:708
  4.7 1.6 %collective-permute-start.1 = (f32[2,96,128]{2,1,0:T(8,128)S(1)}, f32[2,96,128]{2,1,0:T(8,128)S(1)}, u32[]{:S(2)}, u32[]{:S(2)}) collective-permute-start(f32[2,96,128]{2,1,0:T(8,128)S(1)} %get-tuple-element.52), channel_id=1, source_target_pairs={{0,2},{2,0},{4,6},{6,4},{1,3},{3,1},{5,7},{7,5},{8,10},{10,8},{12,... | collective-permute-start | bytes 294920 | tf_op jit(solution)/shard_map/ppermute | solution.py:716
  6.2 1.5 %collective-permute-start.2 = (f32[2,96,128]{2,1,0:T(8,128)S(1)}, f32[2,96,128]{2,1,0:T(8,128)S(1)}, u32[]{:S(2)}, u32[]{:S(2)}) collective-permute-start(f32[2,96,128]{2,1,0:T(8,128)S(1)} %get-tuple-element.53), channel_id=1, source_target_pairs={{0,6},{2,4},{4,2},{6,0},{1,7},{3,5},{5,3},{7,1},{8,14},{10,12},{12... | collective-permute-start | bytes 294920 | tf_op jit(solution)/shard_map/ppermute | solution.py:717
  7.7 2.7 %collective-permute-start.4 = (f32[2,3,2,8,128]{4,3,2,1,0:T(8,128)S(1)}, f32[2,3,2,8,128]{4,3,2,1,0:T(8,128)S(1)}, u32[]{:S(2)}, u32[]{:S(2)}) collective-permute-start(f32[2,3,2,8,128]{4,3,2,1,0:T(8,128)S(1)} %shard_map.49.refs_0_), channel_id=1, source_target_pairs={{0,16},{8,24},{16,0},{24,8},{1,17},{9,25},{17,1},{25,9},{2,18},{10... | collective-permute-start | bytes 147464 | tf_op jit(solution)/shard_map/ppermute | solution.py:708
  10.4 2.4 %collective-permute-done.4.refs_1_ = f32[2,3,2,8,128]{4,3,2,1,0:T(8,128)S(1)} collective-permute-done((f32[2,3,2,8,128]{4,3,2,1,0:T(8,128)S(1)}, f32[2,3,2,8,128]{4,3,2,1,0:T(8,128)S(1)}, u32[]{:S(2)}, u32[]{:S(2)}) %collective-permute-start.4) | collective-permute-done | bytes 49184 | tf_op jit(solution)/shard_map/ppermute | solution.py:708
  13.9 1.1 %collective-permute-done.6.from_gz = f32[472,256]{1,0:T(8,128)S(1)} collective-permute-done((f32[472,256]{1,0:T(8,128)S(1)}, f32[472,256]{1,0:T(8,128)S(1)}, u32[]{:S(2)}, u32[]{:S(2)}) %collective-permute-start.6) | collective-permute-done | bytes 483360 | tf_op jit(solution)/shard_map/ppermute | solution.py:724
  15.1 1.6 %collective-permute-start.9 = (f32[4,3,2,8,128]{4,3,2,1,0:T(8,128)S(1)}, f32[4,3,2,8,128]{4,3,2,1,0:T(8,128)S(1)}, u32[]{:S(2)}, u32[]{:S(2)}) collective-permute-start(f32[4,3,2,8,128]{4,3,2,1,0:T(8,128)S(1)} %get-tuple-element.77.refs_12_), channel_id=1, source_target_pairs={{0,6},{2,4},{4,2},{6,0},{1,7},{3,5},{5,3},{7,1},{8,14},{10,12},{12... | collective-permute-start | bytes 294920 | tf_op jit(solution)/shard_map/ppermute | solution.py:704
  16.7 1.5 %collective-permute-start.8 = (f32[4,3,2,8,128]{4,3,2,1,0:T(8,128)S(1)}, f32[4,3,2,8,128]{4,3,2,1,0:T(8,128)S(1)}, u32[]{:S(2)}, u32[]{:S(2)}) collective-permute-start(f32[4,3,2,8,128]{4,3,2,1,0:T(8,128)S(1)} %get-tuple-element.77.refs_12_), channel_id=1, source_target_pairs={{0,4},{2,6},{4,0},{6,2},{1,5},{3,7},{5,1},{7,3},{8,12},{10,14},{12... | collective-permute-start | bytes 294920 | tf_op jit(solution)/shard_map/ppermute | solution.py:704
  18.7 1.1 %shard_map.52 = (f32[8,8,24,256]{3,2,1,0:T(8,128)S(1)}, f32[10,24,256]{2,1,0:T(8,128)S(1)}, f32[8,24,256]{2,1,0:T(8,128)S(1)}, f32[8,24,256]{2,1,0:T(8,128)S(1)}...) custom-call(f32[8,8,24,256]{3,2,1,0:T(8,128)S(1)} %get-tuple-element, ...), custom_call_target="tpu_custom_call", output_to_operand_aliasing={{0}: (0, {}), {1}: (1, {}), {2}: (2, {}), {3}: (3, {})} | custom-call | flops 2000000000 | tf_op jit(solution)/shard_map/pallas_call | solution.py:671
  19.8 1.5 %collective-permute-done.9.refs_15_ = f32[4,3,2,8,128]{4,3,2,1,0:T(8,128)S(1)} collective-permute-done((f32[4,3,2,8,128]{4,3,2,1,0:T(8,128)S(1)}, f32[4,3,2,8,128]{4,3,2,1,0:T(8,128)S(1)}, u32[]{:S(2)}, u32[]{:S(2)}) %collective-permute-start.9) | collective-permute-done | bytes 98336 | tf_op jit(solution)/shard_map/ppermute | solution.py:704
  21.3 2.6 %collective-permute-done.8.refs_14_ = f32[4,3,2,8,128]{4,3,2,1,0:T(8,128)S(1)} collective-permute-done((f32[4,3,2,8,128]{4,3,2,1,0:T(8,128)S(1)}, f32[4,3,2,8,128]{4,3,2,1,0:T(8,128)S(1)}, u32[]{:S(2)}, u32[]{:S(2)}) %collective-permute-start.8) | collective-permute-done | bytes 98336 | tf_op jit(solution)/shard_map/ppermute | solution.py:704
  23.8 2.0 %shard_map.53 = (f32[8,8,24,256]{3,2,1,0:T(8,128)S(1)}, f32[10,24,256]{2,1,0:T(8,128)S(1)}, f32[8,24,256]{2,1,0:T(8,128)S(1)}, f32[8,24,256]{2,1,0:T(8,128)S(1)}...) custom-call(f32[472,256]{1,0:T(8,128)S(1)} %collective-permute-done., ...), custom_call_target="tpu_custom_call", output_to_operand_aliasing={{0}: (1, {}), {1}: (2, {}), {2}: (3, {}), {3}: (4, {}), {4}... | custom-call | tf_op jit(solution)/shard_map/pallas_call | solution.py:671
  25.9 15.5 %all_to_all.5.fields = f32[16,2,2,8,128]{4,3,2,1,0:T(8,128)S(1)} all-to-all(f32[16,2,2,8,128]{4,3,2,1,0:T(8,128)S(1)} %get-tuple-element.78), channel_id=1, replica_groups=mesh['gx'=4,'gy'=4,'gz'=2] {'gx','gy'}, dimensions={0} | all-to-all | bytes 524288 | tf_op jit(solution)/shard_map/all_to_all | solution.py:741
  42.7 0.9 %collective-permute-done.10.other = f32[16,5,2,8,128]{4,3,2,1,0:T(8,128)S(1)} collective-permute-done((f32[16,5,2,8,128]{4,3,2,1,0:T(8,128)S(1)}, f32[16,5,2,8,128]{4,3,2,1,0:T(8,128)S(1)}, u32[]{:S(2)}, u32[]{:S(2)}) %collective-permute-start.10) | collective-permute-done | bytes 655392 | tf_op jit(solution)/shard_map/ppermute | solution.py:743
  43.6 3.3 %shard_map.55.u1 = f32[2,4,32,128]{3,2,1,0:T(8,128)S(1)} custom-call(f32[16,5,2,8,128]{4,3,2,1,0:T(8,128)S(1)} %shard_map.54.mine, f32[16,5,2,8,128]{4,3,2,1,0:T(8,128)S(1)} %collective-permute-done.10.other), custom_call_target="tpu_custom_call" | custom-call | flops 5000000000 | tf_op jit(solution)/shard_map/pallas_call | solution.py:671
  47.0 0.8 %collective-permute-start.13 = (f32[160,128]{1,0:T(8,128)S(1)}, f32[160,128]{1,0:T(8,128)S(1)}, u32[]{:S(2)}, u32[]{:S(2)}) collective-permute-start(f32[160,128]{1,0:T(8,128)S(1)} %get-tuple-element.84), channel_id=1, source_target_pairs={{0,2},{2,0},{4,6},{6,4},{1,3},{3,1},{5,7},{7,5},{8,10},{10,8},{12,... | collective-permute-start | bytes 245768 | tf_op jit(solution)/shard_map/ppermute | solution.py:764
  48.6 2.0 %collective-permute-start.15 = (f32[160,128]{1,0:T(8,128)S(1)}, f32[160,128]{1,0:T(8,128)S(1)}, u32[]{:S(2)}, u32[]{:S(2)}) collective-permute-start(f32[160,128]{1,0:T(8,128)S(1)} %get-tuple-element.86), channel_id=1, source_target_pairs={{0,6},{2,4},{4,2},{6,0},{1,7},{3,5},{5,3},{7,1},{8,14},{10,12},{12... | collective-permute-start | bytes 245768 | tf_op jit(solution)/shard_map/ppermute | solution.py:764
  50.6 1.3 %collective-permute-done.13.refs_1_ = f32[160,128]{1,0:T(8,128)S(1)} collective-permute-done((f32[160,128]{1,0:T(8,128)S(1)}, f32[160,128]{1,0:T(8,128)S(1)}, u32[]{:S(2)}, u32[]{:S(2)}) %collective-permute-start.13) | collective-permute-done | bytes 81952 | tf_op jit(solution)/shard_map/ppermute | solution.py:764
  51.9 1.1 %collective-permute-done.14.refs_2_ = f32[160,128]{1,0:T(8,128)S(1)} collective-permute-done((f32[160,128]{1,0:T(8,128)S(1)}, f32[160,128]{1,0:T(8,128)S(1)}, u32[]{:S(2)}, u32[]{:S(2)}) %collective-permute-start.14) | collective-permute-done | bytes 81952 | tf_op jit(solution)/shard_map/ppermute | solution.py:764
  53.0 1.8 %collective-permute-done.15.refs_3_ = f32[160,128]{1,0:T(8,128)S(1)} collective-permute-done((f32[160,128]{1,0:T(8,128)S(1)}, f32[160,128]{1,0:T(8,128)S(1)}, u32[]{:S(2)}, u32[]{:S(2)}) %collective-permute-start.15) | collective-permute-done | bytes 81952 | tf_op jit(solution)/shard_map/ppermute | solution.py:764
  54.8 2.5 %shard_map.57 = f32[2,2,4,4,16,128]{5,4,3,2,1,0:T(8,128)S(1)} custom-call(f32[160,128]{1,0:T(8,128)S(1)} %get-tuple-element.83.refs_0_, f32[160,128]{1,0:T(8,128)S(1)} %collective-permute-done.13.refs_1_, f32[160,128]{1,0:T(8,128)S(1)} %collective-permute-done.14.refs_2_, f32[160,128]{1,0:T(8,128)S(1)} %collective-permute-done.15.refs_3_, ...), custom_call_target="tpu_custom_call" | custom-call | tf_op jit(solution)/shard_map/pallas_call | solution.py:671
  57.5 1.5 %collective-permute-done.16.came = f32[2,4,4,16,128]{4,3,2,1,0:T(8,128)S(1)} collective-permute-done((f32[2,4,4,16,128]{4,3,2,1,0:T(8,128)S(1)}, f32[2,4,4,16,128]{4,3,2,1,0:T(8,128)S(1)}, u32[]{:S(2)}, u32[]{:S(2)}) %collective-permute-start.16) | collective-permute-done | bytes 262176 | tf_op jit(solution)/shard_map/ppermute | solution.py:771
  59.0 0.8 %shard_map.58 = f32[2,4,8,16,128]{4,3,2,1,0:T(8,128)} custom-call(f32[2,4,4,16,128]{4,3,2,1,0:T(8,128)S(1)} %get-tuple-element.96.kept, f32[2,4,4,16,128]{4,3,2,1,0:T(8,128)S(1)} %collective-permute-done.16.came), custom_call_target="tpu_custom_call" | custom-call | tf_op jit(solution)/shard_map/pallas_call | solution.py:671
  (25 shorter events, 4.7 us)
Async XLA Ops:
  1.2 3.4 %collective-permute-start = (f32[11,4,16,128]{3,2,1,0:T(8,128)S(1)}, f32[11,4,16,128]{3,2,1,0:T(8,128)S(1)}, u32[]{:S(2)}, u32[]{:S(2)}) collective-permute-start(f32[11,4,16,128]{3,2,1,0:T(8,128)S(1)} %get-tuple-element.51.away), channel_id=1, source_target_pairs={{0,1},{1,0},{2,3},{3,2},{4,5},{5,4},{6,7},{7,6},{8,9},{9,8},{10,11... | collective-permute-start | bytes 1081352 | tf_op jit(solution)/shard_map/ppermute | solution.py:697
  1.9 5.8 %collective-permute-start.3 = (f32[3,2,8,128]{3,2,1,0:T(8,128)S(1)}, f32[3,2,8,128]{3,2,1,0:T(8,128)S(1)}, u32[]{:S(2)}, u32[]{:S(2)}) collective-permute-start(f32[3,2,8,128]{3,2,1,0:T(8,128)S(1)} %shard_map.48.mine), channel_id=1, source_target_pairs={{0,8},{8,0},{16,24},{24,16},{1,9},{9,1},{17,25},{25,17},{2,10},{10... | collective-permute-start | bytes 73736 | tf_op jit(solution)/shard_map/ppermute | solution.py:708
  4.7 8.1 %collective-permute-start.1 = (f32[2,96,128]{2,1,0:T(8,128)S(1)}, f32[2,96,128]{2,1,0:T(8,128)S(1)}, u32[]{:S(2)}, u32[]{:S(2)}) collective-permute-start(f32[2,96,128]{2,1,0:T(8,128)S(1)} %get-tuple-element.52), channel_id=1, source_target_pairs={{0,2},{2,0},{4,6},{6,4},{1,3},{3,1},{5,7},{7,5},{8,10},{10,8},{12,... | collective-permute-start | bytes 294920 | tf_op jit(solution)/shard_map/ppermute | solution.py:716
  6.2 6.6 %collective-permute-start.2 = (f32[2,96,128]{2,1,0:T(8,128)S(1)}, f32[2,96,128]{2,1,0:T(8,128)S(1)}, u32[]{:S(2)}, u32[]{:S(2)}) collective-permute-start(f32[2,96,128]{2,1,0:T(8,128)S(1)} %get-tuple-element.53), channel_id=1, source_target_pairs={{0,6},{2,4},{4,2},{6,0},{1,7},{3,5},{5,3},{7,1},{8,14},{10,12},{12... | collective-permute-start | bytes 294920 | tf_op jit(solution)/shard_map/ppermute | solution.py:717
  7.7 5.1 %collective-permute-start.4 = (f32[2,3,2,8,128]{4,3,2,1,0:T(8,128)S(1)}, f32[2,3,2,8,128]{4,3,2,1,0:T(8,128)S(1)}, u32[]{:S(2)}, u32[]{:S(2)}) collective-permute-start(f32[2,3,2,8,128]{4,3,2,1,0:T(8,128)S(1)} %shard_map.49.refs_0_), channel_id=1, source_target_pairs={{0,16},{8,24},{16,0},{24,8},{1,17},{9,25},{17,1},{25,9},{2,18},{10... | collective-permute-start | bytes 147464 | tf_op jit(solution)/shard_map/ppermute | solution.py:708
  13.2 1.9 %collective-permute-start.6 = (f32[472,256]{1,0:T(8,128)S(1)}, f32[472,256]{1,0:T(8,128)S(1)}, u32[]{:S(2)}, u32[]{:S(2)}) collective-permute-start(f32[472,256]{1,0:T(8,128)S(1)} %get-tuple-element.55), channel_id=1, source_target_pairs={{0,1},{1,0},{2,3},{3,2},{4,5},{5,4},{6,7},{7,6},{8,9},{9,8},{10,11... | collective-permute-start | bytes 1449992 | tf_op jit(solution)/shard_map/ppermute | solution.py:724
  13.2 6.6 %collective-permute-start.5 = (f32[472,256]{1,0:T(8,128)S(1)}, f32[472,256]{1,0:T(8,128)S(1)}, u32[]{:S(2)}, u32[]{:S(2)}) collective-permute-start(f32[472,256]{1,0:T(8,128)S(1)} %get-tuple-element.54), channel_id=1, source_target_pairs={{1,8},{8,1},{9,16},{16,9},{17,24},{24,17},{3,10},{10,3},{11,18},{1... | collective-permute-start | bytes 1449992 | tf_op jit(solution)/shard_map/ppermute | solution.py:723
  15.1 6.1 %collective-permute-start.9 = (f32[4,3,2,8,128]{4,3,2,1,0:T(8,128)S(1)}, f32[4,3,2,8,128]{4,3,2,1,0:T(8,128)S(1)}, u32[]{:S(2)}, u32[]{:S(2)}) collective-permute-start(f32[4,3,2,8,128]{4,3,2,1,0:T(8,128)S(1)} %get-tuple-element.77.refs_12_), channel_id=1, source_target_pairs={{0,6},{2,4},{4,2},{6,0},{1,7},{3,5},{5,3},{7,1},{8,14},{10,12},{12... | collective-permute-start | bytes 294920 | tf_op jit(solution)/shard_map/ppermute | solution.py:704
  16.7 7.1 %collective-permute-start.8 = (f32[4,3,2,8,128]{4,3,2,1,0:T(8,128)S(1)}, f32[4,3,2,8,128]{4,3,2,1,0:T(8,128)S(1)}, u32[]{:S(2)}, u32[]{:S(2)}) collective-permute-start(f32[4,3,2,8,128]{4,3,2,1,0:T(8,128)S(1)} %get-tuple-element.77.refs_12_), channel_id=1, source_target_pairs={{0,4},{2,6},{4,0},{6,2},{1,5},{3,7},{5,1},{7,3},{8,12},{10,14},{12... | collective-permute-start | bytes 294920 | tf_op jit(solution)/shard_map/ppermute | solution.py:704
  18.2 5.7 %collective-permute-start.7 = (f32[4,3,2,8,128]{4,3,2,1,0:T(8,128)S(1)}, f32[4,3,2,8,128]{4,3,2,1,0:T(8,128)S(1)}, u32[]{:S(2)}, u32[]{:S(2)}) collective-permute-start(f32[4,3,2,8,128]{4,3,2,1,0:T(8,128)S(1)} %get-tuple-element.77.refs_12_), channel_id=1, source_target_pairs={{0,2},{2,0},{4,6},{6,4},{1,3},{3,1},{5,7},{7,5},{8,10},{10,8},{12,... | collective-permute-start | bytes 294920 | tf_op jit(solution)/shard_map/ppermute | solution.py:704
  41.5 2.2 %collective-permute-start.10 = (f32[16,5,2,8,128]{4,3,2,1,0:T(8,128)S(1)}, f32[16,5,2,8,128]{4,3,2,1,0:T(8,128)S(1)}, u32[]{:S(2)}, u32[]{:S(2)}) collective-permute-start(f32[16,5,2,8,128]{4,3,2,1,0:T(8,128)S(1)} %shard_map.54.mine), channel_id=1, source_target_pairs={{0,1},{1,0},{2,3},{3,2},{4,5},{5,4},{6,7},{7,6},{8,9},{9,8},{10,11... | collective-permute-start | bytes 1966088 | tf_op jit(solution)/shard_map/ppermute | solution.py:743
  41.5 5.4 %collective-permute-start.11 = (f32[8,16,256]{2,1,0:T(8,128)S(1)}, f32[8,16,256]{2,1,0:T(8,128)S(1)}, u32[]{:S(2)}, u32[]{:S(2)}) collective-permute-start(f32[8,16,256]{2,1,0:T(8,128)S(1)} %get-tuple-element.81), channel_id=1, source_target_pairs={{0,1},{1,0},{2,3},{3,2},{4,5},{5,4},{6,7},{7,6},{8,9},{9,8},{10,11... | collective-permute-start | bytes 393224 | tf_op jit(solution)/shard_map/ppermute | solution.py:740
  42.0 4.9 %collective-permute-start.12 = (f32[8,16,256]{2,1,0:T(8,128)S(1)}, f32[8,16,256]{2,1,0:T(8,128)S(1)}, u32[]{:S(2)}, u32[]{:S(2)}) collective-permute-start(f32[8,16,256]{2,1,0:T(8,128)S(1)} %get-tuple-element.82), channel_id=1, source_target_pairs={{1,8},{8,1},{9,16},{16,9},{17,24},{24,17},{3,10},{10,3},{11,18},{1... | collective-permute-start | bytes 393224 | tf_op jit(solution)/shard_map/ppermute | solution.py:739
  47.0 4.9 %collective-permute-start.13 = (f32[160,128]{1,0:T(8,128)S(1)}, f32[160,128]{1,0:T(8,128)S(1)}, u32[]{:S(2)}, u32[]{:S(2)}) collective-permute-start(f32[160,128]{1,0:T(8,128)S(1)} %get-tuple-element.84), channel_id=1, source_target_pairs={{0,2},{2,0},{4,6},{6,4},{1,3},{3,1},{5,7},{7,5},{8,10},{10,8},{12,... | collective-permute-start | bytes 245768 | tf_op jit(solution)/shard_map/ppermute | solution.py:764
  47.9 5.1 %collective-permute-start.14 = (f32[160,128]{1,0:T(8,128)S(1)}, f32[160,128]{1,0:T(8,128)S(1)}, u32[]{:S(2)}, u32[]{:S(2)}) collective-permute-start(f32[160,128]{1,0:T(8,128)S(1)} %get-tuple-element.85), channel_id=1, source_target_pairs={{0,4},{2,6},{4,0},{6,2},{1,5},{3,7},{5,1},{7,3},{8,12},{10,14},{12... | collective-permute-start | bytes 245768 | tf_op jit(solution)/shard_map/ppermute | solution.py:764
  48.6 6.2 %collective-permute-start.15 = (f32[160,128]{1,0:T(8,128)S(1)}, f32[160,128]{1,0:T(8,128)S(1)}, u32[]{:S(2)}, u32[]{:S(2)}) collective-permute-start(f32[160,128]{1,0:T(8,128)S(1)} %get-tuple-element.86), channel_id=1, source_target_pairs={{0,6},{2,4},{4,2},{6,0},{1,7},{3,5},{5,3},{7,1},{8,14},{10,12},{12... | collective-permute-start | bytes 245768 | tf_op jit(solution)/shard_map/ppermute | solution.py:764
  57.4 1.6 %collective-permute-start.16 = (f32[2,4,4,16,128]{4,3,2,1,0:T(8,128)S(1)}, f32[2,4,4,16,128]{4,3,2,1,0:T(8,128)S(1)}, u32[]{:S(2)}, u32[]{:S(2)}) collective-permute-start(f32[2,4,4,16,128]{4,3,2,1,0:T(8,128)S(1)} %get-tuple-element.95), channel_id=1, source_target_pairs={{0,1},{1,0},{2,3},{3,2},{4,5},{5,4},{6,7},{7,6},{8,9},{9,8},{10,11... | collective-permute-start | bytes 786440 | tf_op jit(solution)/shard_map/ppermute | solution.py:771
